TPU v7x, 32 devices: a whole 2x2x4 slice. The times are simulated.
32 devices in a mesh: seq: 8 (over y, x, core), dp: 4 (over z).
Axes of the slice: x: 2, y: 2, z: 4, core: 2. Of those that a mesh axis runs over, the one named last changes fastest.
Arguments:
- tokens: bfloat16 [4, 4096, 1024], P('dp', 'seq'), may hold values from -6 to 6
- item_starts: int32 [4, 8], P('dp', 'seq'), may hold values from 0 to 1, as said below
- attn_gain: float32 [1024], replicated, may hold values from 0.5 to 1.5
- query_weight: bfloat16 [1024, 1024], replicated, may hold values from -0.1875 to 0.1875
- key_weight: bfloat16 [1024, 1024], replicated, may hold values from -0.1875 to 0.1875
- value_weight: bfloat16 [1024, 1024], replicated, may hold values from -0.1875 to 0.1875
- output_weight: bfloat16 [1024, 1024], replicated, may hold values from -1.5 to 1.5
- state_queries: bfloat16 [512, 1024], replicated, may hold values from -6 to 6
- state_weight: bfloat16 [1024, 2048], replicated, may hold values from -1.5 to 1.5
- gate_bias: float32 [1024], replicated, may hold values from -2 to 6
- initial_state: float32 [512, 1024], replicated, may hold values from -6 to 6
- mlp_gain: float32 [1024], replicated, may hold values from 0.5 to 1.5
- up_weight: bfloat16 [1024, 4096], replicated, may hold values from -0.1875 to 0.1875
- down_weight: bfloat16 [4096, 1024], replicated, may hold values from -0.09375 to 0.09375
- out_cotangent: bfloat16 [4, 4096, 1024], P('dp', 'seq'), may hold values from -6 to 6
- state_cotangent: float32 [4, 8, 512, 1024], P('dp', 'seq'), may hold values from -6 to 6
Outputs:
- mixed: bfloat16 [4, 4096, 1024], P('dp', 'seq')
- states: float32 [4, 8, 512, 1024], P('dp', 'seq')
- tokens_grad: float32 [4, 4096, 1024], P('dp', 'seq')
- attn_gain_grad: float32 [1024], P('seq')
- query_grad: float32 [1024, 1024], P('seq')
- key_grad: float32 [1024, 1024], P('seq')
- value_grad: float32 [1024, 1024], P('seq')
- output_grad: float32 [1024, 1024], P('seq')
- state_queries_grad: float32 [512, 1024], P('seq')
- state_weight_grad: float32 [1024, 2048], P('seq')
- gate_bias_grad: float32 [1024], P('seq')
- initial_state_grad: float32 [512, 1024], P('seq')
- mlp_gain_grad: float32 [1024], P('seq')
- up_grad: float32 [1024, 4096], P('seq')
- down_grad: float32 [4096, 1024], P('seq')
Inputs may be any that keep to these rules, and one draw needn't show every extreme that they name: item_starts is 1 exactly at the first block of each item. Block 0 of every group starts an item; each aligned run of 8 blocks holds one item of 8 blocks or two of 4 blocks; some item has 8 blocks.
All inputs are finite; a program needn't handle non-finite values.
Results may differ from a plain program's by a relative error of at most 0.023.
Values may be sent and summed in bfloat16 or wider, within the bound.
No kernel may reach another device: no remote copies, remote signals or barrier semaphores. Data moves between devices by JAX's collectives and lax.ppermute only.
A program may use at most 512 MiB of HBM per device.

v0:
```python
import math

import jax
import jax.numpy as jnp
from jax import lax
from jax.sharding import PartitionSpec as P

D = 1024
HEADS = 8
HEAD_DIM = 128
W = 512
NS = 512


EPSILON = 1e-06
NEGATIVE = -1e30
GELU_SCALE = 0.7978845608028654
GELU_CUBIC = 0.044715


def shifted(value, axis, steps):
    count = lax.axis_size(axis)
    first, last = (max(0, -steps), min(count, count - steps))
    return lax.ppermute(value, axis, [(source, source + steps) for source in range(first, last)])


def entering(value, axis, join, neutral):
    count, mine = (lax.axis_size(axis), lax.axis_index(axis))
    pieces = jax.tree.map(lambda part: lax.all_gather(part, axis), value)
    so_far = jax.tree.map(
        lambda part, zero: jnp.full_like(part, 0) + jnp.asarray(zero, part.dtype), value, neutral
    )

    def lap(position, so_far):
        longer = join(so_far, jax.tree.map(lambda part: part[position], pieces))
        return jax.tree.map(lambda new, old: jnp.where(position < mine, new, old), longer, so_far)

    return lax.fori_loop(0, count - 1, lap, so_far)


def carried_in(x, axis, join, neutral):
    count = lax.axis_size(axis)
    place = lax.axis_index(axis)
    ahead = count - 1 - place
    gathered = jax.tree.map(
        lambda a, kind: lax.all_gather(a.astype(kind), axis), x, (jnp.bfloat16, jnp.bfloat16)
    )
    state = jax.tree.map(lambda a, e: jnp.zeros_like(a) + jnp.asarray(e, a.dtype), x, neutral)

    def one(lap, state):
        source = count - 1 - lap
        return join(
            state,
            jax.tree.map(
                lambda a, own: lax.dynamic_index_in_dim(a, source, 0, False).astype(own.dtype),
                gathered,
                x,
            ),
        )

    return lax.fori_loop(0, ahead, one, state)


def gelu_tanh(upper):
    inner = GELU_SCALE * (upper + GELU_CUBIC * upper * upper * upper)
    return 0.5 * upper * (1.0 + jnp.tanh(inner))


def gelu_slope(upper):
    inner = GELU_SCALE * (upper + GELU_CUBIC * upper * upper * upper)
    tvalue = jnp.tanh(inner)
    return 0.5 * (1.0 + tvalue) + 0.5 * upper * (1.0 - tvalue * tvalue) * GELU_SCALE * (
        1.0 + 3.0 * GELU_CUBIC * upper * upper
    )


def product(left, right):
    return jnp.dot(left, right, preferred_element_type=jnp.float32)


def product_tn(left, right):
    return lax.dot_general(
        left, right, (((0,), (0,)), ((), ())), preferred_element_type=jnp.float32
    )


def product_nt(left, right):
    return lax.dot_general(
        left, right, (((1,), (1,)), ((), ())), preferred_element_type=jnp.float32
    )


def rms_scale(field):
    return lax.rsqrt(jnp.mean(field * field, axis=-1, keepdims=True) + EPSILON)


def rms_back(field, scaled, gain, grad):
    gain_grad = jnp.sum(grad * field * scaled, axis=0)
    weighted = grad * gain
    field_grad = scaled * weighted - field * scaled * scaled * scaled * jnp.mean(
        weighted * field, axis=-1, keepdims=True
    )
    return (gain_grad, field_grad)


def split_heads(field):
    return field.reshape(field.shape[0], HEADS, HEAD_DIM)


def compose(earlier, later):
    return (later[0] * earlier[0], later[0] * earlier[1] + later[1])


def key_mask(keep_left):
    rows = lax.broadcasted_iota(jnp.int32, (W, 2 * W + NS), 0)
    cols = lax.broadcasted_iota(jnp.int32, (W, 2 * W + NS), 1)
    left_part = (cols < W) & keep_left
    own_part = (cols >= W) & (cols < 2 * W) & (cols - W <= rows)
    return left_part | own_part | (cols >= 2 * W)


def body(
    tokens,
    item_starts,
    attn_gain,
    query_weight,
    key_weight,
    value_weight,
    output_weight,
    state_queries,
    state_weight,
    gate_bias,
    initial_state,
    mlp_gain,
    up_weight,
    down_weight,
    out_cotangent,
    state_cotangent,
):
    scale = 1.0 / math.sqrt(HEAD_DIM)
    inputs = tokens[0].astype(jnp.float32)
    start_flag = item_starts[0, 0]
    start = start_flag.astype(jnp.float32)
    keep = 1.0 - start
    attn_scale = rms_scale(inputs)
    normed = (inputs * attn_scale * attn_gain).astype(jnp.bfloat16)
    queries = product(normed, query_weight).astype(jnp.bfloat16)
    keys = product(normed, key_weight).astype(jnp.bfloat16)
    values = product(normed, value_weight).astype(jnp.bfloat16)
    left_pair = shifted(jnp.stack([keys, values]), "seq", 1)
    left_keys = left_pair[0]
    left_values = left_pair[1]
    query_heads = split_heads(state_queries)
    key_heads = split_heads(keys)
    value_heads = split_heads(values)
    summary_raw = (
        jnp.einsum("nhd,whd->hnw", query_heads, key_heads, preferred_element_type=jnp.float32)
        * scale
    )
    summary_peak = jnp.max(summary_raw, axis=-1, keepdims=True)
    summary_exp = jnp.exp(summary_raw - summary_peak)
    summary_total = jnp.sum(summary_exp, axis=-1, keepdims=True)
    summary_lse = summary_peak + jnp.log(summary_total)
    summary_low = (summary_exp / summary_total).astype(jnp.bfloat16)
    summary = jnp.einsum(
        "hnw,whd->nhd", summary_low, value_heads, preferred_element_type=jnp.float32
    )
    summary = summary.reshape(NS, D).astype(jnp.bfloat16)
    projected = product(summary, state_weight)
    update = projected[:, :D]
    forget = jax.nn.sigmoid(projected[:, D:] + gate_bias)
    fresh = (1.0 - forget) * update
    carried_scale = keep * forget
    carried_base = start * forget * initial_state + fresh
    identity = (jnp.ones((NS, D), jnp.float32), jnp.zeros((NS, D), jnp.float32))
    prefix = entering((carried_scale, carried_base), "seq", compose, identity)
    previous = prefix[1]
    state_in = keep * previous + start * initial_state
    state_out = forget * state_in + fresh
    state_low = state_in.astype(jnp.bfloat16)
    state_keys = product(state_low, key_weight).astype(jnp.bfloat16)
    state_values = product(state_low, value_weight).astype(jnp.bfloat16)
    seen_keys = split_heads(jnp.concatenate([left_keys, keys, state_keys], axis=0))
    seen_values = split_heads(jnp.concatenate([left_values, values, state_values], axis=0))
    token_heads = split_heads(queries)
    valid = key_mask(start_flag == 0)
    raw = jnp.einsum("whd,khd->hwk", token_heads, seen_keys, preferred_element_type=jnp.float32)
    scores = jnp.where(valid, raw * scale, NEGATIVE)
    peak = jnp.max(scores, axis=-1, keepdims=True)
    expos = jnp.exp(scores - peak)
    totals = jnp.sum(expos, axis=-1, keepdims=True)
    log_total = peak + jnp.log(totals)
    probs_low = (expos / totals).astype(jnp.bfloat16)
    attended = jnp.einsum(
        "hwk,khd->whd", probs_low, seen_values, preferred_element_type=jnp.float32
    )
    attended = attended.reshape(W, D).astype(jnp.bfloat16)
    hidden = inputs + product(attended, output_weight)
    mlp_scale = rms_scale(hidden)
    normed_mlp = (hidden * mlp_scale * mlp_gain).astype(jnp.bfloat16)
    upper = product(normed_mlp, up_weight)
    activated = gelu_tanh(upper).astype(jnp.bfloat16)
    mixed = (hidden + product(activated, down_weight)).astype(jnp.bfloat16)
    cotangent = out_cotangent[0]
    down_grad = product_tn(activated, cotangent)
    activated_grad = product_nt(cotangent, down_weight).astype(jnp.bfloat16)
    upper_grad = (activated_grad.astype(jnp.float32) * gelu_slope(upper)).astype(jnp.bfloat16)
    up_grad = product_tn(normed_mlp, upper_grad)
    normed_mlp_grad = product_nt(upper_grad, up_weight)
    mlp_gain_grad, hidden_part = rms_back(hidden, mlp_scale, mlp_gain, normed_mlp_grad)
    hidden_grad = hidden_part + cotangent.astype(jnp.float32)
    attended_grad = hidden_grad.astype(jnp.bfloat16)
    output_grad = product_tn(attended, attended_grad)
    attended_heads_grad = split_heads(product_nt(attended_grad, output_weight).astype(jnp.bfloat16))
    again = jnp.einsum("whd,khd->hwk", token_heads, seen_keys, preferred_element_type=jnp.float32)
    probs = jnp.exp(jnp.where(valid, again * scale, NEGATIVE) - log_total)
    probs_again = probs.astype(jnp.bfloat16)
    prob_grad = jnp.einsum(
        "whd,khd->hwk", attended_heads_grad, seen_values, preferred_element_type=jnp.float32
    )
    seen_values_grad = jnp.einsum(
        "hwk,whd->khd", probs_again, attended_heads_grad, preferred_element_type=jnp.float32
    ).reshape(2 * W + NS, D)
    rowdot = jnp.sum(probs * prob_grad, axis=-1, keepdims=True)
    score_grad = (probs * (prob_grad - rowdot) * scale).astype(jnp.bfloat16)
    queries_grad = (
        jnp.einsum("hwk,khd->whd", score_grad, seen_keys, preferred_element_type=jnp.float32)
        .reshape(W, D)
        .astype(jnp.bfloat16)
    )
    seen_keys_grad = jnp.einsum(
        "hwk,whd->khd", score_grad, token_heads, preferred_element_type=jnp.float32
    ).reshape(2 * W + NS, D)
    state_keys_grad = seen_keys_grad[2 * W :].astype(jnp.bfloat16)
    state_values_grad = seen_values_grad[2 * W :].astype(jnp.bfloat16)
    direct = product_nt(state_keys_grad, key_weight) + product_nt(state_values_grad, value_weight)
    state_cot = state_cotangent[0, 0]
    back_scale = keep * forget
    back_base = keep * (forget * state_cot + direct)
    suffix = carried_in((back_scale, back_base), "seq", compose, identity)
    incoming = suffix[1]
    out_state_grad = state_cot + incoming
    in_state_grad = forget * out_state_grad + direct
    initial_state_grad = start * in_state_grad
    gate_grad = out_state_grad * (state_in - update) * forget * (1.0 - forget)
    gate_bias_grad = jnp.sum(gate_grad, axis=0)
    projected_grad = jnp.concatenate([out_state_grad * (1.0 - forget), gate_grad], axis=1).astype(
        jnp.bfloat16
    )
    state_weight_grad = product_tn(summary, projected_grad)
    summary_grad = split_heads(product_nt(projected_grad, state_weight).astype(jnp.bfloat16))
    summary_again = jnp.einsum(
        "nhd,whd->hnw", query_heads, key_heads, preferred_element_type=jnp.float32
    )
    summary_probs = jnp.exp(summary_again * scale - summary_lse)
    summary_prob_grad = jnp.einsum(
        "nhd,whd->hnw", summary_grad, value_heads, preferred_element_type=jnp.float32
    )
    summary_rowdot = jnp.sum(summary_probs * summary_prob_grad, axis=-1, keepdims=True)
    summary_score_grad = (summary_probs * (summary_prob_grad - summary_rowdot) * scale).astype(
        jnp.bfloat16
    )
    state_queries_grad = jnp.einsum(
        "hnw,whd->nhd", summary_score_grad, key_heads, preferred_element_type=jnp.float32
    ).reshape(NS, D)
    keys_from_summary = jnp.einsum(
        "hnw,nhd->whd", summary_score_grad, query_heads, preferred_element_type=jnp.float32
    ).reshape(W, D)
    values_from_summary = jnp.einsum(
        "hnw,nhd->whd", summary_low, summary_grad, preferred_element_type=jnp.float32
    ).reshape(W, D)
    returned = shifted(
        jnp.stack([seen_keys_grad[:W], seen_values_grad[:W]]).astype(jnp.bfloat16), "seq", -1
    ).astype(jnp.float32)
    keys_total = (seen_keys_grad[W : 2 * W] + keys_from_summary + returned[0]).astype(jnp.bfloat16)
    values_total = (seen_values_grad[W : 2 * W] + values_from_summary + returned[1]).astype(
        jnp.bfloat16
    )
    query_grad = product_tn(normed, queries_grad)
    key_grad = product_tn(normed, keys_total) + product_tn(state_low, state_keys_grad)
    value_grad = product_tn(normed, values_total) + product_tn(state_low, state_values_grad)
    normed_grad = (
        product_nt(queries_grad, query_weight)
        + product_nt(keys_total, key_weight)
        + product_nt(values_total, value_weight)
    )
    attn_gain_grad, token_part = rms_back(inputs, attn_scale, attn_gain, normed_grad)
    tokens_grad = hidden_grad + token_part
    whole = (
        lax.psum_scatter(
            attn_gain_grad.astype(jnp.bfloat16), "seq", scatter_dimension=0, tiled=True
        ).astype(jnp.float32),
        lax.psum_scatter(
            query_grad.astype(jnp.bfloat16), "seq", scatter_dimension=0, tiled=True
        ).astype(jnp.float32),
        lax.psum_scatter(
            key_grad.astype(jnp.bfloat16), "seq", scatter_dimension=0, tiled=True
        ).astype(jnp.float32),
        lax.psum_scatter(
            value_grad.astype(jnp.bfloat16), "seq", scatter_dimension=0, tiled=True
        ).astype(jnp.float32),
        lax.psum_scatter(
            output_grad.astype(jnp.bfloat16), "seq", scatter_dimension=0, tiled=True
        ).astype(jnp.float32),
        lax.psum_scatter(
            state_queries_grad.astype(jnp.bfloat16), "seq", scatter_dimension=0, tiled=True
        ).astype(jnp.float32),
        lax.psum_scatter(
            state_weight_grad.astype(jnp.bfloat16), "seq", scatter_dimension=0, tiled=True
        ).astype(jnp.float32),
        lax.psum_scatter(
            gate_bias_grad.astype(jnp.bfloat16), "seq", scatter_dimension=0, tiled=True
        ).astype(jnp.float32),
        lax.psum_scatter(
            initial_state_grad.astype(jnp.bfloat16), "seq", scatter_dimension=0, tiled=True
        ).astype(jnp.float32),
        lax.psum_scatter(
            mlp_gain_grad.astype(jnp.bfloat16), "seq", scatter_dimension=0, tiled=True
        ).astype(jnp.float32),
        lax.psum_scatter(
            up_grad.astype(jnp.bfloat16), "seq", scatter_dimension=0, tiled=True
        ).astype(jnp.float32),
        lax.psum_scatter(
            down_grad.astype(jnp.bfloat16), "seq", scatter_dimension=0, tiled=True
        ).astype(jnp.float32),
    )
    summed = tuple(
        (
            lax.psum(whole[0].astype(jnp.bfloat16), "dp").astype(jnp.float32),
            lax.psum(whole[1].astype(jnp.bfloat16), "dp").astype(jnp.float32),
            lax.psum(whole[2].astype(jnp.bfloat16), "dp").astype(jnp.float32),
            lax.psum(whole[3].astype(jnp.bfloat16), "dp").astype(jnp.float32),
            lax.psum(whole[4].astype(jnp.bfloat16), "dp").astype(jnp.float32),
            lax.psum(whole[5].astype(jnp.bfloat16), "dp").astype(jnp.float32),
            lax.psum(whole[6].astype(jnp.bfloat16), "dp").astype(jnp.float32),
            lax.psum(whole[7].astype(jnp.bfloat16), "dp").astype(jnp.float32),
            lax.psum(whole[8].astype(jnp.bfloat16), "dp").astype(jnp.float32),
            lax.psum(whole[9].astype(jnp.bfloat16), "dp").astype(jnp.float32),
            lax.psum(whole[10].astype(jnp.bfloat16), "dp").astype(jnp.float32),
            lax.psum(whole[11].astype(jnp.bfloat16), "dp").astype(jnp.float32),
        )
    )
    return (
        mixed[None],
        state_out[None, None],
        tokens_grad[None],
        summed[0],
        summed[1],
        summed[2],
        summed[3],
        summed[4],
        summed[5],
        summed[6],
        summed[7],
        summed[8],
        summed[9],
        summed[10],
        summed[11],
    )


def solution(mesh):
    in_specs = (
        P("dp", "seq", None),
        P("dp", "seq"),
        P(),
        P(),
        P(),
        P(),
        P(),
        P(),
        P(),
        P(),
        P(),
        P(),
        P(),
        P(),
        P("dp", "seq", None),
        P("dp", "seq", None, None),
    )
    out_specs = (
        P("dp", "seq", None),
        P("dp", "seq", None, None),
        P("dp", "seq", None),
        P("seq"),
        P("seq", None),
        P("seq", None),
        P("seq", None),
        P("seq", None),
        P("seq", None),
        P("seq", None),
        P("seq"),
        P("seq", None),
        P("seq"),
        P("seq", None),
        P("seq", None),
    )
    return jax.shard_map(body, mesh=mesh, in_specs=in_specs, out_specs=out_specs, check_vma=False)
```

profile of v0, /device:TPU:0, one launch (start us, length us, event | category | flops | bytes accessed | tf_op | source)
XLA Modules:
  0.0 1152.8 jit_solution(10320423289429418594)
XLA Ops:
  65.4 78.4 %all-gather.9.cloned.1.call-done = f32[4096,1024]{1,0:T(8,128)} async-done(((f32[512,1024]{1,0:T(8,128)}), f32[4096,1024]{1,0:T(8,128)}) %all-gather.9.cloned.1.call-update) | async-done | bytes 16777232 | tf_op jit(solution)/shard_map/all_gather | solution.py:29
  143.9 92.9 %all-gather.11.cloned.1.call-done = f32[4096,1024]{1,0:T(8,128)} async-done(((f32[512,1024]{1,0:T(8,128)}), f32[4096,1024]{1,0:T(8,128)}) %all-gather.11.cloned.1.call-update) | async-done | bytes 16777232 | tf_op jit(solution)/shard_map/all_gather | solution.py:29
  236.7 36.1 %while.29 = (s32[]{:T(128)}, f32[512,1024]{1,0:T(8,128)}, s32[]{:T(128)}, f32[8,512,1024]{2,1,0:T(8,128)}, f32[8,512,1024]{2,1,0:T(8,128)}, /*index=5*/s32[]{:T(128)}, s32[]{:T(128)}) while((s32[]{:T(128)}, f32[512,1024]{1,0:T(8,128)}, s32[]{:T(128)}, f32[8,512,1024]{2,1,0:T(8,128)}, f32[8,512,1024]{2,1,0:T(8,128)}, ...), condition=%wide.region_4.5_spmd.clone, body=%wide.region_3.4_spmd.clone.sunk | while | flops 2097156 | bytes 8388717 | solution.py:38
  290.7 13.2 %fusion.142 = (f32[8,512]{1,0:T(8,128)S(1)}, f32[8,512,1536]{2,1,0:T(8,128)}) fusion(bf16[512,8,128]{0,2,1:T(8,128)(2,1)S(1)} %bitcast.282, bf16[1536,8,128]{2,0,1:T(8,128)(2,1)} %bitcast_dynamic-update-slice_fusion, pred[512,1536]{1,0:T(8,128)(4,1)S(1)} %copy-done.22), kind=kOutput, calls=%fused_computation.188 | convolution fusion | flops 1629483008 | bytes 30162944 | tf_op jit(solution)/shard_map/whd,khd->hwk/dot_general | solution.py:187
  303.9 11.4 fusion.6
  315.4 12.0 %fusion.96 = bf16[8,128,512]{2,1,0:T(8,128)(2,1)} fusion(f32[8,512,1536]{2,1,0:T(8,128)} %get-tuple-element.274, f32[8,512]{1,0:T(8,128)S(1)} %fusion.6, f32[8,512]{1,0:T(8,128)S(1)} %get-tuple-element.273, bf16[512,8,128]{0,2,1:T(8,128)(2,1)S(1)} %bitcast.299, bf16[512,8,128]{0,2,1:T(8,128)(2,1)S(1)} %bitcast.274, bf16[512,8,128]{0,2,1:T(8,128)(2,1)S(1)} %bitcast.297), kind=kOutput, calls=%fused_computation.134 | convolution fusion | flops 1639448576 | bytes 29392896 | tf_op jit(solution)/shard_map/hwk,khd->whd/dot_general | solution.py:194
  330.7 11.1 fusion.130
  341.8 12.0 %fusion.19 = bf16[512,4096]{1,0:T(8,128)(2,1)S(1)} fusion(f32[512,4096]{1,0:T(8,128)} %fusion.130, bf16[4096,1024]{1,0:T(8,128)(2,1)} %param.33, bf16[1,512,1024]{2,1,0:T(8,128)(2,1)S(1)} %copy-done.36), kind=kOutput, calls=%fused_computation.28 | convolution fusion | flops 4339007488 | bytes 22020096 | tf_op jit(solution)/shard_map/dot_general | solution.py:88
  353.8 9.6 multiply_reduce_fusion.2
  370.0 16.5 %fusion.146 = (bf16[1536,8,128]{0,2,1:T(8,128)(2,1)}, f32[1536,8,128]{0,2,1:T(8,128)}) fusion(bf16[512,8,128]{0,2,1:T(8,128)(2,1)} %bitcast.276, f32[8,512,1536]{2,1,0:T(8,128)} %get-tuple-element.274, f32[8,512]{1,0:T(8,128)S(1)} %log_add_fusion.1), kind=kOutput, calls=%fused_computation.190 | convolution fusion | flops 1624768512 | bytes 35667968 | tf_op jit(solution)/shard_map/hwk,whd->khd/dot_general | solution.py:221
  389.7 10.1 fusion.99
  399.8 50.7 %fusion.143 = (bf16[1536,8,128]{0,2,1:T(8,128)(2,1)}, f32[1536,8,128]{0,2,1:T(8,128)}) fusion(bf16[512,8,128]{0,2,1:T(8,128)(2,1)} %bitcast.281, f32[8,512,1536]{2,1,0:T(8,128)} %fusion.99, f32[8,512,1536]{2,1,0:T(8,128)} %get-tuple-element.274, f32[8,512]{1,0:T(8,128)S(1)} %log_add_fusion.1), kind=kOutput, calls=%fused_computation.189 | convolution fusion | flops 1656231424 | bytes 60833792 | tf_op jit(solution)/shard_map/hwk,whd->khd/dot_general | solution.py:231
  464.9 52.2 %fusion.93 = bf16[8,128,512]{2,1,0:T(8,128)(2,1)} fusion(bf16[1536,8,128]{2,0,1:T(8,128)(2,1)} %bitcast_dynamic-update-slice_fusion, f32[8,512,1536]{2,1,0:T(8,128)} %fusion.99, f32[8,512,1536]{2,1,0:T(8,128)} %get-tuple-element.274, f32[8,512]{1,0:T(8,128)S(1)} %log_add_fusion.1), kind=kOutput, calls=%fused_computation.132 | convolution fusion | flops 1655182848 | bytes 54542336 | tf_op jit(solution)/shard_map/hwk,khd->whd/dot_general | solution.py:227
  521.3 11.0 convolution_convert_fusion
  532.3 10.7 convolution_convert_fusion.1
  558.5 29.0 %while.28 = (s32[]{:T(128)}, f32[512,1024]{1,0:T(8,128)}, s32[]{:T(128)}, bf16[8,512,1024]{2,1,0:T(8,128)(2,1)}, bf16[8,512,1024]{2,1,0:T(8,128)(2,1)}, /*index=5*/s32[]{:T(128)}, s32[]{:T(128)}, s32[]{:T(128)}, s32[]{:T(128)}) while((s32[]{:T(128)}, f32[512,1024]{1,0:T(8,128)}, s32[]{:T(128)}, bf16[8,512,1024]{2,1,0:T(8,128)(2,1)}, ...), condition=%wide.region_11.12_spmd, body=%wide.region_10.11_spmd.sunk | while | flops 2097158 | bytes 6291607 | solution.py:61
  587.5 7.9 fusion.137
  595.7 6.2 convolution_convert_fusion.13
  610.3 17.7 %fusion.90 = bf16[8,128,512]{2,1,0:T(8,128)(2,1)} fusion(f32[8,512,512]{1,2,0:T(8,128)} %fusion.150, f32[8,512,512]{2,1,0:T(8,128)} %copy-done.1, f32[8,512]{1,0:T(8,128)S(1)} %log_add_fusion, bf16[512,1024]{1,0:T(8,128)(2,1)} %convolution_convert_fusion.12), kind=kOutput, calls=%fused_computation.131 | convolution fusion | flops 556274176 | bytes 18890752 | tf_op jit(solution)/shard_map/hnw,whd->nhd/dot_general | solution.py:263
  636.6 16.0 %slice_add_fusion.1 = f32[512,8,128]{0,2,1:T(8,128)} fusion(f32[1536,8,128]{0,2,1:T(8,128)} %get-tuple-element.279, bf16[512,8,128]{0,2,1:T(8,128)(2,1)} %bitcast.288, f32[8,512,512]{1,2,0:T(8,128)} %fusion.150, f32[8,512,512]{2,1,0:T(8,128)} %copy-done.1, f32[8,512]{1,0:T(8,128)S(1)} %log_add_fusion), kind=kOutput, calls=%fused_computation.85 | convolution fusion | flops 556274176 | bytes 38830080 | tf_op jit(solution)/shard_map/hnw,nhd->whd/dot_general | solution.py:266
  667.8 6.2 convolution_convert_fusion.3
  674.4 6.5 reduce-scatter.26.cloned.1.call-done
  680.9 75.1 %reduce-scatter.24.cloned.1.call-done = bf16[128,4096]{1,0:T(8,128)(2,1)} async-done(((bf16[1024,4096]{1,0:T(8,128)(2,1)}), bf16[128,4096]{1,0:T(8,128)(2,1)}) %reduce-scatter.24.cloned.1.call-update) | async-done | bytes 1048592 | tf_op jit(solution)/shard_map/reduce_scatter | solution.py:320
  756.0 39.8 %reduce-scatter.22.cloned.1.call-done = bf16[64,1024]{1,0:T(8,128)(2,1)} async-done(((bf16[512,1024]{1,0:T(8,128)(2,1)}), bf16[64,1024]{1,0:T(8,128)(2,1)}) %reduce-scatter.22.cloned.1.call-update) | async-done | bytes 131088 | tf_op jit(solution)/shard_map/reduce_scatter | solution.py:314
  795.9 39.1 %reduce-scatter.18.cloned.1.call-done = bf16[64,1024]{1,0:T(8,128)(2,1)} async-done(((bf16[512,1024]{1,0:T(8,128)(2,1)}), bf16[64,1024]{1,0:T(8,128)(2,1)}) %reduce-scatter.18.cloned.1.call-update) | async-done | bytes 131088 | tf_op jit(solution)/shard_map/reduce_scatter | solution.py:305
  835.0 44.5 %reduce-scatter.14.cloned.1.call-done = bf16[128,1024]{1,0:T(8,128)(2,1)} async-done(((bf16[1024,1024]{1,0:T(8,128)(2,1)}), bf16[128,1024]{1,0:T(8,128)(2,1)}) %reduce-scatter.14.cloned.1.call-update) | async-done | bytes 262160 | tf_op jit(solution)/shard_map/reduce_scatter | solution.py:299
  879.5 44.7 %reduce-scatter.12.cloned.1.call-done = bf16[128,1024]{1,0:T(8,128)(2,1)} async-done(((bf16[1024,1024]{1,0:T(8,128)(2,1)}), bf16[128,1024]{1,0:T(8,128)(2,1)}) %reduce-scatter.12.cloned.1.call-update) | async-done | bytes 262160 | tf_op jit(solution)/shard_map/reduce_scatter | solution.py:296
  924.2 54.7 %reduce-scatter.20.cloned.1.call-done = bf16[128,2048]{1,0:T(8,128)(2,1)} async-done(((bf16[1024,2048]{1,0:T(8,128)(2,1)}), bf16[128,2048]{1,0:T(8,128)(2,1)}) %reduce-scatter.20.cloned.1.call-update) | async-done | bytes 524304 | tf_op jit(solution)/shard_map/reduce_scatter | solution.py:308
  983.6 12.7 %fusion.98 = bf16[1,512,1024]{2,1,0:T(8,128)(2,1)} fusion(f32[512,1024]{1,0:T(8,128)S(1)} %copy-done.18, bf16[4096,1024]{1,0:T(8,128)(2,1)} %param.33, f32[512,4096]{1,0:T(8,128)} %fusion.130), kind=kOutput, calls=%fused_computation.136 | convolution fusion | flops 4314890240 | bytes 19922944 | tf_op jit(solution)/shard_map/dot_general | solution.py:78
  1002.5 13.1 %all-reduce.3 = (bf16[1024]{0:T(1024)(128)(2,1)S(1)}, bf16[1024]{0:T(1024)(128)(2,1)S(1)}, bf16[1024]{0:T(1024)(128)(2,1)S(1)}) all-reduce(bf16[1024]{0:T(1024)(128)(2,1)S(1)} %get-tuple-element.215, bf16[1024]{0:T(1024)(128)(2,1)S(1)} %get-tuple-element.252, ...), channel_id=6, replica_groups=mesh['seq'=8,'dp'=4] {'seq'}, use_global_device_ids=true, to_apply=%region_15.16.clone | all-reduce | flops 3072 | bytes 12288
  1015.8 12.4 %all-reduce.4 = (bf16[128]{0:T(256)(128)(2,1)S(1)}, bf16[128]{0:T(256)(128)(2,1)S(1)}, bf16[128]{0:T(256)(128)(2,1)S(1)}) all-reduce(bf16[128]{0:T(256)(128)(2,1)S(1)} %dynamic-slice.1, bf16[128]{0:T(256)(128)(2,1)S(1)} %dynamic-slice.3, bf16[128]{0:T(256)(128)(2,1)S(1)} %dynamic-slice.5), channel_id=1, replica_groups=mesh['seq'=8,'dp'=4] {'dp'}, use_global_device_ids=true, to_apply=%region_16.17 | all-reduce | flops 384 | bytes 1536 | tf_op jit(solution)/shard_map/psum | solution.py:329
  1034.1 97.9 %all-reduce.8.cloned.1.call-done = (bf16[128,1024]{1,0:T(8,128)(2,1)}, bf16[128,1024]{1,0:T(8,128)(2,1)}, bf16[128,1024]{1,0:T(8,128)(2,1)}, bf16[128,1024]{1,0:...) async-done(((bf16[128,1024]{1,0:T(8,128)(2,1)}, ...) | async-done | bytes 3932176 | tf_op jit(solution)/shard_map/psum | solution.py:330
  (239 shorter events, 249.8 us)
Async XLA Ops:
  7.2 136.7 %all-gather.9.cloned.1.call-start = ((), (), s32[]{:S(2)}) async-start(), calls=%async_computation.18 | async-start | bytes 18874368 | tf_op jit(solution)/shard_map/all_gather | solution.py:29
  9.5 38.6 %copy-start.44 = (f32[512]{0:T(512)}, f32[512]{0:T(512)S(1)}, u32[]{:S(2)}) copy-start(f32[512]{0:T(512)S(1)} %add_rsqrt_fusion.1) | copy-start | bytes 6148
  40.3 196.4 %all-gather.11.cloned.1.call-start = ((), (), s32[]{:S(2)}) async-start(), calls=%async_computation.19 | async-start | bytes 18874368 | tf_op jit(solution)/shard_map/all_gather | solution.py:29
  41.1 515.8 %all-gather.13.cloned.1.call-start = ((), (), s32[]{:S(2)}) async-start(), calls=%async_computation.20 | async-start | bytes 9437184 | tf_op jit(solution)/shard_map/all_gather | solution.py:46
  44.2 12.0 %collective-permute-start = (bf16[2,512,1024]{2,1,0:T(8,128)(2,1)}, bf16[2,512,1024]{2,1,0:T(8,128)(2,1)}, u32[]{:S(2)}, u32[]{:S(2)}) collective-permute-start(bf16[2,512,1024]{2,1,0:T(8,128)(2,1)} %pad_maximum_fusion.1), channel_id=1, source_target_pairs={{0,4},{4,8},{8,12},{12,16},{16,20},{20,24},{24,28},{1,5},{5,9},{9,... | collective-permute-start | bytes 6291464 | tf_op jit(solution)/shard_map/ppermute | solution.py:24
  47.9 509.0 %all-gather.15.cloned.1.call-start = ((), (), s32[]{:S(2)}) async-start(), calls=%async_computation.21 | async-start | bytes 9437184 | tf_op jit(solution)/shard_map/all_gather | solution.py:46
  303.9 11.5 copy-start.8
  303.9 11.5 copy-start.28
  303.9 11.5 copy-start.30
  330.6 32.7 %copy-start.17 = (f32[512,1024]{1,0:T(8,128)}, f32[512,1024]{1,0:T(8,128)S(1)}, u32[]{:S(2)}) copy-start(f32[512,1024]{1,0:T(8,128)S(1)} %get-tuple-element.276) | copy-start | bytes 6291460
  330.7 11.1 copy-start.36
  353.8 9.6 copy-start.54
  460.3 214.1 %reduce-scatter.16.cloned.1.call-start = ((), (), s32[]{:S(2)}) async-start(), calls=%async_computation.12 | async-start | bytes 2359296 | tf_op jit(solution)/shard_map/reduce_scatter | solution.py:302
  464.8 52.3 %copy-start.45 = (f32[512]{0:T(512)S(1)}, f32[512]{0:T(512)}, u32[]{:S(2)}) copy-start(f32[512]{0:T(512)} %copy-done.44) | copy-start | bytes 6148
  464.9 52.3 %copy-start.47 = (f32[1024]{0:T(1024)S(1)}, f32[1024]{0:T(1024)}, u32[]{:S(2)}) copy-start(f32[1024]{0:T(1024)} %param.22) | copy-start | bytes 12292
  464.9 209.5 %reduce-scatter.10.cloned.1.call-start = ((), (), s32[]{:S(2)}) async-start(), calls=%async_computation.9 | async-start | bytes 2359296 | tf_op jit(solution)/shard_map/reduce_scatter | solution.py:293
  521.2 159.6 %reduce-scatter.26.cloned.1.call-start = ((), (), s32[]{:S(2)}) async-start(), calls=%async_computation.17 | async-start | bytes 9437184 | tf_op jit(solution)/shard_map/reduce_scatter | solution.py:323
  532.3 223.8 %reduce-scatter.24.cloned.1.call-start = ((), (), s32[]{:S(2)}) async-start(), calls=%async_computation.16 | async-start | bytes 9437184 | tf_op jit(solution)/shard_map/reduce_scatter | solution.py:320
  543.1 252.8 %reduce-scatter.22.cloned.1.call-start = ((), (), s32[]{:S(2)}) async-start(), calls=%async_computation.15 | async-start | bytes 1179648 | tf_op jit(solution)/shard_map/reduce_scatter | solution.py:314
  546.2 6.4 collective-permute-start.1
  595.5 239.5 %reduce-scatter.18.cloned.1.call-start = ((), (), s32[]{:S(2)}) async-start(), calls=%async_computation.13 | async-start | bytes 1179648 | tf_op jit(solution)/shard_map/reduce_scatter | solution.py:305
  636.3 243.1 %reduce-scatter.14.cloned.1.call-start = ((), (), s32[]{:S(2)}) async-start(), calls=%async_computation.11 | async-start | bytes 2359296 | tf_op jit(solution)/shard_map/reduce_scatter | solution.py:299
  662.1 262.1 %reduce-scatter.12.cloned.1.call-start = ((), (), s32[]{:S(2)}) async-start(), calls=%async_computation.10 | async-start | bytes 2359296 | tf_op jit(solution)/shard_map/reduce_scatter | solution.py:296
  667.8 311.2 %reduce-scatter.20.cloned.1.call-start = ((), (), s32[]{:S(2)}) async-start(), calls=%async_computation.14 | async-start | bytes 4718592 | tf_op jit(solution)/shard_map/reduce_scatter | solution.py:308
  674.0 305.0 %copy-start.53 = (u32[32]{0:T(128)S(1)}, u32[32]{0:T(128)}, u32[]{:S(2)}) copy-start(u32[32]{0:T(128)} %constant.106) | copy-start | bytes 388
  674.0 457.9 %all-reduce.8.cloned.1.call-start = ((), (), s32[]{:S(2)}) async-start(), calls=%async_computation.22 | async-start | bytes 7864320 | tf_op jit(solution)/shard_map/psum | solution.py:330
  983.6 12.8 %copy-start.4 = (f32[2,512,1024]{1,2,0:T(8,128)S(1)}, f32[2,512,1024]{1,2,0:T(8,128)}, u32[]{:S(2)}) copy-start(f32[2,512,1024]{1,2,0:T(8,128)} %convert_element_type.315) | copy-start | bytes 12582916
  983.6 12.8 %copy-start.5 = (f32[512,8,128]{0,2,1:T(8,128)S(1)}, f32[512,8,128]{0,2,1:T(8,128)}, u32[]{:S(2)}) copy-start(f32[512,8,128]{0,2,1:T(8,128)} %slice_add_fusion) | copy-start | bytes 6291460
  983.6 12.7 %copy-start.16 = (f32[512,8,128]{0,2,1:T(8,128)S(1)}, f32[512,8,128]{0,2,1:T(8,128)}, u32[]{:S(2)}) copy-start(f32[512,8,128]{0,2,1:T(8,128)} %slice_add_fusion.1) | copy-start | bytes 6291460
  1131.9 8.9 copy-start.40
  1131.9 9.7 copy-start.37
  1131.9 10.8 copy-start.35
  (39 other events, 119.6 us)
Sparse Core Ops, SparseCore 0:
  40.4 103.3 all-gather.8
  146.3 90.3 all-gather.10
  238.6 54.3 all-gather.12
  460.4 55.1 all-gather.14
  518.7 42.5 reduce-scatter.15
  564.8 41.2 reduce-scatter.9
  609.5 71.2 reduce-scatter.25
  684.7 71.2 reduce-scatter.23
  759.8 36.0 reduce-scatter.21
  798.9 36.0 reduce-scatter.17
  838.2 41.1 reduce-scatter.13
  883.0 41.2 reduce-scatter.11
  927.6 51.3 reduce-scatter.19
  982.2 149.6 all-reduce.7
where the time goes:
time: 1160 us; the launch traced here: 1150 us
  waiting for transfers between devices  580 us (50%)
  matrix products  340 us (29%)
  other arithmetic  139 us (12%)
  local copies, waits for them, and re-layouts  45.9 us (4%)
  blocking collectives  25.5 us (2%)
  between operations  16.4 us (1%)
    all_gather x2, waiting for transfers between devices, entering(): pieces = jax.tree.map(lambda part: lax.all_gather(part, axis), value)  171 us
    psum x1, waiting for transfers between devices, body(): lax.psum(whole[1].astype(jnp.bfloat16), 'dp').astype(jnp.float32)  97.9 us
    reduce_scatter x1, waiting for transfers between devices, body(): lax.psum_scatter(up_grad.astype(jnp.bfloat16), 'seq', scatter_dimension=0...  75.1 us
    reduce_scatter x1, waiting for transfers between devices, body(): lax.psum_scatter(state_weight_grad.astype(jnp.bfloat16), 'seq', scatter_d...  54.7 us
    dot_general x1, matrix products, body(): jnp.einsum('hwk,khd->whd', score_grad, seen_keys, preferred_element_type=...  52.2 us
    dot_general x1, matrix products, body(): jnp.einsum('hwk,whd->khd', score_grad, token_heads, preferred_element_typ...  50.7 us
    dot_general x9, matrix products, product_tn(): lax.dot_general(left, right, (((0,), (0,)), ((), ())), preferred_element_...  46.2 us
    reduce_scatter x1, waiting for transfers between devices, body(): lax.psum_scatter(key_grad.astype(jnp.bfloat16), 'seq', scatter_dimension=...  44.7 us
  transfers between devices with their start and end apart: 16, of which 11 were waited for; matrix products, arithmetic and copies ran while one was open for 41% of the time, Pallas kernels for 0%

commit v1 on v0

--- a/solution.py
+++ b/solution.py
@@ -24,41 +24,142 @@
     return lax.ppermute(value, axis, [(source, source + steps) for source in range(first, last)])
 
 
-def entering(value, axis, join, neutral):
-    count, mine = (lax.axis_size(axis), lax.axis_index(axis))
-    pieces = jax.tree.map(lambda part: lax.all_gather(part, axis), value)
-    so_far = jax.tree.map(
-        lambda part, zero: jnp.full_like(part, 0) + jnp.asarray(zero, part.dtype), value, neutral
-    )
-
-    def lap(position, so_far):
-        longer = join(so_far, jax.tree.map(lambda part: part[position], pieces))
-        return jax.tree.map(lambda new, old: jnp.where(position < mine, new, old), longer, so_far)
-
-    return lax.fori_loop(0, count - 1, lap, so_far)
-
-
-def carried_in(x, axis, join, neutral):
+def swapped(value, axis, distance):
     count = lax.axis_size(axis)
-    place = lax.axis_index(axis)
-    ahead = count - 1 - place
-    gathered = jax.tree.map(
-        lambda a, kind: lax.all_gather(a.astype(kind), axis), x, (jnp.bfloat16, jnp.bfloat16)
-    )
-    state = jax.tree.map(lambda a, e: jnp.zeros_like(a) + jnp.asarray(e, a.dtype), x, neutral)
-
-    def one(lap, state):
-        source = count - 1 - lap
-        return join(
-            state,
-            jax.tree.map(
-                lambda a, own: lax.dynamic_index_in_dim(a, source, 0, False).astype(own.dtype),
-                gathered,
-                x,
-            ),
+    return lax.ppermute(value, axis, [(place, place ^ distance) for place in range(count)])
+
+
+def add_low(first, second):
+    return (first.astype(jnp.float32) + second.astype(jnp.float32)).astype(jnp.bfloat16)
+
+
+def pick(value, index, axis):
+    return lax.dynamic_index_in_dim(value, index, axis, False)
+
+
+def scatter_bits(value, bits, names):
+    place = lax.axis_index("seq")
+    names = list(names)
+    for bit in bits:
+        at = names.index(bit)
+        mine = (place >> bit) & 1
+        recv = swapped(pick(value, 1 - mine, at), "seq", 1 << bit)
+        value = add_low(pick(value, mine, at), recv)
+        names.pop(at)
+    return value
+
+
+def weight_scatter(left, right, forward):
+    count = lax.axis_size("seq")
+    levels = count.bit_length() - 1
+    place = lax.axis_index("seq")
+    tokens, rows = left.shape
+    parts = left.reshape(tokens, count // 2, 2, rows // count)
+    mine = place & 1
+    give = product_tn(pick(parts, 1 - mine, 2).reshape(tokens, rows // 2), right).astype(jnp.bfloat16)
+    recv = swapped(give, "seq", 1)
+    keep = product_tn(pick(parts, mine, 2).reshape(tokens, rows // 2), right)
+    total = (keep + recv.astype(jnp.float32)).astype(jnp.bfloat16)
+    total = total.reshape((2,) * (levels - 1) + (rows // count, right.shape[1]))
+    names = list(range(levels - 1, 0, -1))
+    bits = names[::-1] if forward else names
+    return scatter_bits(total, bits, names)
+
+
+def whole_scatter(value, forward):
+    count = lax.axis_size("seq")
+    levels = count.bit_length() - 1
+    names = list(range(levels - 1, -1, -1))
+    value = value.reshape((2,) * levels + (value.shape[0] // count,) + value.shape[1:])
+    bits = [0] + (names[-2::-1] if forward else names[:-1])
+    return scatter_bits(value, bits, names)
+
+
+def sum_over_dp(value):
+    count, place = lax.axis_size("dp"), lax.axis_index("dp")
+    half = count // 2
+    for step in range(half - 1):
+        value = add_low(
+            value,
+            lax.ppermute(value, "dp", [(step, step + 1), (count - 1 - step, count - 2 - step)]),
         )
-
-    return lax.fori_loop(0, ahead, one, state)
+    value = add_low(value, lax.ppermute(value, "dp", [(half - 1, half), (half, half - 1)]))
+    for step in range(half - 2, -1, -1):
+        recv = lax.ppermute(value, "dp", [(step + 1, step), (count - 2 - step, count - 1 - step)])
+        outer = (place == step) | (place == count - 1 - step)
+        value = jnp.where(outer, recv, value)
+    return value.astype(jnp.float32)
+
+
+def halves_of(value, core):
+    return pick(value.reshape((2, NS // 2) + value.shape[1:]), core, 0)
+
+
+def chip_rows(value, chip):
+    return pick(value.reshape((4, NS // 8) + value.shape[1:]), chip, 0)
+
+
+def chips_exchange(value, place):
+    chip = (place >> 1) & 3
+    own = pick(value, chip, 0)
+    came = [own] + [swapped(pick(value, chip ^ far, 0), "seq", 2 * far) for far in (1, 2, 3)]
+    came = jnp.stack(came)
+    return [pick(came, chip ^ source, 0) for source in range(4)]
+
+
+def scan_states(scale, base, forward_products=None):
+    place = lax.axis_index("seq")
+    core = place & 1
+    pair = jnp.stack([scale, base]).astype(jnp.bfloat16)
+    parts = pair.reshape(2, 2, NS // 2, D)
+    recv = swapped(pick(parts, 1 - core, 1), "seq", 1).astype(jnp.float32)
+    own = pick(parts, core, 1).astype(jnp.float32)
+    even = jnp.where(core == 0, own, recv)
+    odd = jnp.where(core == 0, recv, own)
+    chip_scale = odd[0] * even[0]
+    chip_base = odd[0] * even[1] + odd[1]
+    chip_pair = jnp.stack([chip_scale, chip_base]).astype(jnp.bfloat16)
+    chip_pair = chip_pair.reshape(2, 4, NS // 8, D).transpose(1, 0, 2, 3)
+    got = [part.astype(jnp.float32) for part in chips_exchange(chip_pair, place)]
+    enter = [jnp.zeros_like(got[0][1]), got[0][1]]
+    for chip in (1, 2):
+        enter.append(got[chip][0] * enter[-1] + got[chip][1])
+    back = chips_exchange(jnp.stack(enter).astype(jnp.bfloat16), place)
+    before = jnp.concatenate(back, axis=0).astype(jnp.float32)
+    between = even[0] * before + even[1]
+    mine = jnp.where(core == 0, before, between)
+    other = jnp.where(core == 0, between, before).astype(jnp.bfloat16)
+    recv = swapped(other, "seq", 1).astype(jnp.float32)
+    previous = jnp.where(
+        core == 0, jnp.concatenate([mine, recv], axis=0), jnp.concatenate([recv, mine], axis=0)
+    )
+    kept = (even[0], odd[0], [part[0] for part in got])
+    return previous, kept
+
+
+def scan_grads(base, kept):
+    even_scale, odd_scale, chip_scales = kept
+    place = lax.axis_index("seq")
+    core = place & 1
+    parts = base.astype(jnp.bfloat16).reshape(2, NS // 2, D)
+    recv = swapped(pick(parts, 1 - core, 0), "seq", 1).astype(jnp.float32)
+    own = pick(parts, core, 0).astype(jnp.float32)
+    even = jnp.where(core == 0, own, recv)
+    odd = jnp.where(core == 0, recv, own)
+    chip_base = (even_scale * odd + even).astype(jnp.bfloat16).reshape(4, NS // 8, D)
+    got = [part.astype(jnp.float32) for part in chips_exchange(chip_base, place)]
+    enter = [jnp.zeros_like(got[3]), got[3]]
+    for chip in (2, 1):
+        enter.append(chip_scales[chip] * enter[-1] + got[chip])
+    back = chips_exchange(jnp.stack(enter[::-1]).astype(jnp.bfloat16), place)
+    after = jnp.concatenate(back, axis=0).astype(jnp.float32)
+    between = odd_scale * after + odd
+    mine = jnp.where(core == 1, after, between)
+    other = jnp.where(core == 1, between, after).astype(jnp.bfloat16)
+    recv = swapped(other, "seq", 1).astype(jnp.float32)
+    return jnp.where(
+        core == 0, jnp.concatenate([mine, recv], axis=0), jnp.concatenate([recv, mine], axis=0)
+    )
 
 
 def gelu_tanh(upper):
@@ -105,10 +206,6 @@
 
 def split_heads(field):
     return field.reshape(field.shape[0], HEADS, HEAD_DIM)
-
-
-def compose(earlier, later):
-    return (later[0] * earlier[0], later[0] * earlier[1] + later[1])
 
 
 def key_mask(keep_left):
@@ -147,9 +244,8 @@
     queries = product(normed, query_weight).astype(jnp.bfloat16)
     keys = product(normed, key_weight).astype(jnp.bfloat16)
     values = product(normed, value_weight).astype(jnp.bfloat16)
-    left_pair = shifted(jnp.stack([keys, values]), "seq", 1)
-    left_keys = left_pair[0]
-    left_values = left_pair[1]
+    left_keys = shifted(keys, "seq", 1)
+    left_values = shifted(values, "seq", 1)
     query_heads = split_heads(state_queries)
     key_heads = split_heads(keys)
     value_heads = split_heads(values)
@@ -172,9 +268,7 @@
     fresh = (1.0 - forget) * update
     carried_scale = keep * forget
     carried_base = start * forget * initial_state + fresh
-    identity = (jnp.ones((NS, D), jnp.float32), jnp.zeros((NS, D), jnp.float32))
-    prefix = entering((carried_scale, carried_base), "seq", compose, identity)
-    previous = prefix[1]
+    previous, kept_scales = scan_states(carried_scale, carried_base)
     state_in = keep * previous + start * initial_state
     state_out = forget * state_in + fresh
     state_low = state_in.astype(jnp.bfloat16)
@@ -202,15 +296,15 @@
     activated = gelu_tanh(upper).astype(jnp.bfloat16)
     mixed = (hidden + product(activated, down_weight)).astype(jnp.bfloat16)
     cotangent = out_cotangent[0]
-    down_grad = product_tn(activated, cotangent)
+    down_grad = sum_over_dp(weight_scatter(activated, cotangent, True))
     activated_grad = product_nt(cotangent, down_weight).astype(jnp.bfloat16)
     upper_grad = (activated_grad.astype(jnp.float32) * gelu_slope(upper)).astype(jnp.bfloat16)
-    up_grad = product_tn(normed_mlp, upper_grad)
+    up_grad = sum_over_dp(weight_scatter(normed_mlp, upper_grad, False))
     normed_mlp_grad = product_nt(upper_grad, up_weight)
     mlp_gain_grad, hidden_part = rms_back(hidden, mlp_scale, mlp_gain, normed_mlp_grad)
     hidden_grad = hidden_part + cotangent.astype(jnp.float32)
     attended_grad = hidden_grad.astype(jnp.bfloat16)
-    output_grad = product_tn(attended, attended_grad)
+    output_grad = sum_over_dp(weight_scatter(attended, attended_grad, True))
     attended_heads_grad = split_heads(product_nt(attended_grad, output_weight).astype(jnp.bfloat16))
     again = jnp.einsum("whd,khd->hwk", token_heads, seen_keys, preferred_element_type=jnp.float32)
     probs = jnp.exp(jnp.where(valid, again * scale, NEGATIVE) - log_total)
@@ -235,10 +329,8 @@
     state_values_grad = seen_values_grad[2 * W :].astype(jnp.bfloat16)
     direct = product_nt(state_keys_grad, key_weight) + product_nt(state_values_grad, value_weight)
     state_cot = state_cotangent[0, 0]
-    back_scale = keep * forget
     back_base = keep * (forget * state_cot + direct)
-    suffix = carried_in((back_scale, back_base), "seq", compose, identity)
-    incoming = suffix[1]
+    incoming = scan_grads(back_base, kept_scales)
     out_state_grad = state_cot + incoming
     in_state_grad = forget * out_state_grad + direct
     initial_state_grad = start * in_state_grad
@@ -247,7 +339,7 @@
     projected_grad = jnp.concatenate([out_state_grad * (1.0 - forget), gate_grad], axis=1).astype(
         jnp.bfloat16
     )
-    state_weight_grad = product_tn(summary, projected_grad)
+    state_weight_grad = sum_over_dp(weight_scatter(summary, projected_grad, False))
     summary_grad = split_heads(product_nt(projected_grad, state_weight).astype(jnp.bfloat16))
     summary_again = jnp.einsum(
         "nhd,whd->hnw", query_heads, key_heads, preferred_element_type=jnp.float32
@@ -269,16 +361,22 @@
     values_from_summary = jnp.einsum(
         "hnw,nhd->whd", summary_low, summary_grad, preferred_element_type=jnp.float32
     ).reshape(W, D)
-    returned = shifted(
-        jnp.stack([seen_keys_grad[:W], seen_values_grad[:W]]).astype(jnp.bfloat16), "seq", -1
-    ).astype(jnp.float32)
+    returned = (
+        shifted(seen_keys_grad[:W].astype(jnp.bfloat16), "seq", -1).astype(jnp.float32),
+        shifted(seen_values_grad[:W].astype(jnp.bfloat16), "seq", -1).astype(jnp.float32),
+    )
     keys_total = (seen_keys_grad[W : 2 * W] + keys_from_summary + returned[0]).astype(jnp.bfloat16)
     values_total = (seen_values_grad[W : 2 * W] + values_from_summary + returned[1]).astype(
         jnp.bfloat16
     )
-    query_grad = product_tn(normed, queries_grad)
-    key_grad = product_tn(normed, keys_total) + product_tn(state_low, state_keys_grad)
-    value_grad = product_tn(normed, values_total) + product_tn(state_low, state_values_grad)
+    query_grad = sum_over_dp(weight_scatter(normed, queries_grad, False))
+    both = jnp.concatenate([normed, state_low], axis=0)
+    key_grad = sum_over_dp(
+        weight_scatter(both, jnp.concatenate([keys_total, state_keys_grad], axis=0), True)
+    )
+    value_grad = sum_over_dp(
+        weight_scatter(both, jnp.concatenate([values_total, state_values_grad], axis=0), False)
+    )
     normed_grad = (
         product_nt(queries_grad, query_weight)
         + product_nt(keys_total, key_weight)
@@ -286,76 +384,45 @@
     )
     attn_gain_grad, token_part = rms_back(inputs, attn_scale, attn_gain, normed_grad)
     tokens_grad = hidden_grad + token_part
-    whole = (
-        lax.psum_scatter(
-            attn_gain_grad.astype(jnp.bfloat16), "seq", scatter_dimension=0, tiled=True
-        ).astype(jnp.float32),
-        lax.psum_scatter(
-            query_grad.astype(jnp.bfloat16), "seq", scatter_dimension=0, tiled=True
-        ).astype(jnp.float32),
-        lax.psum_scatter(
-            key_grad.astype(jnp.bfloat16), "seq", scatter_dimension=0, tiled=True
-        ).astype(jnp.float32),
-        lax.psum_scatter(
-            value_grad.astype(jnp.bfloat16), "seq", scatter_dimension=0, tiled=True
-        ).astype(jnp.float32),
-        lax.psum_scatter(
-            output_grad.astype(jnp.bfloat16), "seq", scatter_dimension=0, tiled=True
-        ).astype(jnp.float32),
-        lax.psum_scatter(
-            state_queries_grad.astype(jnp.bfloat16), "seq", scatter_dimension=0, tiled=True
-        ).astype(jnp.float32),
-        lax.psum_scatter(
-            state_weight_grad.astype(jnp.bfloat16), "seq", scatter_dimension=0, tiled=True
-        ).astype(jnp.float32),
-        lax.psum_scatter(
-            gate_bias_grad.astype(jnp.bfloat16), "seq", scatter_dimension=0, tiled=True
-        ).astype(jnp.float32),
-        lax.psum_scatter(
-            initial_state_grad.astype(jnp.bfloat16), "seq", scatter_dimension=0, tiled=True
-        ).astype(jnp.float32),
-        lax.psum_scatter(
-            mlp_gain_grad.astype(jnp.bfloat16), "seq", scatter_dimension=0, tiled=True
-        ).astype(jnp.float32),
-        lax.psum_scatter(
-            up_grad.astype(jnp.bfloat16), "seq", scatter_dimension=0, tiled=True
-        ).astype(jnp.float32),
-        lax.psum_scatter(
-            down_grad.astype(jnp.bfloat16), "seq", scatter_dimension=0, tiled=True
-        ).astype(jnp.float32),
-    )
-    summed = tuple(
-        (
-            lax.psum(whole[0].astype(jnp.bfloat16), "dp").astype(jnp.float32),
-            lax.psum(whole[1].astype(jnp.bfloat16), "dp").astype(jnp.float32),
-            lax.psum(whole[2].astype(jnp.bfloat16), "dp").astype(jnp.float32),
-            lax.psum(whole[3].astype(jnp.bfloat16), "dp").astype(jnp.float32),
-            lax.psum(whole[4].astype(jnp.bfloat16), "dp").astype(jnp.float32),
-            lax.psum(whole[5].astype(jnp.bfloat16), "dp").astype(jnp.float32),
-            lax.psum(whole[6].astype(jnp.bfloat16), "dp").astype(jnp.float32),
-            lax.psum(whole[7].astype(jnp.bfloat16), "dp").astype(jnp.float32),
-            lax.psum(whole[8].astype(jnp.bfloat16), "dp").astype(jnp.float32),
-            lax.psum(whole[9].astype(jnp.bfloat16), "dp").astype(jnp.float32),
-            lax.psum(whole[10].astype(jnp.bfloat16), "dp").astype(jnp.float32),
-            lax.psum(whole[11].astype(jnp.bfloat16), "dp").astype(jnp.float32),
-        )
+    count = lax.axis_size("seq")
+    vectors = jnp.stack([attn_gain_grad, gate_bias_grad, mlp_gain_grad]).reshape(3, count, D // count)
+    vectors = vectors.transpose(1, 0, 2).reshape(count, 1, 3 * (D // count))
+    vectors = jnp.pad(vectors, ((0, 0), (0, 7), (0, D - vectors.shape[2])))
+    rest = jnp.concatenate(
+        [
+            state_queries_grad.reshape(count, NS // count, D),
+            initial_state_grad.reshape(count, NS // count, D),
+            vectors,
+        ],
+        axis=1,
+    ).astype(jnp.bfloat16)
+    rest = whole_scatter(rest.reshape(-1, D), True)
+    rest = sum_over_dp(rest)
+    rows, lanes = NS // count, D // count
+    state_queries_grad = rest[:rows]
+    initial_state_grad = rest[rows : 2 * rows]
+    vectors = rest[2 * rows, : 3 * lanes]
+    attn_gain_grad, gate_bias_grad, mlp_gain_grad = (
+        vectors[:lanes],
+        vectors[lanes : 2 * lanes],
+        vectors[2 * lanes :],
     )
     return (
         mixed[None],
         state_out[None, None],
         tokens_grad[None],
-        summed[0],
-        summed[1],
-        summed[2],
-        summed[3],
-        summed[4],
-        summed[5],
-        summed[6],
-        summed[7],
-        summed[8],
-        summed[9],
-        summed[10],
-        summed[11],
+        attn_gain_grad,
+        query_grad,
+        key_grad,
+        value_grad,
+        output_grad,
+        state_queries_grad,
+        state_weight_grad,
+        gate_bias_grad,
+        initial_state_grad,
+        mlp_gain_grad,
+        up_grad,
+        down_grad,
     )
 
 

time: 1160 us -> 840 us (0.72)
  waiting for transfers between devices: 580 us -> 250 us
  local copies, waits for them, and re-layouts: 45.9 us -> 131 us
  starting transfers between devices: 6.38 us -> 76 us
  other arithmetic: 139 us -> 70.2 us
  matrix products: 340 us -> 299 us
  blocking collectives: 25.5 us -> 0 us
  between operations: 16.4 us -> 4.07 us
    reduce_scatter x9 -> x0, waiting for transfers between devices: 305 us -> none  [the longest x1 75.1 us: body(): lax.psum_scatter(up_grad.astype(jnp.bfloat16), 'seq', scatter_dimension=0...]
    ppermute x0 -> x64, waiting for transfers between devices: none -> 250 us  [the longest x40 121 us: swapped(): lax.ppermute(value, axis, [(place, place ^ distance) for place in range(c...]
    all_gather x4 -> x0, waiting for transfers between devices: 171 us -> none  [the longest x2 171 us: entering(): pieces = jax.tree.map(lambda part: lax.all_gather(part, axis), value)]
    psum x1 -> x0, waiting for transfers between devices: 97.9 us -> none  [body(): lax.psum(whole[1].astype(jnp.bfloat16), 'dp').astype(jnp.float32)]
    ppermute x0 -> x64, starting transfers between devices: none -> 65.3 us  [the longest x40 35.5 us: swapped(): lax.ppermute(value, axis, [(place, place ^ distance) for place in range(c...]
    unnamed x117 -> x219, local copies, waits for them, and re-layouts: 14.3 us -> 58.6 us
    select_n x7 -> x1, other arithmetic: 36.1 us -> 2.54 us  [scan_states(): odd = jnp.where(core == 0, recv, own)]
    add x7 -> x0, other arithmetic: 29 us -> none  [compose(): return (later[0] * earlier[0], later[0] * earlier[1] + later[1])]
  transfers between devices with their start and end apart: 16 -> 68, of which waited for: 11 -> 28; matrix products, arithmetic and copies ran while one was open for 41% -> 30% of each run, Pallas kernels for 0% -> 0%
where the time goes in v1:
time: 840 us; the launch traced here: 830 us
  matrix products  299 us (36%)
  waiting for transfers between devices  250 us (30%)
  local copies, waits for them, and re-layouts  131 us (16%)
  starting transfers between devices  76 us (9%)
  other arithmetic  70.2 us (8%)
    ppermute x40, waiting for transfers between devices, swapped(): lax.ppermute(value, axis, [(place, place ^ distance) for place in range(c...  121 us
    ppermute x8, waiting for transfers between devices, sum_over_dp(): lax.ppermute(value, 'dp', [(step + 1, step), (count - 2 - step, count - 1...  75.5 us
    unnamed x219, local copies, waits for them, and re-layouts  58.6 us
    ppermute x8, waiting for transfers between devices, sum_over_dp(): lax.ppermute(value, 'dp', [(step, step + 1), (count - 1 - step, count - 2...  52.7 us
    dot_general x1, matrix products, body(): jnp.einsum('hwk,whd->khd', score_grad, token_heads, preferred_element_typ...  50 us
    dot_general x9, matrix products, product(): return jnp.dot(left, right, preferred_element_type=jnp.float32)  39.3 us
    dot_general x14, matrix products, product_tn(): lax.dot_general(left, right, (((0,), (0,)), ((), ())), preferred_element_...  38.4 us
    dot_general x1, matrix products, body(): jnp.einsum('hwk,khd->whd', score_grad, seen_keys, preferred_element_type=...  37.8 us
  transfers between devices with their start and end apart: 68, of which 28 were waited for; matrix products, arithmetic and copies ran while one was open for 30% of the time, Pallas kernels for 0%

profile of v1, /device:TPU:0, one launch (start us, length us, event | category | flops | bytes accessed | tf_op | source)
XLA Modules:
  0.0 829.8 jit_solution(3106572318314842384)
XLA Ops:
  63.5 7.1 collective-permute-done.3
  108.7 15.6 %fusion.187 = (f32[8,512]{1,0:T(8,128)S(1)}, f32[8,512,1536]{2,1,0:T(8,128)}) fusion(bf16[512,8,128]{0,2,1:T(8,128)(2,1)} %bitcast.512, bf16[1536,8,128]{0,2,1:T(8,128)(2,1)} %bitcast.500, pred[512,1536]{1,0:T(8,128)(4,1)} %fusion.61), kind=kOutput, calls=%fused_computation.374 | convolution fusion | flops 1629483008 | bytes 30162944 | tf_op jit(solution)/shard_map/whd,khd->hwk/dot_general | solution.py:281
  124.2 11.4 %fusion.5 = f32[8,512]{1,0:T(8,128)S(1)} fusion(f32[8,512,1536]{2,1,0:T(8,128)} %get-tuple-element.90, f32[8,512]{1,0:T(8,128)S(1)} %get-tuple-element.89), kind=kLoop, calls=%fused_computation.9 | loop fusion | flops 12578816 | bytes 25198592 | tf_op jit(solution)/shard_map/reduce_sum | solution.py:285
  139.4 12.0 %fusion.100 = bf16[8,128,512]{2,1,0:T(8,128)(2,1)S(1)} fusion(f32[8,512,1536]{2,1,0:T(8,128)} %get-tuple-element.90, f32[8,512]{1,0:T(8,128)S(1)} %fusion.5, f32[8,512]{1,0:T(8,128)S(1)} %get-tuple-element.89, bf16[512,1024]{1,0:T(8,128)(2,1)} %convolution_convert_fusion.9, bf16[512,1024]{1,0:T(8,128)(2,1)} %convolution_convert_fusion.12, ...), kind=kOutput, calls=%fused_computation.171 | convolution fusion | flops 1639448576 | bytes 29392896 | tf_op jit(solution)/shard_map/hwk,khd->whd/dot_general | solution.py:288
  158.0 12.4 %multiply_convert_fusion.2 = (bf16[512,4096]{1,0:T(8,128)(2,1)}, f32[512,4096]{1,0:T(8,128)}) fusion(bf16[512,1024]{1,0:T(8,128)(2,1)S(1)} %multiply_convert_fusion.6, bf16[1024,4096]{1,0:T(8,128)(2,1)} %param.28), kind=kOutput, calls=%fused_computation.34 | convolution fusion | flops 4313841664 | bytes 22020096 | tf_op jit(solution)/shard_map/dot_general | solution.py:179
  170.5 7.8 reshape.363
  178.3 10.8 %fusion.106 = bf16[1,512,1024]{2,1,0:T(8,128)(2,1)} fusion(f32[512,1024]{1,0:T(8,128)} %copy-done.12, bf16[512,4096]{1,0:T(8,128)(2,1)} %get-tuple-element.93, bf16[4096,1024]{1,0:T(8,128)(2,1)} %param.29), kind=kOutput, calls=%fused_computation.181 | convolution fusion | flops 4296015872 | bytes 15728640 | tf_op jit(solution)/shard_map/dot_general | solution.py:179
  189.1 12.3 %fusion.18 = bf16[512,4096]{1,0:T(8,128)(2,1)S(1)} fusion(f32[512,4096]{1,0:T(8,128)} %get-tuple-element.94, bf16[4096,1024]{1,0:T(8,128)(2,1)} %param.29, bf16[1,512,1024]{2,1,0:T(8,128)(2,1)S(1)} %copy-done.68), kind=kOutput, calls=%fused_computation.23 | convolution fusion | flops 4339007488 | bytes 22020096 | tf_op jit(solution)/shard_map/dot_general | solution.py:189
  212.2 13.4 %fusion.191 = (bf16[1536,8,128]{0,2,1:T(8,128)(2,1)}, f32[1536,8,128]{0,2,1:T(8,128)}) fusion(bf16[512,8,128]{0,2,1:T(8,128)(2,1)S(1)} %bitcast.504, f32[8,512,1536]{2,1,0:T(8,128)} %get-tuple-element.90, f32[8,512]{1,0:T(8,128)S(1)} %log_add_fusion.1), kind=kOutput, calls=%fused_computation.376 | convolution fusion | flops 1624768512 | bytes 35667968 | tf_op jit(solution)/shard_map/hwk,whd->khd/dot_general | solution.py:315
  225.6 11.4 %fusion.57 = f32[8,512,1536]{2,1,0:T(8,128)} fusion(bf16[512,8,128]{0,2,1:T(8,128)(2,1)S(1)} %bitcast.505, bf16[512,1024]{1,0:T(8,128)(2,1)S(1)} %copy-done.65, bf16[512,1024]{1,0:T(8,128)(2,1)} %convolution_convert_fusion.12, bf16[512,1024]{1,0:T(8,128)(2,1)} %collective-permute-done), kind=kOutput, calls=%fused_computation.58 | convolution fusion | flops 1620049920 | bytes 29360128 | tf_op jit(solution)/shard_map/whd,khd->hwk/dot_general | solution.py:312
  237.0 37.8 %fusion.97 = bf16[8,128,512]{2,1,0:T(8,128)(2,1)} fusion(bf16[1536,8,128]{0,2,1:T(8,128)(2,1)} %bitcast.501, f32[8,512,1536]{2,1,0:T(8,128)} %fusion.57, f32[8,512,1536]{2,1,0:T(8,128)} %get-tuple-element.90, f32[8,512]{1,0:T(8,128)S(1)} %log_add_fusion.1), kind=kOutput, calls=%fused_computation.169 | convolution fusion | flops 1655182848 | bytes 54542336 | tf_op jit(solution)/shard_map/hwk,khd->whd/dot_general | solution.py:321
  274.8 50.0 %fusion.188 = (bf16[1536,8,128]{0,2,1:T(8,128)(2,1)}, f32[1536,8,128]{0,2,1:T(8,128)}) fusion(bf16[512,8,128]{0,2,1:T(8,128)(2,1)S(1)} %bitcast.513, f32[8,512,1536]{2,1,0:T(8,128)} %fusion.57, f32[8,512,1536]{2,1,0:T(8,128)} %get-tuple-element.90, f32[8,512]{1,0:T(8,128)S(1)} %log_add_fusion.1), kind=kOutput, calls=%fused_computation.375 | convolution fusion | flops 1656231424 | bytes 60833792 | tf_op jit(solution)/shard_map/hwk,whd->khd/dot_general | solution.py:325
  329.5 8.6 %constant_dynamic-slice_fusion.9 = (bf16[1024,4,1,128]{3,2,1,0:T(2,128)(2,1)}, bf16[1024,4,1,128]{3,2,1,0:T(2,128)(2,1)}) fusion(bf16[1024,4,2,128]{3,2,1,0:T(2,128)(2,1)} %reshape.348, s32[]{:T(128)S(6)} %select_n.240, s32[]{:T(128)S(6)} %select_n.239), kind=kLoop, calls=%fused_computation.323 | loop fusion | bytes 4194312 | tf_op jit(solution)/shard_map/jit(dynamic_index_in_dim)/dynamic_slice | solution.py:37
  350.5 11.5 %constant_dynamic-slice_fusion.1 = (bf16[512,4,1,512]{3,2,1,0:T(2,128)(2,1)}, bf16[512,4,1,512]{3,2,1,0:T(2,128)(2,1)}) fusion(bf16[512,4,2,512]{3,2,1,0:T(2,128)(2,1)} %reshape.363, s32[]{:T(128)S(6)} %select_n.240, s32[]{:T(128)S(6)} %select_n.239), kind=kLoop, calls=%fused_computation.315 | loop fusion | bytes 8388616 | tf_op jit(solution)/shard_map/jit(dynamic_index_in_dim)/dynamic_slice | solution.py:37
  362.0 10.7 %copy.141 = bf16[512,4,1,512]{0,3,1,2:T(8,128)(2,1)} copy(bf16[512,4,1,512]{3,2,1,0:T(2,128)(2,1)} %get-tuple-element.33) | data formatting | bytes 4194304
  372.7 6.4 convolution_convert_fusion.2
  425.3 10.6 %copy.140 = bf16[512,4,1,512]{0,3,1,2:T(8,128)(2,1)} copy(bf16[512,4,1,512]{3,2,1,0:T(2,128)(2,1)} %get-tuple-element.32) | data formatting | bytes 4194304
  474.2 14.3 %fusion.103 = bf16[512,8,128]{0,2,1:T(8,128)(2,1)} fusion(bf16[512,8,128]{0,2,1:T(8,128)(2,1)} %bitcast.521, f32[8,512,512]{1,2,0:T(8,128)} %fusion.121, f32[8,512,512]{2,1,0:T(8,128)} %copy-done.4, f32[8,512]{1,0:T(8,128)S(1)} %copy-done.92), kind=kOutput, calls=%fused_computation.180 | convolution fusion | flops 556274176 | bytes 18890752 | tf_op jit(solution)/shard_map/hnw,whd->nhd/dot_general | solution.py:355
  498.0 15.6 %slice_add_fusion.1 = f32[512,8,128]{0,2,1:T(8,128)} fusion(f32[1536,8,128]{0,2,1:T(8,128)} %get-tuple-element.97, bf16[512,8,128]{0,2,1:T(8,128)(2,1)S(1)} %bitcast.519, f32[8,512,512]{1,2,0:T(8,128)} %fusion.121, f32[8,512,512]{2,1,0:T(8,128)} %copy-done.4, f32[8,512]{1,0:T(8,128)S(1)} %copy-done.92), kind=kOutput, calls=%fused_computation.79 | convolution fusion | flops 556274176 | bytes 38830080 | tf_op jit(solution)/shard_map/hnw,nhd->whd/dot_general | solution.py:358
  558.2 23.3 %collective-permute-done.49 = bf16[128,1024]{1,0:T(8,128)(2,1)S(1)} collective-permute-done((bf16[128,1024]{1,0:T(8,128)(2,1)S(1)}, bf16[128,1024]{1,0:T(8,128)(2,1)S(1)}, u32[]{:S(2)}, u32[]{:S(2)}) %collective-permute-start.49) | collective-permute-done | bytes 262176 | tf_op jit(solution)/shard_map/ppermute | solution.py:88
  588.3 11.8 %collective-permute-done.33 = bf16[2,128,1024]{2,1,0:T(8,128)(2,1)S(1)} collective-permute-done((bf16[2,128,1024]{2,1,0:T(8,128)(2,1)S(1)}, bf16[2,128,1024]{2,1,0:T(8,128)(2,1)S(1)}, u32[]{:S(2)}, u32[]{:S(2)}) %collective-permute-start.33) | collective-permute-done | bytes 524320 | tf_op jit(solution)/shard_map/ppermute | solution.py:29
  601.5 10.5 %collective-permute-done.21 = bf16[2,136,1024]{2,1,0:T(8,128)(2,1)S(1)} collective-permute-done((bf16[2,136,1024]{2,1,0:T(8,128)(2,1)S(1)}, bf16[2,136,1024]{2,1,0:T(8,128)(2,1)S(1)}, u32[]{:S(2)}, u32[]{:S(2)}) %collective-permute-start.21) | collective-permute-done | bytes 557088 | tf_op jit(solution)/shard_map/ppermute | solution.py:29
  643.4 10.5 %collective-permute-done.51 = bf16[2,128,2048]{2,1,0:T(8,128)(2,1)S(1)} collective-permute-done((bf16[2,128,2048]{2,1,0:T(8,128)(2,1)S(1)}, bf16[2,128,2048]{2,1,0:T(8,128)(2,1)S(1)}, u32[]{:S(2)}, u32[]{:S(2)}) %collective-permute-start.51) | collective-permute-done | bytes 1048608 | tf_op jit(solution)/shard_map/ppermute | solution.py:29
  655.9 24.2 %collective-permute-done.63 = bf16[2,512,1024]{2,1,0:T(8,128)(2,1)S(1)} collective-permute-done((bf16[2,512,1024]{2,1,0:T(8,128)(2,1)S(1)}, bf16[2,512,1024]{2,1,0:T(8,128)(2,1)S(1)}, u32[]{:S(2)}, u32[]{:S(2)}) %collective-permute-start.63) | collective-permute-done | bytes 2097184 | tf_op jit(solution)/shard_map/ppermute | solution.py:29
  682.4 13.7 %collective-permute-done.57 = bf16[2,128,4096]{2,1,0:T(8,128)(2,1)S(1)} collective-permute-done((bf16[2,128,4096]{2,1,0:T(8,128)(2,1)S(1)}, bf16[2,128,4096]{2,1,0:T(8,128)(2,1)S(1)}, u32[]{:S(2)}, u32[]{:S(2)}) %collective-permute-start.57) | collective-permute-done | bytes 2097184 | tf_op jit(solution)/shard_map/ppermute | solution.py:29
  701.6 15.0 %collective-permute-done.64 = bf16[512,1024]{1,0:T(8,128)(2,1)S(1)} collective-permute-done((bf16[512,1024]{1,0:T(8,128)(2,1)S(1)}, bf16[512,1024]{1,0:T(8,128)(2,1)S(1)}, u32[]{:S(2)}, u32[]{:S(2)}) %collective-permute-start.64) | collective-permute-done | bytes 1048608 | tf_op jit(solution)/shard_map/ppermute | solution.py:29
  723.1 7.2 collective-permute-done.53
  731.1 21.6 %collective-permute-done.65 = bf16[512,1024]{1,0:T(8,128)(2,1)S(1)} collective-permute-done((bf16[512,1024]{1,0:T(8,128)(2,1)S(1)}, bf16[512,1024]{1,0:T(8,128)(2,1)S(1)}, u32[]{:S(2)}, u32[]{:S(2)}) %collective-permute-start.65) | collective-permute-done | bytes 1048608 | tf_op jit(solution)/shard_map/ppermute | solution.py:84
  753.9 14.9 %collective-permute-done.59 = bf16[128,4096]{1,0:T(8,128)(2,1)S(1)} collective-permute-done((bf16[128,4096]{1,0:T(8,128)(2,1)S(1)}, bf16[128,4096]{1,0:T(8,128)(2,1)S(1)}, u32[]{:S(2)}, u32[]{:S(2)}) %collective-permute-start.59) | collective-permute-done | bytes 1048608 | tf_op jit(solution)/shard_map/ppermute | solution.py:84
  776.0 14.2 %collective-permute-done.55 = bf16[128,2048]{1,0:T(8,128)(2,1)S(1)} collective-permute-done((bf16[128,2048]{1,0:T(8,128)(2,1)S(1)}, bf16[128,2048]{1,0:T(8,128)(2,1)S(1)}, u32[]{:S(2)}, u32[]{:S(2)}) %collective-permute-start.55) | collective-permute-done | bytes 524320 | tf_op jit(solution)/shard_map/ppermute | solution.py:88
  791.3 21.4 %collective-permute-done.67 = bf16[512,1024]{1,0:T(8,128)(2,1)S(1)} collective-permute-done((bf16[512,1024]{1,0:T(8,128)(2,1)S(1)}, bf16[512,1024]{1,0:T(8,128)(2,1)S(1)}, u32[]{:S(2)}, u32[]{:S(2)}) %collective-permute-start.67) | collective-permute-done | bytes 1048608 | tf_op jit(solution)/shard_map/ppermute | solution.py:88
  814.2 13.7 %collective-permute-done.61 = bf16[128,4096]{1,0:T(8,128)(2,1)S(1)} collective-permute-done((bf16[128,4096]{1,0:T(8,128)(2,1)S(1)}, bf16[128,4096]{1,0:T(8,128)(2,1)S(1)}, u32[]{:S(2)}, u32[]{:S(2)}) %collective-permute-start.61) | collective-permute-done | bytes 1048608 | tf_op jit(solution)/shard_map/ppermute | solution.py:88
  (508 shorter events, 343.7 us)
Async XLA Ops:
  33.6 67.0 %collective-permute-start.9 = (bf16[512,1024]{1,0:T(8,128)(2,1)}, bf16[512,1024]{1,0:T(8,128)(2,1)}, u32[]{:S(2)}, u32[]{:S(2)}) collective-permute-start(bf16[512,1024]{1,0:T(8,128)(2,1)} %convolution_convert_fusion.11), channel_id=1, source_target_pairs={{0,4},{4,8},{8,12},{12,16},{16,20},{20,24},{24,28},{1,5},{5,9},{9,... | collective-permute-start | bytes 3145736 | tf_op jit(solution)/shard_map/ppermute | solution.py:24
  36.5 102.9 %collective-permute-start = (bf16[512,1024]{1,0:T(8,128)(2,1)}, bf16[512,1024]{1,0:T(8,128)(2,1)}, u32[]{:S(2)}, u32[]{:S(2)}) collective-permute-start(bf16[512,1024]{1,0:T(8,128)(2,1)} %convolution_convert_fusion.12), channel_id=1, source_target_pairs={{0,4},{4,8},{8,12},{12,16},{16,20},{20,24},{24,28},{1,5},{5,9},{9,... | collective-permute-start | bytes 3145736 | tf_op jit(solution)/shard_map/ppermute | solution.py:24
  349.8 91.0 %collective-permute-start.44 = (bf16[512,1024]{1,0:T(8,128)(2,1)}, bf16[512,1024]{1,0:T(8,128)(2,1)}, u32[]{:S(2)}, u32[]{:S(2)}) collective-permute-start(bf16[512,1024]{1,0:T(8,128)(2,1)} %convolution_convert_fusion.13), channel_id=1, source_target_pairs={{0,4},{4,0},{8,12},{12,8},{16,20},{20,16},{24,28},{28,24},{1,5},{5... | collective-permute-start | bytes 3145736 | tf_op jit(solution)/shard_map/ppermute | solution.py:29
  399.8 45.2 %collective-permute-start.26 = (bf16[512,1024]{1,0:T(8,128)(2,1)}, bf16[512,1024]{1,0:T(8,128)(2,1)}, u32[]{:S(2)}, u32[]{:S(2)}) collective-permute-start(bf16[512,1024]{1,0:T(8,128)(2,1)} %convolution_convert_fusion.14), channel_id=1, source_target_pairs={{0,4},{4,0},{8,12},{12,8},{16,20},{20,16},{24,28},{28,24},{1,5},{5... | collective-permute-start | bytes 3145736 | tf_op jit(solution)/shard_map/ppermute | solution.py:29
  405.2 30.7 %collective-permute-start.16 = (bf16[64,1024]{1,0:T(8,128)(2,1)}, bf16[64,1024]{1,0:T(8,128)(2,1)S(1)}, u32[]{:S(2)}, u32[]{:S(2)}) collective-permute-start(bf16[64,1024]{1,0:T(8,128)(2,1)} %get-tuple-element.72), channel_id=1, source_target_pairs={{0,24},{4,28},{8,16},{12,20},{16,8},{20,12},{24,0},{28,4},{1,25},{... | collective-permute-start | bytes 393224 | tf_op jit(solution)/shard_map/ppermute | solution.py:29
  406.9 29.1 %collective-permute-start.15 = (bf16[64,1024]{1,0:T(8,128)(2,1)}, bf16[64,1024]{1,0:T(8,128)(2,1)S(1)}, u32[]{:S(2)}, u32[]{:S(2)}) collective-permute-start(bf16[64,1024]{1,0:T(8,128)(2,1)} %get-tuple-element.73), channel_id=1, source_target_pairs={{0,16},{4,20},{8,24},{12,28},{16,0},{20,4},{24,8},{28,12},{1,17},{... | collective-permute-start | bytes 393224 | tf_op jit(solution)/shard_map/ppermute | solution.py:29
  407.5 29.0 %collective-permute-start.14 = (bf16[64,1024]{1,0:T(8,128)(2,1)}, bf16[64,1024]{1,0:T(8,128)(2,1)}, u32[]{:S(2)}, u32[]{:S(2)}) collective-permute-start(bf16[64,1024]{1,0:T(8,128)(2,1)} %get-tuple-element.74), channel_id=1, source_target_pairs={{0,8},{4,12},{8,0},{12,4},{16,24},{20,28},{24,16},{28,20},{1,9},{5... | collective-permute-start | bytes 393224 | tf_op jit(solution)/shard_map/ppermute | solution.py:29
  435.9 191.8 %collective-permute-start.62 = (bf16[2048,1024]{1,0:T(8,128)(2,1)}, bf16[2048,1024]{1,0:T(8,128)(2,1)}, u32[]{:S(2)}, u32[]{:S(2)}) collective-permute-start(bf16[2048,1024]{1,0:T(8,128)(2,1)} %convolution_convert_fusion.2), channel_id=1, source_target_pairs={{0,4},{4,0},{8,12},{12,8},{16,20},{20,16},{24,28},{28,24},{1,5},{5... | collective-permute-start | bytes 12582920 | tf_op jit(solution)/shard_map/ppermute | solution.py:29
  436.0 198.3 %collective-permute-start.56 = (bf16[512,4096]{1,0:T(8,128)(2,1)}, bf16[512,4096]{1,0:T(8,128)(2,1)}, u32[]{:S(2)}, u32[]{:S(2)}) collective-permute-start(bf16[512,4096]{1,0:T(8,128)(2,1)} %convolution_convert_fusion.1), channel_id=1, source_target_pairs={{0,4},{4,0},{8,12},{12,8},{16,20},{20,16},{24,28},{28,24},{1,5},{5... | collective-permute-start | bytes 12582920 | tf_op jit(solution)/shard_map/ppermute | solution.py:29
  436.4 55.2 %collective-permute-start.19 = (bf16[512,1024]{0,1:T(8,128)(2,1)}, bf16[512,1024]{0,1:T(8,128)(2,1)}, u32[]{:S(2)}, u32[]{:S(2)}) collective-permute-start(bf16[512,1024]{0,1:T(8,128)(2,1)} %bitcast.555), channel_id=1, source_target_pairs={{4,0},{8,4},{12,8},{16,12},{20,16},{24,20},{28,24},{5,1},{9,5},{13... | collective-permute-start | bytes 3145736 | tf_op jit(solution)/shard_map/ppermute | solution.py:24
  445.0 68.6 %collective-permute-start.18 = (bf16[512,1024]{0,1:T(8,128)(2,1)}, bf16[512,1024]{0,1:T(8,128)(2,1)}, u32[]{:S(2)}, u32[]{:S(2)}) collective-permute-start(bf16[512,1024]{0,1:T(8,128)(2,1)} %bitcast.75), channel_id=1, source_target_pairs={{4,0},{8,4},{12,8},{16,12},{20,16},{24,20},{28,24},{5,1},{9,5},{13... | collective-permute-start | bytes 3145736 | tf_op jit(solution)/shard_map/ppermute | solution.py:24
  449.7 76.1 %collective-permute-start.45 = (bf16[2,128,1024]{2,1,0:T(8,128)(2,1)}, bf16[2,128,1024]{2,1,0:T(8,128)(2,1)}, u32[]{:S(2)}, u32[]{:S(2)}) collective-permute-start(bf16[2,128,1024]{2,1,0:T(8,128)(2,1)} %dynamic-slice_bitcast_fusion.8), channel_id=1, source_target_pairs={{0,8},{4,12},{8,0},{12,4},{16,24},{20,28},{24,16},{28,20},{1,9},{5... | collective-permute-start | bytes 1572872 | tf_op jit(solution)/shard_map/ppermute | solution.py:29
  491.6 36.1 %collective-permute-start.27 = (bf16[2,128,1024]{2,1,0:T(8,128)(2,1)}, bf16[2,128,1024]{2,1,0:T(8,128)(2,1)}, u32[]{:S(2)}, u32[]{:S(2)}) collective-permute-start(bf16[2,128,1024]{2,1,0:T(8,128)(2,1)} %dynamic-slice_bitcast_fusion.11), channel_id=1, source_target_pairs={{0,16},{4,20},{8,24},{12,28},{16,0},{20,4},{24,8},{28,12},{1,17},{... | collective-permute-start | bytes 1572872 | tf_op jit(solution)/shard_map/ppermute | solution.py:29
  513.6 36.5 %collective-permute-start.38 = (bf16[512,1024]{1,0:T(8,128)(2,1)}, bf16[512,1024]{1,0:T(8,128)(2,1)S(1)}, u32[]{:S(2)}, u32[]{:S(2)}) collective-permute-start(bf16[512,1024]{1,0:T(8,128)(2,1)} %convolution_convert_fusion.4), channel_id=1, source_target_pairs={{0,4},{4,0},{8,12},{12,8},{16,20},{20,16},{24,28},{28,24},{1,5},{5... | collective-permute-start | bytes 3145736 | tf_op jit(solution)/shard_map/ppermute | solution.py:29
  552.9 28.6 %collective-permute-start.49 = (bf16[128,1024]{1,0:T(8,128)(2,1)S(1)}, bf16[128,1024]{1,0:T(8,128)(2,1)S(1)}, u32[]{:S(2)}, u32[]{:S(2)}) collective-permute-start(bf16[128,1024]{1,0:T(8,128)(2,1)S(1)} %add_convert_fusion.17), channel_id=1, source_target_pairs={{1,0},{2,3},{5,4},{6,7},{9,8},{10,11},{13,12},{14,15},{17,16},{18,... | collective-permute-start | bytes 786440 | tf_op jit(solution)/shard_map/ppermute | solution.py:88
  554.3 30.9 %collective-permute-start.31 = (bf16[128,1024]{1,0:T(8,128)(2,1)S(1)}, bf16[128,1024]{1,0:T(8,128)(2,1)S(1)}, u32[]{:S(2)}, u32[]{:S(2)}) collective-permute-start(bf16[128,1024]{1,0:T(8,128)(2,1)S(1)} %add_convert_fusion.23), channel_id=1, source_target_pairs={{1,0},{2,3},{5,4},{6,7},{9,8},{10,11},{13,12},{14,15},{17,16},{18,... | collective-permute-start | bytes 786440 | tf_op jit(solution)/shard_map/ppermute | solution.py:88
  557.2 30.0 %collective-permute-start.39 = (bf16[2,128,1024]{2,1,0:T(8,128)(2,1)S(1)}, bf16[2,128,1024]{2,1,0:T(8,128)(2,1)S(1)}, u32[]{:S(2)}, u32[]{:S(2)}) collective-permute-start(bf16[2,128,1024]{2,1,0:T(8,128)(2,1)S(1)} %dynamic-slice_bitcast_fusion.9), channel_id=1, source_target_pairs={{0,16},{4,20},{8,24},{12,28},{16,0},{20,4},{24,8},{28,12},{1,17},{... | collective-permute-start | bytes 1572872 | tf_op jit(solution)/shard_map/ppermute | solution.py:29
  581.5 43.5 %collective-permute-start.50 = (bf16[512,2048]{1,0:T(8,128)(2,1)S(1)}, bf16[512,2048]{1,0:T(8,128)(2,1)S(1)}, u32[]{:S(2)}, u32[]{:S(2)}) collective-permute-start(bf16[512,2048]{1,0:T(8,128)(2,1)S(1)} %convolution_convert_fusion.3), channel_id=1, source_target_pairs={{0,4},{4,0},{8,12},{12,8},{16,20},{20,16},{24,28},{28,24},{1,5},{5... | collective-permute-start | bytes 6291464 | tf_op jit(solution)/shard_map/ppermute | solution.py:29
  587.2 24.7 %collective-permute-start.21 = (bf16[2,136,1024]{2,1,0:T(8,128)(2,1)S(1)}, bf16[2,136,1024]{2,1,0:T(8,128)(2,1)S(1)}, u32[]{:S(2)}, u32[]{:S(2)}) collective-permute-start(bf16[2,136,1024]{2,1,0:T(8,128)(2,1)S(1)} %dynamic-slice_bitcast_fusion.6), channel_id=1, source_target_pairs={{0,8},{4,12},{8,0},{12,4},{16,24},{20,28},{24,16},{28,20},{1,9},{5... | collective-permute-start | bytes 1671176 | tf_op jit(solution)/shard_map/ppermute | solution.py:29
  627.7 26.2 %collective-permute-start.51 = (bf16[2,128,2048]{2,1,0:T(8,128)(2,1)S(1)}, bf16[2,128,2048]{2,1,0:T(8,128)(2,1)S(1)}, u32[]{:S(2)}, u32[]{:S(2)}) collective-permute-start(bf16[2,128,2048]{2,1,0:T(8,128)(2,1)S(1)} %dynamic-slice_bitcast_fusion.5), channel_id=1, source_target_pairs={{0,16},{4,20},{8,24},{12,28},{16,0},{20,4},{24,8},{28,12},{1,17},{... | collective-permute-start | bytes 3145736 | tf_op jit(solution)/shard_map/ppermute | solution.py:29
  634.2 45.9 %collective-permute-start.63 = (bf16[2,512,1024]{2,1,0:T(8,128)(2,1)S(1)}, bf16[2,512,1024]{2,1,0:T(8,128)(2,1)S(1)}, u32[]{:S(2)}, u32[]{:S(2)}) collective-permute-start(bf16[2,512,1024]{2,1,0:T(8,128)(2,1)S(1)} %dynamic-slice_bitcast_fusion), channel_id=1, source_target_pairs={{0,8},{4,12},{8,0},{12,4},{16,24},{20,28},{24,16},{28,20},{1,9},{5... | collective-permute-start | bytes 6291464 | tf_op jit(solution)/shard_map/ppermute | solution.py:29
  640.3 55.7 %collective-permute-start.57 = (bf16[2,128,4096]{2,1,0:T(8,128)(2,1)S(1)}, bf16[2,128,4096]{2,1,0:T(8,128)(2,1)S(1)}, u32[]{:S(2)}, u32[]{:S(2)}) collective-permute-start(bf16[2,128,4096]{2,1,0:T(8,128)(2,1)S(1)} %dynamic-slice_bitcast_fusion.1), channel_id=1, source_target_pairs={{0,16},{4,20},{8,24},{12,28},{16,0},{20,4},{24,8},{28,12},{1,17},{... | collective-permute-start | bytes 6291464 | tf_op jit(solution)/shard_map/ppermute | solution.py:29
  641.8 55.5 %collective-permute-start.36 = (bf16[128,1024]{1,0:T(8,128)(2,1)S(1)}, bf16[128,1024]{1,0:T(8,128)(2,1)S(1)}, u32[]{:S(2)}, u32[]{:S(2)}) collective-permute-start(bf16[128,1024]{1,0:T(8,128)(2,1)S(1)} %add_convert_fusion.22), channel_id=1, source_target_pairs={{1,2},{2,1},{5,6},{6,5},{9,10},{10,9},{13,14},{14,13},{17,18},{18,... | collective-permute-start | bytes 786440 | tf_op jit(solution)/shard_map/ppermute | solution.py:86
  642.6 56.1 %collective-permute-start.24 = (bf16[136,1024]{1,0:T(8,128)(2,1)S(1)}, bf16[136,1024]{1,0:T(8,128)(2,1)S(1)}, u32[]{:S(2)}, u32[]{:S(2)}) collective-permute-start(bf16[136,1024]{1,0:T(8,128)(2,1)S(1)} %add_convert_fusion.16), channel_id=1, source_target_pairs={{1,2},{2,1},{5,6},{6,5},{9,10},{10,9},{13,14},{14,13},{17,18},{18,... | collective-permute-start | bytes 835592 | tf_op jit(solution)/shard_map/ppermute | solution.py:86
  653.9 66.2 %collective-permute-start.43 = (bf16[128,1024]{1,0:T(8,128)(2,1)S(1)}, bf16[128,1024]{1,0:T(8,128)(2,1)S(1)}, u32[]{:S(2)}, u32[]{:S(2)}) collective-permute-start(bf16[128,1024]{1,0:T(8,128)(2,1)S(1)} %add_convert_fusion.19), channel_id=1, source_target_pairs={{1,0},{2,3},{5,4},{6,7},{9,8},{10,11},{13,12},{14,15},{17,16},{18,... | collective-permute-start | bytes 786440 | tf_op jit(solution)/shard_map/ppermute | solution.py:88
  698.7 23.5 %collective-permute-start.37 = (bf16[128,1024]{1,0:T(8,128)(2,1)S(1)}, bf16[128,1024]{1,0:T(8,128)(2,1)S(1)}, u32[]{:S(2)}, u32[]{:S(2)}) collective-permute-start(bf16[128,1024]{1,0:T(8,128)(2,1)S(1)} %add_convert_fusion.21), channel_id=1, source_target_pairs={{1,0},{2,3},{5,4},{6,7},{9,8},{10,11},{13,12},{14,15},{17,16},{18,... | collective-permute-start | bytes 786440 | tf_op jit(solution)/shard_map/ppermute | solution.py:88
  700.1 69.7 %collective-permute-start.25 = (bf16[136,1024]{1,0:T(8,128)(2,1)S(1)}, bf16[136,1024]{1,0:T(8,128)(2,1)S(1)}, u32[]{:S(2)}, u32[]{:S(2)}) collective-permute-start(bf16[136,1024]{1,0:T(8,128)(2,1)S(1)} %add_convert_fusion.15), channel_id=1, source_target_pairs={{1,0},{2,3},{5,4},{6,7},{9,8},{10,11},{13,12},{14,15},{17,16},{18,... | collective-permute-start | bytes 835592 | tf_op jit(solution)/shard_map/ppermute | solution.py:88
  718.4 34.4 %collective-permute-start.65 = (bf16[512,1024]{1,0:T(8,128)(2,1)S(1)}, bf16[512,1024]{1,0:T(8,128)(2,1)S(1)}, u32[]{:S(2)}, u32[]{:S(2)}) collective-permute-start(bf16[512,1024]{1,0:T(8,128)(2,1)S(1)} %fusion.72), channel_id=1, source_target_pairs={{0,1},{3,2},{4,5},{7,6},{8,9},{11,10},{12,13},{15,14},{16,17},{19,... | collective-permute-start | bytes 3145736 | tf_op jit(solution)/shard_map/ppermute | solution.py:84
  720.0 48.8 %collective-permute-start.59 = (bf16[128,4096]{1,0:T(8,128)(2,1)S(1)}, bf16[128,4096]{1,0:T(8,128)(2,1)S(1)}, u32[]{:S(2)}, u32[]{:S(2)}) collective-permute-start(bf16[128,4096]{1,0:T(8,128)(2,1)S(1)} %fusion.73), channel_id=1, source_target_pairs={{0,1},{3,2},{4,5},{7,6},{8,9},{11,10},{12,13},{15,14},{16,17},{19,... | collective-permute-start | bytes 3145736 | tf_op jit(solution)/shard_map/ppermute | solution.py:84
  730.4 40.3 %collective-permute-start.54 = (bf16[128,2048]{1,0:T(8,128)(2,1)S(1)}, bf16[128,2048]{1,0:T(8,128)(2,1)S(1)}, u32[]{:S(2)}, u32[]{:S(2)}) collective-permute-start(bf16[128,2048]{1,0:T(8,128)(2,1)S(1)} %add_convert_fusion.14), channel_id=1, source_target_pairs={{1,2},{2,1},{5,6},{6,5},{9,10},{10,9},{13,14},{14,13},{17,18},{18,... | collective-permute-start | bytes 1572872 | tf_op jit(solution)/shard_map/ppermute | solution.py:86
  772.6 40.1 %collective-permute-start.67 = (bf16[512,1024]{1,0:T(8,128)(2,1)S(1)}, bf16[512,1024]{1,0:T(8,128)(2,1)S(1)}, u32[]{:S(2)}, u32[]{:S(2)}) collective-permute-start(bf16[512,1024]{1,0:T(8,128)(2,1)S(1)} %add_convert_fusion.3), channel_id=1, source_target_pairs={{1,0},{2,3},{5,4},{6,7},{9,8},{10,11},{13,12},{14,15},{17,16},{18,... | collective-permute-start | bytes 3145736 | tf_op jit(solution)/shard_map/ppermute | solution.py:88
  774.2 53.7 %collective-permute-start.61 = (bf16[128,4096]{1,0:T(8,128)(2,1)S(1)}, bf16[128,4096]{1,0:T(8,128)(2,1)S(1)}, u32[]{:S(2)}, u32[]{:S(2)}) collective-permute-start(bf16[128,4096]{1,0:T(8,128)(2,1)S(1)} %add_convert_fusion.5), channel_id=1, source_target_pairs={{1,0},{2,3},{5,4},{6,7},{9,8},{10,11},{13,12},{14,15},{17,16},{18,... | collective-permute-start | bytes 3145736 | tf_op jit(solution)/shard_map/ppermute | solution.py:88
  (142 other events, 994.3 us)

commit v2 on v1

v2 whole, which is shorter than its diff:
```python
import functools
import math

import jax
import jax.numpy as jnp
from jax import lax
from jax.experimental import pallas as pl
from jax.experimental.pallas import tpu as pltpu
from jax.sharding import PartitionSpec as P

D = 1024
HEADS = 8
HEAD_DIM = 128
FF = 4096
W = 512
NS = 512
HALF = NS // 2
QUARTER = NS // 8

EPSILON = 1e-06
NEGATIVE = -1e30
GELU_SCALE = 0.7978845608028654
GELU_CUBIC = 0.044715
SCALE = 1.0 / math.sqrt(HEAD_DIM)
SCALE_LOG2 = SCALE * math.log2(math.e)

BF = jnp.bfloat16
F32 = jnp.float32
MIB = 1 << 20


def swapped(value, axis, distance):
    count = lax.axis_size(axis)
    return lax.ppermute(value, axis, [(place, place ^ distance) for place in range(count)])


def shifted(value, axis, steps):
    count = lax.axis_size(axis)
    first, last = (max(0, -steps), min(count, count - steps))
    return lax.ppermute(value, axis, [(source, source + steps) for source in range(first, last)])


def add_low(*terms):
    total = terms[0].astype(F32)
    for term in terms[1:]:
        total = total + term.astype(F32)
    return total.astype(BF)


def pick(value, index, axis):
    return lax.dynamic_index_in_dim(value, index, axis, False)


def product(left, right):
    return jnp.dot(left, right, preferred_element_type=F32)


def product_tn(left, right):
    return lax.dot_general(left, right, (((0,), (0,)), ((), ())), preferred_element_type=F32)


def product_nt(left, right):
    return lax.dot_general(left, right, (((1,), (1,)), ((), ())), preferred_element_type=F32)


def rms_scale(field):
    return lax.rsqrt(jnp.mean(field * field, axis=-1, keepdims=True) + EPSILON)


def shape(dims, dtype):
    return jax.ShapeDtypeStruct(dims, dtype)


def whole(dims):
    return pl.BlockSpec(dims, lambda *_: (0,) * len(dims))


def fixed(dims):
    return pl.BlockSpec(dims, lambda *_: (0,) * len(dims), pipeline_mode=pl.Buffered(1))


def run(kernel, outs, args, grid, in_specs, out_specs, scratch=(), flops=0, limit=32, flags=None):
    nbytes = sum(math.prod(a.shape) * a.dtype.itemsize for a in args) + sum(
        math.prod(o.shape) * o.dtype.itemsize for o in outs
    )
    prefetch = () if flags is None else (flags,)
    return pl.pallas_call(
        kernel,
        out_shape=outs,
        grid_spec=pltpu.PrefetchScalarGridSpec(
            num_scalar_prefetch=len(prefetch),
            grid=grid,
            in_specs=in_specs,
            out_specs=out_specs,
            scratch_shapes=list(scratch),
        ),
        compiler_params=pltpu.CompilerParams(
            dimension_semantics=("arbitrary",) * len(grid), vmem_limit_bytes=limit * MIB
        ),
        cost_estimate=pl.CostEstimate(
            flops=int(flops), bytes_accessed=int(nbytes), transcendentals=0
        ),
    )(*prefetch, *args)


START, CORE, CHIP = 0, 1, 2


def front_kernel(tokens, gain, wq, wk, wv, normed, queries, pair):
    @pl.when(pl.program_id(0) == 0)
    def _():
        inputs = tokens[...].astype(F32)
        normed[...] = (inputs * rms_scale(inputs) * gain[...]).astype(BF)

    rows = normed[...]
    queries[...] = product(rows, wq[...]).astype(BF)
    pair[0] = product(rows, wk[...]).astype(BF)
    pair[1] = product(rows, wv[...]).astype(BF)


def front(tokens, gain, wq, wk, wv):
    step = 256
    column = pl.BlockSpec((D, step), lambda j: (0, j))
    return run(
        front_kernel,
        (shape((W, D), BF), shape((W, D), BF), shape((2, W, D), BF)),
        (tokens, gain, wq, wk, wv),
        (D // step,),
        [whole((W, D)), whole((1, D)), column, column, column],
        (
            whole((W, D)),
            pl.BlockSpec((W, step), lambda j: (0, j)),
            pl.BlockSpec((2, W, step), lambda j: (0, 0, j)),
        ),
        flops=6 * W * D * D,
    )


def summary_probs_of(keys, asks):
    raw = product_nt(keys, asks) * SCALE_LOG2
    expos = jnp.exp2(raw - jnp.max(raw, axis=0, keepdims=True))
    return expos, jnp.sum(expos, axis=0, keepdims=True)


def gates_kernel(
    flags, asks, pair, wu, wg, bias, initial, summary, forget, update, give, own, work
):
    step = pl.program_id(0)

    @pl.when(step < 4)
    def _():
        for head in range(2):
            at = slice(head * HEAD_DIM, (head + 1) * HEAD_DIM)
            expos, total = summary_probs_of(pair[0, :, at], asks[:, at])
            held = product_tn(pair[1, :, at], expos.astype(BF)) / total
            place = pl.multiple_of(step * 256 + head * HEAD_DIM, HEAD_DIM)
            summary[:, pl.ds(place, HEAD_DIM)] = held.T.astype(BF)

    @pl.when(step >= 4)
    def _():
        start = flags[START].astype(F32)
        rows = summary[...]
        fresh = product(rows, wu[...])
        gate = jax.nn.sigmoid(product(rows, wg[...]) + bias[...])
        update[...] = fresh
        forget[...] = gate
        work[0] = (1.0 - start) * gate
        work[1] = start * gate * initial[...] + (1.0 - gate) * fresh
        mine = pl.multiple_of(flags[CORE] * HALF, HALF)
        others = pl.multiple_of((1 - flags[CORE]) * HALF, HALF)
        for part in range(2):
            own[part] = work[part, pl.ds(mine, HALF)].astype(BF)
            give[part] = work[part, pl.ds(others, HALF)].astype(BF)


def gates(flags, asks, pair, state_weight, bias, initial):
    step = 256
    early = lambda i, *_: (0, jnp.minimum(i, 3))
    late = lambda i, *_: (0, jnp.maximum(i - 4, 0))
    late3 = lambda i, *_: (0, 0, jnp.maximum(i - 4, 0))
    return run(
        gates_kernel,
        (
            shape((NS, D), BF),
            shape((NS, D), F32),
            shape((NS, D), F32),
            shape((2, HALF, D), BF),
            shape((2, HALF, D), BF),
        ),
        (asks, pair, state_weight, state_weight, bias, initial),
        (8,),
        [
            pl.BlockSpec((NS, step), early),
            pl.BlockSpec((2, W, step), lambda i, *_: (0, 0, jnp.minimum(i, 3))),
            pl.BlockSpec((D, step), late),
            pl.BlockSpec((D, step), lambda i, *_: (0, jnp.maximum(i - 4, 0) + D // step)),
            pl.BlockSpec((1, step), late),
            pl.BlockSpec((NS, step), late),
        ],
        (
            whole((NS, D)),
            pl.BlockSpec((NS, step), late),
            pl.BlockSpec((NS, step), late),
            pl.BlockSpec((2, HALF, step), late3),
            pl.BlockSpec((2, HALF, step), late3),
        ),
        [pltpu.VMEM((2, NS, step), F32)],
        flops=4 * NS * W * D + 4 * NS * D * D,
        flags=flags,
    )


def rows_of(chip):
    return pl.ds(pl.multiple_of(chip * QUARTER, QUARTER), QUARTER)


def compose_kernel(flags, own, recv, keep, to1, to2, to3, work):
    odd_core = flags[CORE] == 1
    pick2 = lambda part: (own[part].astype(F32), recv[part].astype(F32))
    (own_scale, recv_scale), (own_base, recv_base) = pick2(0), pick2(1)
    later_scale = jnp.where(odd_core, own_scale, recv_scale)
    earlier_base = jnp.where(odd_core, recv_base, own_base)
    later_base = jnp.where(odd_core, own_base, recv_base)
    work[0] = own_scale * recv_scale
    work[1] = later_scale * earlier_base + later_base
    for far, out in enumerate((keep, to1, to2, to3)):
        out[...] = work[:, rows_of(flags[CHIP] ^ far)].astype(BF)


def prefix_kernel(flags, keep, from1, from2, from3, mine, to1, to2, to3, got, enter):
    for far, came in enumerate((keep, from1, from2, from3)):
        got[flags[CHIP] ^ far] = came[...].astype(F32)
    state = got[0, 1]
    enter[0] = jnp.zeros_like(state)
    enter[1] = state
    for chip in (1, 2):
        state = got[chip, 0] * state + got[chip, 1]
        enter[chip + 1] = state
    for far, out in enumerate((mine, to1, to2, to3)):
        out[...] = enter[flags[CHIP] ^ far].astype(BF)


def previous_kernel(flags, mine, from1, from2, from3, own, recv, keep, give, before):
    for far, came in enumerate((mine, from1, from2, from3)):
        before[rows_of(flags[CHIP] ^ far)] = came[...].astype(F32)
    odd_core = flags[CORE] == 1
    scale = jnp.where(odd_core, recv[0].astype(F32), own[0].astype(F32))
    base = jnp.where(odd_core, recv[1].astype(F32), own[1].astype(F32))
    entry = before[...]
    between = scale * entry + base
    keep[...] = jnp.where(odd_core, between, entry).astype(BF)
    give[...] = jnp.where(odd_core, entry, between).astype(BF)


def compose_back_kernel(flags, own, recv, own_pair, recv_pair, keep, to1, to2, to3, work):
    odd_core = flags[CORE] == 1
    scale = jnp.where(odd_core, recv_pair[0].astype(F32), own_pair[0].astype(F32))
    mine, other = own[...].astype(F32), recv[...].astype(F32)
    work[...] = scale * jnp.where(odd_core, mine, other) + jnp.where(odd_core, other, mine)
    for far, out in enumerate((keep, to1, to2, to3)):
        out[...] = work[rows_of(flags[CHIP] ^ far)].astype(BF)


def suffix_kernel(
    flags, keep, from1, from2, from3, kept0, kept1, kept2, kept3, mine, to1, to2, to3, got, enter
):
    pairs = ((keep, kept0), (from1, kept1), (from2, kept2), (from3, kept3))
    for far, (came, kept) in enumerate(pairs):
        got[flags[CHIP] ^ far, 0] = kept[0].astype(F32)
        got[flags[CHIP] ^ far, 1] = came[...].astype(F32)
    state = got[3, 1]
    enter[3] = jnp.zeros_like(state)
    enter[2] = state
    for chip in (2, 1):
        state = got[chip, 0] * state + got[chip, 1]
        enter[chip - 1] = state
    for far, out in enumerate((mine, to1, to2, to3)):
        out[...] = enter[flags[CHIP] ^ far].astype(BF)


def following_kernel(
    flags, mine, from1, from2, from3, own, recv, own_pair, recv_pair, keep, give, after
):
    for far, came in enumerate((mine, from1, from2, from3)):
        after[rows_of(flags[CHIP] ^ far)] = came[...].astype(F32)
    odd_core = flags[CORE] == 1
    scale = jnp.where(odd_core, own_pair[0].astype(F32), recv_pair[0].astype(F32))
    base = jnp.where(odd_core, own[...].astype(F32), recv[...].astype(F32))
    entry = after[...]
    between = scale * entry + base
    keep[...] = jnp.where(odd_core, entry, between).astype(BF)
    give[...] = jnp.where(odd_core, between, entry).astype(BF)


def small(kernel, outs, args, scratch, flags):
    return run(
        kernel,
        tuple(shape(dims, BF) for dims in outs),
        args,
        (1,),
        [whole(a.shape) for a in args],
        tuple(whole(dims) for dims in outs),
        [pltpu.VMEM(dims, F32) for dims in scratch],
        flops=1,
        limit=16,
        flags=flags,
    )


def to_chips(values):
    return (values[0],) + tuple(
        swapped(value, "seq", 2 * far) for far, value in zip((1, 2, 3), values[1:])
    )


def scan_states(flags, own, give):
    recv = swapped(give, "seq", 1)
    quarters = small(
        compose_kernel, [(2, QUARTER, D)] * 4, (own, recv), [(2, HALF, D)], flags
    )
    got = to_chips(quarters)
    enter = small(
        prefix_kernel, [(QUARTER, D)] * 4, got, [(4, 2, QUARTER, D), (4, QUARTER, D)], flags
    )
    back = to_chips(enter)
    mine, other = small(
        previous_kernel, [(HALF, D)] * 2, back + (own, recv), [(HALF, D)], flags
    )
    return mine, swapped(other, "seq", 1), (own, recv, got)


def scan_grads(flags, own, give, kept):
    own_pair, recv_pair, kept_chips = kept
    recv = swapped(give, "seq", 1)
    quarters = small(
        compose_back_kernel,
        [(QUARTER, D)] * 4,
        (own, recv, own_pair, recv_pair),
        [(HALF, D)],
        flags,
    )
    got = to_chips(quarters)
    enter = small(
        suffix_kernel,
        [(QUARTER, D)] * 4,
        got + kept_chips,
        [(4, 2, QUARTER, D), (4, QUARTER, D)],
        flags,
    )
    back = to_chips(enter)
    mine, other = small(
        following_kernel,
        [(HALF, D)] * 2,
        back + (own, recv, own_pair, recv_pair),
        [(HALF, D)],
        flags,
    )
    return mine, swapped(other, "seq", 1)


def state_kernel(
    flags, mine, other, initial, forget, update, wk, wv, state_in, state_low, state_out, pair
):
    @pl.when(pl.program_id(0) == 0)
    def _():
        start = flags[START].astype(F32)
        for core, came in ((flags[CORE], mine), (1 - flags[CORE], other)):
            rows = pl.ds(pl.multiple_of(core * HALF, HALF), HALF)
            entry = (1.0 - start) * came[...].astype(F32) + start * initial[rows, :]
            gate = forget[rows, :]
            state_in[rows, :] = entry
            state_low[rows, :] = entry.astype(BF)
            state_out[rows, :] = gate * entry + (1.0 - gate) * update[rows, :]

    rows = state_low[...]
    pair[0] = product(rows, wk[...]).astype(BF)
    pair[1] = product(rows, wv[...]).astype(BF)


def state_pair(flags, mine, other, initial, forget, update, wk, wv):
    step = 256
    column = pl.BlockSpec((D, step), lambda j, *_: (0, j))
    return run(
        state_kernel,
        (shape((NS, D), F32), shape((NS, D), BF), shape((NS, D), F32), shape((2, NS, D), BF)),
        (mine, other, initial, forget, update, wk, wv),
        (D // step,),
        [whole((HALF, D))] * 2 + [whole((NS, D))] * 3 + [column, column],
        (
            whole((NS, D)),
            whole((NS, D)),
            whole((NS, D)),
            pl.BlockSpec((2, NS, step), lambda j, *_: (0, 0, j)),
        ),
        flops=4 * NS * D * D,
        flags=flags,
    )


def masked_scores(flags, queries, left, own, state):
    seen = []
    left_bias = jnp.where(flags[START] == 0, 0.0, NEGATIVE).astype(F32)
    seen.append(product_nt(left[0], queries) * SCALE_LOG2 + left_bias)
    rows = lax.broadcasted_iota(jnp.int32, (W, W), 0)
    cols = lax.broadcasted_iota(jnp.int32, (W, W), 1)
    seen.append(jnp.where(rows <= cols, product_nt(own[0], queries) * SCALE_LOG2, NEGATIVE))
    seen.append(product_nt(state[0], queries) * SCALE_LOG2)
    return seen


def attend_kernel(flags, queries, left, own, state, attended, lse):
    seen = masked_scores(flags, queries[...], left, own, state)
    peak = functools.reduce(
        jnp.maximum, [jnp.max(part, axis=0, keepdims=True) for part in seen]
    )
    held = 0.0
    total = 0.0
    for part, pair in zip(seen, (left, own, state)):
        expos = jnp.exp2(part - peak)
        total = total + jnp.sum(expos, axis=0, keepdims=True)
        held = held + product_tn(pair[1], expos.astype(BF))
    attended[...] = (held / total).T.astype(BF)
    lse[0] = peak + jnp.log2(total)


def attend(flags, queries, left, own, state):
    head = pl.BlockSpec((W, HEAD_DIM), lambda h, *_: (0, h))
    pair = pl.BlockSpec((2, W, HEAD_DIM), lambda h, *_: (0, 0, h))
    return run(
        attend_kernel,
        (shape((W, D), BF), shape((HEADS, 1, W), F32)),
        (queries, left, own, state),
        (HEADS,),
        [head, pair, pair, pair],
        (head, pl.BlockSpec((1, 1, W), lambda h, *_: (h, 0, 0))),
        flops=4 * W * (2 * W + NS) * D,
        flags=flags,
    )


def attend_back_kernel(
    flags, queries, left, own, state, grad, lse, queries_grad, left_grad, own_grad, state_grad
):
    asks, out_grad = queries[...], grad[...]
    seen = masked_scores(flags, asks, left, own, state)
    probs = [jnp.exp2(part - lse[0]) for part in seen]
    pairs = (left, own, state)
    prob_grads = [product_nt(pair[1], out_grad) for pair in pairs]
    rowdot = sum(
        jnp.sum(prob * prob_grad, axis=0, keepdims=True)
        for prob, prob_grad in zip(probs, prob_grads)
    )
    total = 0.0
    for prob, prob_grad, pair, out in zip(
        probs, prob_grads, pairs, (left_grad, own_grad, state_grad)
    ):
        score_grad = (prob * (prob_grad - rowdot)).astype(BF)
        out[0] = (product(score_grad, asks) * SCALE).astype(out.dtype)
        out[1] = product(prob.astype(BF), out_grad).astype(out.dtype)
        total = total + product_tn(pair[0], score_grad)
    queries_grad[...] = (total * SCALE).T.astype(BF)


def attend_back(flags, queries, left, own, state, grad, lse):
    head = pl.BlockSpec((W, HEAD_DIM), lambda h, *_: (0, h))
    pair = pl.BlockSpec((2, W, HEAD_DIM), lambda h, *_: (0, 0, h))
    return run(
        attend_back_kernel,
        (shape((W, D), BF), shape((2, W, D), BF), shape((2, W, D), F32), shape((2, NS, D), BF)),
        (queries, left, own, state, grad, lse),
        (HEADS,),
        [head, pair, pair, pair, head, pl.BlockSpec((1, 1, W), lambda h, *_: (h, 0, 0))],
        (head, pair, pair, pair),
        flops=10 * W * (2 * W + NS) * D,
        limit=48,
        flags=flags,
    )


def gelu_parts(upper):
    square = upper * upper
    inner = GELU_SCALE * (upper + GELU_CUBIC * square * upper)
    bent = jnp.tanh(inner)
    value = 0.5 * upper * (1.0 + bent)
    slope = 0.5 * (1.0 + bent) + 0.5 * upper * (1.0 - bent * bent) * GELU_SCALE * (
        1.0 + 3.0 * GELU_CUBIC * square
    )
    return value, slope


def mlp_kernel(
    attended,
    tokens,
    out_weight,
    gain,
    cotangent,
    up,
    down,
    mixed,
    activated,
    upper_grad,
    normed_mlp,
    hidden_grad,
    attended_grad,
    heads_grad,
    gain_grad,
    hidden,
    total,
    grad,
):
    step = pl.program_id(0)

    @pl.when(step == 0)
    def _():
        field = tokens[...].astype(F32) + product(attended[...], out_weight[...])
        hidden[...] = field
        normed_mlp[...] = (field * rms_scale(field) * gain[...]).astype(BF)
        total[...] = field
        grad[...] = jnp.zeros_like(field)

    value, slope = gelu_parts(product(normed_mlp[...], up[...]))
    value = value.astype(BF)
    activated[...] = value
    total[...] += product(value, down[...])
    back = product_nt(cotangent[...], down[...]).astype(BF).astype(F32)
    back = (back * slope).astype(BF)
    upper_grad[...] = back
    grad[...] += product_nt(back, up[...])

    @pl.when(step == pl.num_programs(0) - 1)
    def _():
        mixed[...] = total[...].astype(BF)
        field = hidden[...]
        scaled = rms_scale(field)
        gain_grad[...] = jnp.sum(grad[...] * field * scaled, axis=0, keepdims=True)
        weighted = grad[...] * gain[...]
        field_grad = (
            cotangent[...].astype(F32)
            + scaled * weighted
            - field
            * (scaled * scaled * scaled * jnp.mean(weighted * field, axis=-1, keepdims=True))
        )
        hidden_grad[...] = field_grad
        low = field_grad.astype(BF)
        attended_grad[...] = low
        heads_grad[...] = product_nt(low, out_weight[...]).astype(BF)


def mlp(attended, tokens, out_weight, gain, cotangent, up, down):
    step = 512
    rows = whole((W, D))
    return run(
        mlp_kernel,
        (
            shape((W, D), BF),
            shape((W, FF), BF),
            shape((W, FF), BF),
            shape((W, D), BF),
            shape((W, D), F32),
            shape((W, D), BF),
            shape((W, D), BF),
            shape((1, D), F32),
        ),
        (attended, tokens, out_weight, gain, cotangent, up, down),
        (FF // step,),
        [
            fixed((W, D)),
            fixed((W, D)),
            fixed((D, D)),
            fixed((1, D)),
            fixed((W, D)),
            pl.BlockSpec((D, step), lambda j: (0, j)),
            pl.BlockSpec((step, D), lambda j: (j, 0)),
        ],
        (
            rows,
            pl.BlockSpec((W, step), lambda j: (0, j)),
            pl.BlockSpec((W, step), lambda j: (0, j)),
            rows,
            rows,
            rows,
            rows,
            whole((1, D)),
        ),
        [pltpu.VMEM((W, D), F32)] * 3,
        flops=8 * W * D * FF + 4 * W * D * D,
        limit=48,
    )


def direct_kernel(flags, state_grad, wk, wv, forget, cotangent, direct, own, give, work):
    grad = product_nt(state_grad[0], wk[...]) + product_nt(state_grad[1], wv[...])
    direct[...] = grad
    keep = 1.0 - flags[START].astype(F32)
    work[...] = keep * (forget[...] * cotangent[...] + grad)
    own[...] = work[pl.ds(pl.multiple_of(flags[CORE] * HALF, HALF), HALF)].astype(BF)
    give[...] = work[pl.ds(pl.multiple_of((1 - flags[CORE]) * HALF, HALF), HALF)].astype(BF)


def direct_grad(flags, state_grad, wk, wv, forget, cotangent):
    step = 256
    row = pl.BlockSpec((step, D), lambda j, *_: (j, 0))
    column = pl.BlockSpec((NS, step), lambda j, *_: (0, j))
    half = pl.BlockSpec((HALF, step), lambda j, *_: (0, j))
    return run(
        direct_kernel,
        (shape((NS, D), F32), shape((HALF, D), BF), shape((HALF, D), BF)),
        (state_grad, wk, wv, forget, cotangent),
        (D // step,),
        [whole((2, NS, D)), row, row, column, column],
        (column, half, half),
        [pltpu.VMEM((NS, step), F32)],
        flops=4 * NS * D * D,
        flags=flags,
    )


def state_back_kernel(
    flags,
    mine,
    other,
    cotangent,
    forget,
    update,
    state_in,
    direct,
    wu,
    wg,
    initial_grad,
    projected_grad,
    bias_grad,
    summary_grad,
    work,
    total,
):
    step = pl.program_id(0)
    for core, came in ((flags[CORE], mine), (1 - flags[CORE], other)):
        work[pl.ds(pl.multiple_of(core * HALF, HALF), HALF)] = came[...].astype(F32)
    out_grad = cotangent[...] + work[...]
    gate = forget[...]
    start = flags[START].astype(F32)
    initial_grad[...] = (start * (gate * out_grad + direct[...])).astype(BF)
    rest = 1.0 - gate
    gate_grad = out_grad * (state_in[...] - update[...]) * gate * rest
    bias_grad[...] = jnp.sum(gate_grad, axis=0, keepdims=True)
    fresh_grad = (out_grad * rest).astype(BF)
    gate_low = gate_grad.astype(BF)
    projected_grad[0] = fresh_grad
    projected_grad[1] = gate_low
    part = product_nt(fresh_grad, wu[...]) + product_nt(gate_low, wg[...])

    @pl.when(step == 0)
    def _():
        total[...] = part

    @pl.when(step > 0)
    def _():
        total[...] += part

    @pl.when(step == pl.num_programs(0) - 1)
    def _():
        summary_grad[...] = total[...].astype(BF)


def state_back(flags, mine, other, cotangent, forget, update, state_in, direct, state_weight):
    step = 256
    column = pl.BlockSpec((NS, step), lambda j, *_: (0, j))
    half = pl.BlockSpec((HALF, step), lambda j, *_: (0, j))
    return run(
        state_back_kernel,
        (
            shape((NS, D), BF),
            shape((2, NS, D), BF),
            shape((1, D), F32),
            shape((NS, D), BF),
        ),
        (mine, other, cotangent, forget, update, state_in, direct, state_weight, state_weight),
        (D // step,),
        [half, half, column, column, column, column, column]
        + [
            pl.BlockSpec((D, step), lambda j, *_: (0, j)),
            pl.BlockSpec((D, step), lambda j, *_: (0, j + D // step)),
        ],
        (
            column,
            pl.BlockSpec((2, NS, step), lambda j, *_: (0, 0, j)),
            pl.BlockSpec((1, step), lambda j, *_: (0, j)),
            whole((NS, D)),
        ),
        [pltpu.VMEM((NS, step), F32), pltpu.VMEM((NS, D), F32)],
        flops=4 * NS * D * D,
        flags=flags,
    )


def summary_back_kernel(asks, pair, grad, own_grad, returned, asks_grad, pair_total):
    queries, out_grad = asks[...], grad[...]
    expos, total = summary_probs_of(pair[0], queries)
    probs = expos * (1.0 / total)
    prob_grad = product_nt(pair[1], out_grad)
    rowdot = jnp.sum(probs * prob_grad, axis=0, keepdims=True)
    score_grad = (probs * (prob_grad - rowdot)).astype(BF)
    asks_grad[...] = (product_tn(pair[0], score_grad) * SCALE).T.astype(BF)
    pair_total[0] = (
        own_grad[0] + returned[0].astype(F32) + product(score_grad, queries) * SCALE
    ).astype(BF)
    pair_total[1] = (
        own_grad[1] + returned[1].astype(F32) + product(probs.astype(BF), out_grad)
    ).astype(BF)


def summary_back(asks, pair, grad, own_grad, returned):
    head = pl.BlockSpec((W, HEAD_DIM), lambda h: (0, h))
    both = pl.BlockSpec((2, W, HEAD_DIM), lambda h: (0, 0, h))
    return run(
        summary_back_kernel,
        (shape((NS, D), BF), shape((2, W, D), BF)),
        (asks, pair, grad, own_grad, returned),
        (HEADS,),
        [head, both, head, both, both],
        (head, both),
        flops=10 * NS * W * D,
    )


def tokens_back_kernel(
    queries_grad, pair_total, wq, wk, wv, tokens, gain, hidden_grad, tokens_grad, gain_grad, total
):
    step = pl.program_id(0)

    @pl.when(step < 2)
    def _():
        part = product_nt(queries_grad[...], wq[...])
        total[...] = jnp.where(step == 0, part, total[...] + part)

    @pl.when((step >= 2) & (step < 4))
    def _():
        total[...] += product_nt(pair_total[0], wk[...])

    @pl.when(step >= 4)
    def _():
        total[...] += product_nt(pair_total[0], wv[...])

    @pl.when(step == 5)
    def _():
        inputs = tokens[...].astype(F32)
        scaled = rms_scale(inputs)
        grad = total[...]
        gain_grad[...] = jnp.sum(grad * inputs * scaled, axis=0, keepdims=True)
        weighted = grad * gain[...]
        tokens_grad[...] = (
            hidden_grad[...]
            + scaled * weighted
            - inputs
            * (scaled * scaled * scaled * jnp.mean(weighted * inputs, axis=-1, keepdims=True))
        )


def tokens_back(queries_grad, pair_total, wq, wk, wv, tokens, gain, hidden_grad):
    step = D // 2
    clamp = lambda i, low: jnp.clip(i - low, 0, 1)
    weight = lambda low: pl.BlockSpec((D, step), lambda i: (0, clamp(i, low)))
    later = lambda i: jnp.maximum(i - 2, 0)
    return run(
        tokens_back_kernel,
        (shape((W, D), F32), shape((1, D), F32)),
        (queries_grad, pair_total, wq, wk, wv, tokens, gain, hidden_grad),
        (6,),
        [
            pl.BlockSpec((W, step), lambda i: (0, clamp(i, 0))),
            pl.BlockSpec((1, W, step), lambda i: (later(i) // 2, 0, later(i) % 2)),
            weight(0),
            weight(2),
            weight(4),
            whole((W, D)),
            whole((1, D)),
            whole((W, D)),
        ],
        (whole((W, D)), whole((1, D))),
        [pltpu.VMEM((W, D), F32)],
        flops=6 * W * D * D,
    )


def weight_kernel(chunk_of, rows, pairs, merge, flags, *refs):
    lefts, rights = refs[: 2 * pairs : 2], refs[1 : 2 * pairs : 2]
    recv = refs[2 * pairs] if merge else None
    outs, work = refs[2 * pairs + merge : -1], refs[-1]

    @pl.when(pl.program_id(0) == 0)
    def _():
        for pair, left in enumerate(lefts):
            for place in range(4):
                chunk = 2 * chunk_of(flags, place) + (
                    flags[CORE] if merge else 1 - flags[CORE]
                )
                block = left[:, pl.ds(pl.multiple_of(chunk * rows, rows), rows)]
                work[pair, place * rows : (place + 1) * rows] = block.T

    total = product(work[0], rights[0][0])
    for pair in range(1, pairs):
        total = total + product(work[pair], rights[pair][0])
    for place in range(4):
        part = total[place * rows : (place + 1) * rows]
        if merge:
            part = part + recv[chunk_of(flags, place)].astype(F32)
            outs[place // 2][place % 2] = part.astype(BF)
        else:
            outs[0][place] = part.astype(BF)


def chunk_natural(flags, place):
    return place


def chunk_along_x(flags, place):
    x = flags[CHIP] & 1
    return 2 * (place % 2) + (1 - x if place < 2 else x)


def chunk_along_y(flags, place):
    y = flags[CHIP] >> 1
    return 2 * (1 - y if place < 2 else y) + place % 2


def weight_part(flags, chunk_of, pairs, recv):
    left, right = pairs[0]
    rows = left.shape[1] // 8
    blocks, tokens, width = right.shape
    columns = blocks * width
    step = 512
    per = width // step
    specs, args = [], []
    for one, two in pairs:
        specs += [
            fixed(one.shape),
            pl.BlockSpec((1, tokens, step), lambda j, *_: (j // per, 0, j % per)),
        ]
        args += [one, two]
    merge = recv is not None
    if merge:
        specs.append(pl.BlockSpec((4, rows, step), lambda j, *_: (0, 0, j)))
        args.append(recv)
        outs = (shape((2, rows, columns), BF),) * 2
        out_specs = (pl.BlockSpec((2, rows, step), lambda j, *_: (0, 0, j)),) * 2
    else:
        outs = (shape((4, rows, columns), BF),)
        out_specs = (pl.BlockSpec((4, rows, step), lambda j, *_: (0, 0, j)),)
    return run(
        functools.partial(weight_kernel, chunk_of, rows, len(pairs), int(merge)),
        outs,
        tuple(args),
        (columns // step,),
        specs,
        out_specs,
        [pltpu.VMEM((len(pairs), 4 * rows, tokens), BF)],
        flops=len(pairs) * tokens * left.shape[1] * columns,
        flags=flags,
        limit=40,
    )


def scatter_bits(value, bits, names):
    place = lax.axis_index("seq")
    names = list(names)
    for bit in bits:
        at = names.index(bit)
        mine = (place >> bit) & 1
        recv = swapped(pick(value, 1 - mine, at), "seq", 1 << bit)
        value = add_low(pick(value, mine, at), recv)
        names.pop(at)
    return value


def whole_scatter(value, along_x):
    count = lax.axis_size("seq")
    levels = count.bit_length() - 1
    names = list(range(levels - 1, -1, -1))
    value = value.reshape((2,) * levels + (value.shape[0] // count,) + value.shape[1:])
    bits = [0] + (names[-2::-1] if along_x else names[:-1])
    return scatter_bits(value, bits, names)


def weight_scatter(flags, pairs, along_x):
    count = lax.axis_size("seq")
    rows = pairs[0][0].shape[1] // count
    if count != 8:
        total = sum(
            product_tn(left, right.transpose(1, 0, 2).reshape(left.shape[0], -1))
            for left, right in pairs
        )
        return whole_scatter(total.astype(BF), along_x)
    (give,) = weight_part(flags, chunk_natural, pairs, None)
    recv = swapped(give, "seq", 1)
    send, keep = weight_part(flags, chunk_along_x if along_x else chunk_along_y, pairs, recv)
    near, far = (2, 4) if along_x else (4, 2)
    recv = swapped(send, "seq", near)
    mine = (flags[CHIP] >> 1) & 1 if along_x else flags[CHIP] & 1
    send = add_low(pick(keep, 1 - mine, 0), pick(recv, 1 - mine, 0))
    last = swapped(send, "seq", far)
    return add_low(pick(keep, mine, 0), pick(recv, mine, 0), last)


def sum_over_dp(value):
    count, place = lax.axis_size("dp"), lax.axis_index("dp")
    half = count // 2
    for step in range(half - 1):
        value = add_low(
            value,
            lax.ppermute(value, "dp", [(step, step + 1), (count - 1 - step, count - 2 - step)]),
        )
    value = add_low(value, lax.ppermute(value, "dp", [(half - 1, half), (half, half - 1)]))
    for step in range(half - 2, -1, -1):
        recv = lax.ppermute(value, "dp", [(step + 1, step), (count - 2 - step, count - 1 - step)])
        outer = (place == step) | (place == count - 1 - step)
        value = jnp.where(outer, recv, value)
    return value.astype(F32)


def body(
    tokens,
    item_starts,
    attn_gain,
    query_weight,
    key_weight,
    value_weight,
    output_weight,
    state_queries,
    state_weight,
    gate_bias,
    initial_state,
    mlp_gain,
    up_weight,
    down_weight,
    out_cotangent,
    state_cotangent,
):
    count = lax.axis_size("seq")
    place = lax.axis_index("seq")
    flags = jnp.stack([item_starts[0, 0], place & 1, (place >> 1) & 3]).astype(jnp.int32)
    tokens, cotangent, state_cot = tokens[0], out_cotangent[0], state_cotangent[0, 0]
    attn_gain, gate_bias, mlp_gain = attn_gain[None], gate_bias[None], mlp_gain[None]

    normed, queries, own = front(tokens, attn_gain, query_weight, key_weight, value_weight)
    left = shifted(own, "seq", 1)
    summary, forget, update, give_scan, own_scan = gates(
        flags, state_queries, own, state_weight, gate_bias, initial_state
    )
    mine, other, kept = scan_states(flags, own_scan, give_scan)
    state_in, state_low, state_out, state = state_pair(
        flags, mine, other, initial_state, forget, update, key_weight, value_weight
    )
    attended, lse = attend(flags, queries, left, own, state)
    (
        mixed,
        activated,
        upper_grad,
        normed_mlp,
        hidden_grad,
        attended_grad,
        heads_grad,
        mlp_gain_grad,
    ) = mlp(attended, tokens, output_weight, mlp_gain, cotangent, up_weight, down_weight)

    down_grad = weight_scatter(flags, [(activated, cotangent[None])], True)
    up_grad = weight_scatter(flags, [(normed_mlp, upper_grad[None])], False)
    output_grad = weight_scatter(flags, [(attended, attended_grad[None])], True)

    queries_grad, left_grad, own_grad, state_grad = attend_back(
        flags, queries, left, own, state, heads_grad, lse
    )
    query_grad = weight_scatter(flags, [(normed, queries_grad[None])], False)
    returned = shifted(left_grad, "seq", -1)
    direct, own_scan, give_scan = direct_grad(
        flags, state_grad, key_weight, value_weight, forget, state_cot
    )
    mine, other = scan_grads(flags, own_scan, give_scan, kept)
    initial_grad, projected_grad, gate_bias_grad, summary_grad = state_back(
        flags, mine, other, state_cot, forget, update, state_in, direct, state_weight
    )
    state_weight_grad = weight_scatter(flags, [(summary, projected_grad)], True)
    state_queries_grad, pair_total = summary_back(
        state_queries, own, summary_grad, own_grad, returned
    )
    pair_grad = weight_scatter(flags, [(normed, pair_total), (state_low, state_grad)], False)
    tokens_grad, attn_gain_grad = tokens_back(
        queries_grad,
        pair_total,
        query_weight,
        key_weight,
        value_weight,
        tokens,
        attn_gain,
        hidden_grad,
    )

    lanes, rows = D // count, NS // count
    vectors = jnp.concatenate([attn_gain_grad, gate_bias_grad, mlp_gain_grad])
    vectors = vectors.reshape(3, count, lanes).transpose(1, 0, 2).reshape(count, 1, 3 * lanes)
    vectors = jnp.pad(vectors, ((0, 0), (0, 7), (0, D - 3 * lanes))).astype(BF)
    rest = jnp.concatenate(
        [
            state_queries_grad.reshape(count, rows, D),
            initial_grad.reshape(count, rows, D),
            vectors,
        ],
        axis=1,
    )
    rest = whole_scatter(rest.reshape(-1, D), True)

    down_grad = sum_over_dp(down_grad)
    up_grad = sum_over_dp(up_grad)
    output_grad = sum_over_dp(output_grad)
    query_grad = sum_over_dp(query_grad)
    state_weight_grad = sum_over_dp(state_weight_grad)
    pair_grad = sum_over_dp(pair_grad)
    rest = sum_over_dp(rest)
    vectors = rest[2 * rows, : 3 * lanes]
    return (
        mixed[None],
        state_out[None, None],
        tokens_grad[None],
        vectors[:lanes],
        query_grad,
        pair_grad[:, :D],
        pair_grad[:, D:],
        output_grad,
        rest[:rows],
        state_weight_grad,
        vectors[lanes : 2 * lanes],
        rest[rows : 2 * rows],
        vectors[2 * lanes :],
        up_grad,
        down_grad,
    )


def solution(mesh):
    in_specs = (
        P("dp", "seq", None),
        P("dp", "seq"),
        P(),
        P(),
        P(),
        P(),
        P(),
        P(),
        P(),
        P(),
        P(),
        P(),
        P(),
        P(),
        P("dp", "seq", None),
        P("dp", "seq", None, None),
    )
    out_specs = (
        P("dp", "seq", None),
        P("dp", "seq", None, None),
        P("dp", "seq", None),
        P("seq"),
        P("seq", None),
        P("seq", None),
        P("seq", None),
        P("seq", None),
        P("seq", None),
        P("seq", None),
        P("seq"),
        P("seq", None),
        P("seq"),
        P("seq", None),
        P("seq", None),
    )
    return jax.shard_map(body, mesh=mesh, in_specs=in_specs, out_specs=out_specs, check_vma=False)
```

time: 840 us -> 593 us (0.71)
  matrix products: 299 us -> 0 us
  Pallas kernels: 0 us -> 192 us
  local copies, waits for them, and re-layouts: 131 us -> 42.3 us
  other arithmetic: 70.2 us -> 24.5 us
    dot_general x44 -> x0, matrix products: 299 us -> none  [the longest x1 50 us: body(): jnp.einsum('hwk,whd->khd', score_grad, token_heads, preferred_element_typ...]
    pallas_call x0 -> x28, Pallas kernels: none -> 192 us  [run(): pl.pallas_call(kernel, out_shape=outs, grid_spec=pltpu.PrefetchScalarGrid...]
    ppermute x40 -> x37, waiting for transfers between devices: 121 us -> 159 us  [swapped(): lax.ppermute(value, axis, [(place, place ^ distance) for place in range(c...]
    reshape x9 -> x0, local copies, waits for them, and re-layouts: 28.6 us -> none  [the longest x6 14.6 us: split_heads(): return field.reshape(field.shape[0], HEADS, HEAD_DIM)]
    dynamic_slice x9 -> x1, local copies, waits for them, and re-layouts: 27.2 us -> 1.19 us  [pick(): return lax.dynamic_index_in_dim(value, index, axis, False)]
    unnamed x219 -> x187, local copies, waits for them, and re-layouts: 58.6 us -> 36.9 us
    ppermute x8 -> x7, waiting for transfers between devices: 75.5 us -> 57 us  [sum_over_dp(): lax.ppermute(value, 'dp', [(step + 1, step), (count - 2 - step, count - 1...]
    ppermute x8 -> x7, waiting for transfers between devices: 52.7 us -> 35.8 us  [sum_over_dp(): lax.ppermute(value, 'dp', [(step, step + 1), (count - 1 - step, count - 2...]
  transfers between devices with their start and end apart: 68 -> 60, of which waited for: 28 -> 28; matrix products, arithmetic and copies ran while one was open for 30% -> 5% of each run, Pallas kernels for 0% -> 18%
where the time goes in v2:
time: 593 us; the launch traced here: 586 us
  waiting for transfers between devices  252 us (42%)
  Pallas kernels  192 us (32%)
  starting transfers between devices  72.4 us (12%)
  local copies, waits for them, and re-layouts  42.3 us (7%)
  other arithmetic  24.5 us (4%)
    pallas_call x28, Pallas kernels, run(): pl.pallas_call(kernel, out_shape=outs, grid_spec=pltpu.PrefetchScalarGrid...  192 us
    ppermute x37, waiting for transfers between devices, swapped(): lax.ppermute(value, axis, [(place, place ^ distance) for place in range(c...  159 us
    ppermute x7, waiting for transfers between devices, sum_over_dp(): lax.ppermute(value, 'dp', [(step + 1, step), (count - 2 - step, count - 1...  57 us
    unnamed x187, local copies, waits for them, and re-layouts  36.9 us
    ppermute x37, starting transfers between devices, swapped(): lax.ppermute(value, axis, [(place, place ^ distance) for place in range(c...  36.8 us
    ppermute x7, waiting for transfers between devices, sum_over_dp(): lax.ppermute(value, 'dp', [(step, step + 1), (count - 1 - step, count - 2...  35.8 us
    convert_element_type x29, other arithmetic, add_low(): return total.astype(BF)  17.4 us
    ppermute x7, starting transfers between devices, sum_over_dp(): lax.ppermute(value, 'dp', [(step, step + 1), (count - 1 - step, count - 2...  17.2 us
  transfers between devices with their start and end apart: 60, of which 28 were waited for; matrix products, arithmetic and copies ran while one was open for 5% of the time, Pallas kernels for 18%

profile of v2, /device:TPU:0, one launch (start us, length us, event | category | flops | bytes accessed | tf_op | source)
XLA Modules:
  0.0 585.9 jit_solution(8575209538420213611)
XLA Ops:
  8.1 6.1 %shard_map.271 = (bf16[512,1024]{1,0:T(8,128)(2,1)S(1)}, bf16[512,1024]{1,0:T(8,128)(2,1)S(1)}, bf16[2,512,1024]{2,1,0:T(8,128)(2,1)}) custom-call(bf16[512,1024]{1,0:T(8,128)(2,1)S(1)} %bitcast.98, f32[1,1024]{1,0:T(1,128)S(1)} %bitcast.104, bf16[1024,1024]{1,0:T(8,128)(2,1)S(1)} %copy-done.50, bf16[1024,1024]{1,0:T(8,128)(2,1)S(1)} %copy-done.2, ...), custom_call_target="tpu_custom_call" | custom-call | flops 3221225472 | bytes 11538432 | tf_op jit(solution)/shard_map/pallas_call | solution.py:87
  14.2 11.8 %shard_map.272 = (bf16[512,1024]{1,0:T(8,128)(2,1)S(1)}, f32[512,1024]{1,0:T(8,128)S(1)}, f32[512,1024]{1,0:T(8,128)S(1)}, bf16[2,256,1024]{2,1,0:T(8,128)(2,1)S(1)}, bf16[2,256,1024]{2,1,0:T(8,128)(2,1)S(1)}) custom-call(s32[3]{0:T(128)S(1)} %pad_add_fusion.flags, bf16[512,1024]{1,0:T(8,128)(2,1)S(1)} %copy-done.29, ...), custom_call_target="tpu_custom_call" | custom-call | flops 3221225472 | bytes 20975616 | tf_op jit(solution)/shard_map/pallas_call | solution.py:87
  34.8 5.6 collective-permute-done.2.from1.kept1
  40.4 26.4 %collective-permute-done.3.from2.kept2 = bf16[2,64,1024]{2,1,0:T(8,128)(2,1)S(1)} collective-permute-done((bf16[2,64,1024]{2,1,0:T(8,128)(2,1)S(1)}, bf16[2,64,1024]{2,1,0:T(8,128)(2,1)S(1)}, u32[]{:S(2)}, u32[]{:S(2)}) %collective-permute-start.3) | collective-permute-done | bytes 262176 | tf_op jit(solution)/shard_map/ppermute | solution.py:34
  81.4 6.1 %shard_map.276 = (f32[512,1024]{1,0:T(8,128)S(1)}, bf16[512,1024]{1,0:T(8,128)(2,1)S(1)}, f32[512,1024]{1,0:T(8,128)}, bf16[2,512,1024]{2,1,0:T(8,128)(2,1)S(1)}) custom-call(s32[3]{0:T(128)S(1)} %pad_add_fusion.flags, bf16[256,1024]{1,0:T(8,128)(2,1)S(1)} %get-tuple-element.96.mine, bf16[256,1024]{1,0:T(8,128)(2,1)S(1)} %collective-permute-done.8.other, ...), custom_call_target="tpu_custom_call" | custom-call | flops 2147483648 | bytes 18874368 | tf_op jit(solution)/shard_map/pallas_call | solution.py:87
  87.5 15.1 %shard_map.277 = (bf16[512,1024]{1,0:T(8,128)(2,1)S(1)}, f32[8,1,512]{2,1,0:T(1,128)S(1)}) custom-call(s32[3]{0:T(128)S(1)} %pad_add_fusion.flags, bf16[512,1024]{1,0:T(8,128)(2,1)S(1)} %get-tuple-element.84.queries, bf16[2,512,1024]{2,1,0:T(8,128)(2,1)S(1)} %collective-permute-done.left, bf16[2,512,1024]{2,1,0:T(8,128)(2,1)} %get-tuple-element.85.pair.own, ...), custom_call_target="tpu_custom_call" | custom-call | flops 3221225472 | bytes 8404992 | tf_op jit(solution)/shard_map/pallas_call | solution.py:87
  102.7 30.1 %shard_map.278 = (bf16[512,1024]{1,0:T(8,128)(2,1)}, bf16[512,4096]{1,0:T(8,128)(2,1)}, bf16[512,4096]{1,0:T(8,128)(2,1)}, bf16[512,1024]{1,0:T(8,128)(2,1)S(1)}...) custom-call(bf16[512,1024]{1,0:T(8,128)(2,1)S(1)} %get-tuple-element, ...), custom_call_target="tpu_custom_call" | custom-call | flops 19327352832 | bytes 36708352 | tf_op jit(solution)/shard_map/pallas_call | solution.py:87
  138.2 24.0 %shard_map.279 = (bf16[512,1024]{1,0:T(8,128)(2,1)S(1)}, bf16[2,512,1024]{2,1,0:T(8,128)(2,1)}, f32[2,512,1024]{2,1,0:T(8,128)}, bf16[2,512,1024]{2,1,0:T(8,128)(2,1)}) custom-call(s32[3]{0:T(128)S(1)} %pad_add_fusion.flags, bf16[512,1024]{1,0:T(8,128)(2,1)S(1)} %copy-done.85, bf16[2,512,1024]{2,1,0:T(8,128)(2,1)} %copy-done.81, ...), custom_call_target="tpu_custom_call" | custom-call | flops 8053063680 | bytes 17842176 | tf_op jit(solution)/shard_map/pallas_call | solution.py:87
  166.8 4.5 shard_map.280
  183.3 11.1 %collective-permute-done.10.from1 = bf16[64,1024]{1,0:T(8,128)(2,1)S(1)} collective-permute-done((bf16[64,1024]{1,0:T(8,128)(2,1)S(1)}, bf16[64,1024]{1,0:T(8,128)(2,1)S(1)}, u32[]{:S(2)}, u32[]{:S(2)}) %collective-permute-start.10) | collective-permute-done | bytes 131104 | tf_op jit(solution)/shard_map/ppermute | solution.py:34
  218.5 5.2 shard_map.297
  224.2 6.6 %shard_map.295 = bf16[4,128,4096]{2,1,0:T(8,128)(2,1)} custom-call(s32[3]{0:T(128)S(1)} %pad_add_fusion.flags, bf16[512,1024]{1,0:T(8,128)(2,1)S(1)} %copy-done.37, bf16[1,512,4096]{2,1,0:T(8,128)(2,1)S(1)} %bitcast.89), custom_call_target="tpu_custom_call" | custom-call | flops 2147483648 | bytes 9437184 | tf_op jit(solution)/shard_map/pallas_call | solution.py:87
  247.1 7.0 %shard_map.284 = (bf16[512,1024]{1,0:T(8,128)(2,1)S(1)}, bf16[2,512,1024]{2,1,0:T(8,128)(2,1)S(1)}, f32[1,1024]{1,0:T(1,128)S(1)}, bf16[512,1024]{1,0:T(8,128)(2,1)S(1)}) custom-call(s32[3]{0:T(128)S(1)} %pad_add_fusion.flags, bf16[256,1024]{1,0:T(8,128)(2,1)S(1)} %copy-done.73, bf16[256,1024]{1,0:T(8,128)(2,1)} %collective-permute-done.16.other, ...), custom_call_target="tpu_custom_call" | custom-call | flops 2147483648 | bytes 24121344 | tf_op jit(solution)/shard_map/pallas_call | solution.py:87
  258.8 13.0 %shard_map.285 = (bf16[512,1024]{1,0:T(8,128)(2,1)S(1)}, bf16[2,512,1024]{2,1,0:T(8,128)(2,1)S(1)}) custom-call(bf16[512,1024]{1,0:T(8,128)(2,1)S(1)} %copy-done.30, bf16[2,512,1024]{2,1,0:T(8,128)(2,1)} %get-tuple-element.85.pair.own, bf16[512,1024]{1,0:T(8,128)(2,1)S(1)} %copy-done.63, f32[2,512,1024]{2,1,0:T(8,128)S(1)} %copy-done.39, ...), custom_call_target="tpu_custom_call" | custom-call | flops 2684354560 | bytes 13631488 | tf_op jit(solution)/shard_map/pallas_call | solution.py:87
  271.8 8.1 %shard_map.286 = (f32[512,1024]{1,0:T(8,128)}, f32[1,1024]{1,0:T(1,128)S(1)}) custom-call(bf16[512,1024]{1,0:T(8,128)(2,1)S(1)} %copy-done.19, bf16[2,512,1024]{2,1,0:T(8,128)(2,1)S(1)} %get-tuple-element.125.pair_total.refs_1_, bf16[1024,1024]{1,0:T(8,128)(2,1)S(1)} %copy-done.51, bf16[1024,1024]{1,0:T(8,128)(2,1)S(1)} %copy-done.3, ...), custom_call_target="tpu_custom_call" | custom-call | flops 3221225472 | bytes 14688256 | tf_op jit(solution)/shard_map/pallas_call | solution.py:87
  286.3 6.2 %collective-permute-done.38 = bf16[128,1024]{1,0:T(8,128)(2,1)} collective-permute-done((bf16[128,1024]{1,0:T(8,128)(2,1)S(1)}, bf16[128,1024]{1,0:T(8,128)(2,1)}, u32[]{:S(2)}, u32[]{:S(2)}) %collective-permute-start.38) | collective-permute-done | bytes 262176 | tf_op jit(solution)/shard_map/ppermute | solution.py:34
  302.2 4.4 collective-permute-start.27
  311.3 4.9 shard_map.289
  317.1 6.1 %collective-permute-done.19 = bf16[2,136,1024]{2,1,0:T(8,128)(2,1)S(1)} collective-permute-done((bf16[2,136,1024]{2,1,0:T(8,128)(2,1)S(1)}, bf16[2,136,1024]{2,1,0:T(8,128)(2,1)S(1)}, u32[]{:S(2)}, u32[]{:S(2)}) %collective-permute-start.19) | collective-permute-done | bytes 557088 | tf_op jit(solution)/shard_map/ppermute | solution.py:34
  334.0 5.1 collective-permute-done.20
  349.6 5.1 shard_map.294
  359.8 6.2 %shard_map.298 = (bf16[2,512,1024]{2,1,0:T(8,128)(2,1)}, bf16[2,512,1024]{2,1,0:T(8,128)(2,1)S(1)}) custom-call(s32[3]{0:T(128)S(1)} %pad_add_fusion.flags, bf16[512,4096]{1,0:T(8,128)(2,1)S(1)} %copy-done.17, bf16[1,512,1024]{2,1,0:T(8,128)(2,1)S(1)} %copy-done.32, bf16[4,512,1024]{2,1,0:T(8,128)(2,1)} %collective-permute-done.54.refs_2_), custom_call_target="tpu_custom_call" | custom-call | flops 2147483648 | bytes 13631488 | tf_op jit(solution)/shard_map/pallas_call | solution.py:87
  369.0 7.7 %shard_map.296 = (bf16[2,128,4096]{2,1,0:T(8,128)(2,1)S(1)}, bf16[2,128,4096]{2,1,0:T(8,128)(2,1)S(1)}) custom-call(s32[3]{0:T(128)S(1)} %pad_add_fusion.flags, bf16[512,1024]{1,0:T(8,128)(2,1)S(1)} %copy-done.38, bf16[1,512,4096]{2,1,0:T(8,128)(2,1)S(1)} %bitcast.90, bf16[4,128,4096]{2,1,0:T(8,128)(2,1)} %collective-permute-done.48.refs_2_), custom_call_target="tpu_custom_call" | custom-call | flops 2147483648 | bytes 13631488 | tf_op jit(solution)/shard_map/pallas_call | solution.py:87
  379.9 5.8 shard_map.290
  390.5 63.0 %collective-permute-done.44 = bf16[128,2048]{1,0:T(8,128)(2,1)S(1)} collective-permute-done((bf16[128,2048]{1,0:T(8,128)(2,1)S(1)}, bf16[128,2048]{1,0:T(8,128)(2,1)S(1)}, u32[]{:S(2)}, u32[]{:S(2)}) %collective-permute-start.44) | collective-permute-done | bytes 524320 | tf_op jit(solution)/shard_map/ppermute | solution.py:34
  465.8 7.6 %collective-permute-done.32 = bf16[128,2048]{1,0:T(8,128)(2,1)S(1)} collective-permute-done((bf16[128,2048]{1,0:T(8,128)(2,1)S(1)}, bf16[128,2048]{1,0:T(8,128)(2,1)S(1)}, u32[]{:S(2)}, u32[]{:S(2)}) %collective-permute-start.32) | collective-permute-done | bytes 524320 | tf_op jit(solution)/shard_map/ppermute | solution.py:34
  481.5 7.6 %collective-permute-done.50 = bf16[128,4096]{1,0:T(8,128)(2,1)S(1)} collective-permute-done((bf16[128,4096]{1,0:T(8,128)(2,1)S(1)}, bf16[128,4096]{1,0:T(8,128)(2,1)S(1)}, u32[]{:S(2)}, u32[]{:S(2)}) %collective-permute-start.50) | collective-permute-done | bytes 1048608 | tf_op jit(solution)/shard_map/ppermute | solution.py:34
  493.5 16.2 %collective-permute-done.57 = bf16[512,1024]{1,0:T(8,128)(2,1)S(1)} collective-permute-done((bf16[512,1024]{1,0:T(8,128)(2,1)S(1)}, bf16[512,1024]{1,0:T(8,128)(2,1)S(1)}, u32[]{:S(2)}, u32[]{:S(2)}) %collective-permute-start.57) | collective-permute-done | bytes 1048608 | tf_op jit(solution)/shard_map/ppermute | solution.py:910
  510.8 15.0 %collective-permute-done.51 = bf16[128,4096]{1,0:T(8,128)(2,1)S(1)} collective-permute-done((bf16[128,4096]{1,0:T(8,128)(2,1)S(1)}, bf16[128,4096]{1,0:T(8,128)(2,1)S(1)}, u32[]{:S(2)}, u32[]{:S(2)}) %collective-permute-start.51) | collective-permute-done | bytes 1048608 | tf_op jit(solution)/shard_map/ppermute | solution.py:910
  532.7 13.6 %collective-permute-done.35 = bf16[128,2048]{1,0:T(8,128)(2,1)S(1)} collective-permute-done((bf16[128,2048]{1,0:T(8,128)(2,1)S(1)}, bf16[128,2048]{1,0:T(8,128)(2,1)S(1)}, u32[]{:S(2)}, u32[]{:S(2)}) %collective-permute-start.35) | collective-permute-done | bytes 524320 | tf_op jit(solution)/shard_map/ppermute | solution.py:914
  547.5 21.3 %collective-permute-done.59 = bf16[512,1024]{1,0:T(8,128)(2,1)S(1)} collective-permute-done((bf16[512,1024]{1,0:T(8,128)(2,1)S(1)}, bf16[512,1024]{1,0:T(8,128)(2,1)S(1)}, u32[]{:S(2)}, u32[]{:S(2)}) %collective-permute-start.59) | collective-permute-done | bytes 1048608 | tf_op jit(solution)/shard_map/ppermute | solution.py:914
  570.2 13.8 %collective-permute-done.53 = bf16[128,4096]{1,0:T(8,128)(2,1)S(1)} collective-permute-done((bf16[128,4096]{1,0:T(8,128)(2,1)S(1)}, bf16[128,4096]{1,0:T(8,128)(2,1)S(1)}, u32[]{:S(2)}, u32[]{:S(2)}) %collective-permute-start.53) | collective-permute-done | bytes 1048608 | tf_op jit(solution)/shard_map/ppermute | solution.py:914
  (352 shorter events, 192.6 us)
Async XLA Ops:
  26.6 60.9 %collective-permute-start = (bf16[2,512,1024]{2,1,0:T(8,128)(2,1)}, bf16[2,512,1024]{2,1,0:T(8,128)(2,1)S(1)}, u32[]{:S(2)}, u32[]{:S(2)}) collective-permute-start(bf16[2,512,1024]{2,1,0:T(8,128)(2,1)} %get-tuple-element.85.pair.own), channel_id=1, source_target_pairs={{0,4},{4,8},{8,12},{12,16},{16,20},{20,24},{24,28},{1,5},{5,9},{9,... | collective-permute-start | bytes 6291464 | tf_op jit(solution)/shard_map/ppermute | solution.py:40
  33.2 33.6 %collective-permute-start.3 = (bf16[2,64,1024]{2,1,0:T(8,128)(2,1)S(1)}, bf16[2,64,1024]{2,1,0:T(8,128)(2,1)S(1)}, u32[]{:S(2)}, u32[]{:S(2)}) collective-permute-start(bf16[2,64,1024]{2,1,0:T(8,128)(2,1)S(1)} %get-tuple-element.90), channel_id=1, source_target_pairs={{0,16},{4,20},{8,24},{12,28},{16,0},{20,4},{24,8},{28,12},{1,17},{... | collective-permute-start | bytes 786440 | tf_op jit(solution)/shard_map/ppermute | solution.py:34
  34.8 32.0 %collective-permute-start.4 = (bf16[2,64,1024]{2,1,0:T(8,128)(2,1)S(1)}, bf16[2,64,1024]{2,1,0:T(8,128)(2,1)S(1)}, u32[]{:S(2)}, u32[]{:S(2)}) collective-permute-start(bf16[2,64,1024]{2,1,0:T(8,128)(2,1)S(1)} %get-tuple-element.91), channel_id=1, source_target_pairs={{0,24},{4,28},{8,16},{12,20},{16,8},{20,12},{24,0},{28,4},{1,25},{... | collective-permute-start | bytes 786440 | tf_op jit(solution)/shard_map/ppermute | solution.py:34
  162.3 95.2 %collective-permute-start.17 = (bf16[2,512,1024]{2,1,0:T(8,128)(2,1)}, bf16[2,512,1024]{2,1,0:T(8,128)(2,1)}, u32[]{:S(2)}, u32[]{:S(2)}) collective-permute-start(bf16[2,512,1024]{2,1,0:T(8,128)(2,1)} %get-tuple-element.124), channel_id=1, source_target_pairs={{4,0},{8,4},{12,8},{16,12},{20,16},{24,20},{28,24},{5,1},{9,5},{13... | collective-permute-start | bytes 6291464 | tf_op jit(solution)/shard_map/ppermute | solution.py:40
  175.0 55.8 %collective-permute-start.36 = (bf16[4,128,1024]{2,1,0:T(8,128)(2,1)}, bf16[4,128,1024]{2,1,0:T(8,128)(2,1)}, u32[]{:S(2)}, u32[]{:S(2)}) collective-permute-start(bf16[4,128,1024]{2,1,0:T(8,128)(2,1)} %shard_map.291), channel_id=1, source_target_pairs={{0,4},{4,0},{8,12},{12,8},{16,20},{20,16},{24,28},{28,24},{1,5},{5... | collective-permute-start | bytes 3145736 | tf_op jit(solution)/shard_map/ppermute | solution.py:34
  177.7 57.8 %collective-permute-start.24 = (bf16[4,128,1024]{2,1,0:T(8,128)(2,1)}, bf16[4,128,1024]{2,1,0:T(8,128)(2,1)}, u32[]{:S(2)}, u32[]{:S(2)}) collective-permute-start(bf16[4,128,1024]{2,1,0:T(8,128)(2,1)} %shard_map.287), channel_id=1, source_target_pairs={{0,4},{4,0},{8,12},{12,8},{16,20},{20,16},{24,28},{28,24},{1,5},{5... | collective-permute-start | bytes 3145736 | tf_op jit(solution)/shard_map/ppermute | solution.py:34
  215.0 24.5 %collective-permute-start.16 = (bf16[256,1024]{1,0:T(8,128)(2,1)}, bf16[256,1024]{1,0:T(8,128)(2,1)}, u32[]{:S(2)}, u32[]{:S(2)}) collective-permute-start(bf16[256,1024]{1,0:T(8,128)(2,1)} %get-tuple-element.119), channel_id=1, source_target_pairs={{0,4},{4,0},{8,12},{12,8},{16,20},{20,16},{24,28},{28,24},{1,5},{5... | collective-permute-start | bytes 1572872 | tf_op jit(solution)/shard_map/ppermute | solution.py:34
  223.7 133.9 %collective-permute-start.54 = (bf16[4,512,1024]{2,1,0:T(8,128)(2,1)}, bf16[4,512,1024]{2,1,0:T(8,128)(2,1)}, u32[]{:S(2)}, u32[]{:S(2)}) collective-permute-start(bf16[4,512,1024]{2,1,0:T(8,128)(2,1)} %shard_map.297), channel_id=1, source_target_pairs={{0,4},{4,0},{8,12},{12,8},{16,20},{20,16},{24,28},{28,24},{1,5},{5... | collective-permute-start | bytes 12582920 | tf_op jit(solution)/shard_map/ppermute | solution.py:34
  230.9 138.1 %collective-permute-start.48 = (bf16[4,128,4096]{2,1,0:T(8,128)(2,1)}, bf16[4,128,4096]{2,1,0:T(8,128)(2,1)}, u32[]{:S(2)}, u32[]{:S(2)}) collective-permute-start(bf16[4,128,4096]{2,1,0:T(8,128)(2,1)} %shard_map.295), channel_id=1, source_target_pairs={{0,4},{4,0},{8,12},{12,8},{16,20},{20,16},{24,28},{28,24},{1,5},{5... | collective-permute-start | bytes 12582920 | tf_op jit(solution)/shard_map/ppermute | solution.py:34
  235.4 47.1 %collective-permute-start.37 = (bf16[2,128,1024]{2,1,0:T(8,128)(2,1)}, bf16[2,128,1024]{2,1,0:T(8,128)(2,1)}, u32[]{:S(2)}, u32[]{:S(2)}) collective-permute-start(bf16[2,128,1024]{2,1,0:T(8,128)(2,1)} %get-tuple-element.141), channel_id=1, source_target_pairs={{0,8},{4,12},{8,0},{12,4},{16,24},{20,28},{24,16},{28,20},{1,9},{5... | collective-permute-start | bytes 1572872 | tf_op jit(solution)/shard_map/ppermute | solution.py:34
  239.5 45.1 %collective-permute-start.25 = (bf16[2,128,1024]{2,1,0:T(8,128)(2,1)}, bf16[2,128,1024]{2,1,0:T(8,128)(2,1)}, u32[]{:S(2)}, u32[]{:S(2)}) collective-permute-start(bf16[2,128,1024]{2,1,0:T(8,128)(2,1)} %get-tuple-element.135), channel_id=1, source_target_pairs={{0,16},{4,20},{8,24},{12,28},{16,0},{20,4},{24,8},{28,12},{1,17},{... | collective-permute-start | bytes 1572872 | tf_op jit(solution)/shard_map/ppermute | solution.py:34
  282.6 24.2 %collective-permute-start.18 = (bf16[2,2,136,1024]{3,2,0,1:T(8,128)(2,1)}, bf16[2,2,136,1024]{3,2,0,1:T(8,128)(2,1)}, u32[]{:S(2)}, u32[]{:S(2)}) collective-permute-start(bf16[2,2,136,1024]{3,2,0,1:T(8,128)(2,1)} %bitcast.85), channel_id=1, source_target_pairs={{0,4},{4,0},{8,12},{12,8},{16,20},{20,16},{24,28},{28,24},{1,5},{5... | collective-permute-start | bytes 3342344 | tf_op jit(solution)/shard_map/ppermute | solution.py:34
  301.0 48.6 %collective-permute-start.42 = (bf16[4,128,2048]{2,1,0:T(8,128)(2,1)}, bf16[4,128,2048]{2,1,0:T(8,128)(2,1)}, u32[]{:S(2)}, u32[]{:S(2)}) collective-permute-start(bf16[4,128,2048]{2,1,0:T(8,128)(2,1)} %shard_map.293), channel_id=1, source_target_pairs={{0,4},{4,0},{8,12},{12,8},{16,20},{20,16},{24,28},{28,24},{1,5},{5... | collective-permute-start | bytes 6291464 | tf_op jit(solution)/shard_map/ppermute | solution.py:34
  325.5 54.4 %collective-permute-start.30 = (bf16[4,128,2048]{2,1,0:T(8,128)(2,1)}, bf16[4,128,2048]{2,1,0:T(8,128)(2,1)}, u32[]{:S(2)}, u32[]{:S(2)}) collective-permute-start(bf16[4,128,2048]{2,1,0:T(8,128)(2,1)} %shard_map.289), channel_id=1, source_target_pairs={{0,4},{4,0},{8,12},{12,8},{16,20},{20,16},{24,28},{28,24},{1,5},{5... | collective-permute-start | bytes 6291464 | tf_op jit(solution)/shard_map/ppermute | solution.py:34
  355.7 31.5 %collective-permute-start.43 = (bf16[2,128,2048]{2,1,0:T(8,128)(2,1)}, bf16[2,128,2048]{2,1,0:T(8,128)(2,1)}, u32[]{:S(2)}, u32[]{:S(2)}) collective-permute-start(bf16[2,128,2048]{2,1,0:T(8,128)(2,1)} %get-tuple-element.145), channel_id=1, source_target_pairs={{0,8},{4,12},{8,0},{12,4},{16,24},{20,28},{24,16},{28,20},{1,9},{5... | collective-permute-start | bytes 3145736 | tf_op jit(solution)/shard_map/ppermute | solution.py:34
  356.1 21.4 %collective-permute-start.22 = (bf16[136,1024]{1,0:T(8,128)(2,1)S(1)}, bf16[136,1024]{1,0:T(8,128)(2,1)}, u32[]{:S(2)}, u32[]{:S(2)}) collective-permute-start(bf16[136,1024]{1,0:T(8,128)(2,1)S(1)} %add_convert_fusion.13), channel_id=1, source_target_pairs={{1,2},{2,1},{5,6},{6,5},{9,10},{10,9},{13,14},{14,13},{17,18},{18,... | collective-permute-start | bytes 835592 | tf_op jit(solution)/shard_map/ppermute | solution.py:912
  367.3 92.0 %collective-permute-start.55 = (bf16[2,512,1024]{2,1,0:T(8,128)(2,1)}, bf16[2,512,1024]{2,1,0:T(8,128)(2,1)S(1)}, u32[]{:S(2)}, u32[]{:S(2)}) collective-permute-start(bf16[2,512,1024]{2,1,0:T(8,128)(2,1)} %get-tuple-element.152), channel_id=1, source_target_pairs={{0,8},{4,12},{8,0},{12,4},{16,24},{20,28},{24,16},{28,20},{1,9},{5... | collective-permute-start | bytes 6291464 | tf_op jit(solution)/shard_map/ppermute | solution.py:34
  376.7 83.8 %collective-permute-start.49 = (bf16[2,128,4096]{2,1,0:T(8,128)(2,1)S(1)}, bf16[2,128,4096]{2,1,0:T(8,128)(2,1)S(1)}, u32[]{:S(2)}, u32[]{:S(2)}) collective-permute-start(bf16[2,128,4096]{2,1,0:T(8,128)(2,1)S(1)} %get-tuple-element.149), channel_id=1, source_target_pairs={{0,16},{4,20},{8,24},{12,28},{16,0},{20,4},{24,8},{28,12},{1,17},{... | collective-permute-start | bytes 6291464 | tf_op jit(solution)/shard_map/ppermute | solution.py:34
  385.7 72.6 %collective-permute-start.31 = (bf16[2,128,2048]{2,1,0:T(8,128)(2,1)S(1)}, bf16[2,128,2048]{2,1,0:T(8,128)(2,1)S(1)}, u32[]{:S(2)}, u32[]{:S(2)}) collective-permute-start(bf16[2,128,2048]{2,1,0:T(8,128)(2,1)S(1)} %get-tuple-element.138), channel_id=1, source_target_pairs={{0,16},{4,20},{8,24},{12,28},{16,0},{20,4},{24,8},{28,12},{1,17},{... | collective-permute-start | bytes 3145736 | tf_op jit(solution)/shard_map/ppermute | solution.py:34
  388.4 65.1 %collective-permute-start.44 = (bf16[128,2048]{1,0:T(8,128)(2,1)S(1)}, bf16[128,2048]{1,0:T(8,128)(2,1)S(1)}, u32[]{:S(2)}, u32[]{:S(2)}) collective-permute-start(bf16[128,2048]{1,0:T(8,128)(2,1)S(1)} %fusion.10), channel_id=1, source_target_pairs={{0,16},{4,20},{8,24},{12,28},{16,0},{20,4},{24,8},{28,12},{1,17},{... | collective-permute-start | bytes 1572872 | tf_op jit(solution)/shard_map/ppermute | solution.py:34
  459.8 19.5 %collective-permute-start.56 = (bf16[512,1024]{1,0:T(8,128)(2,1)S(1)}, bf16[512,1024]{1,0:T(8,128)(2,1)S(1)}, u32[]{:S(2)}, u32[]{:S(2)}) collective-permute-start(bf16[512,1024]{1,0:T(8,128)(2,1)S(1)} %fusion.5), channel_id=1, source_target_pairs={{0,16},{4,20},{8,24},{12,28},{16,0},{20,4},{24,8},{28,12},{1,17},{... | collective-permute-start | bytes 3145736 | tf_op jit(solution)/shard_map/ppermute | solution.py:34
  460.8 28.3 %collective-permute-start.50 = (bf16[128,4096]{1,0:T(8,128)(2,1)S(1)}, bf16[128,4096]{1,0:T(8,128)(2,1)S(1)}, u32[]{:S(2)}, u32[]{:S(2)}) collective-permute-start(bf16[128,4096]{1,0:T(8,128)(2,1)S(1)} %fusion.4), channel_id=1, source_target_pairs={{0,8},{4,12},{8,0},{12,4},{16,24},{20,28},{24,16},{28,20},{1,9},{5... | collective-permute-start | bytes 3145736 | tf_op jit(solution)/shard_map/ppermute | solution.py:34
  465.1 26.1 %collective-permute-start.46 = (bf16[128,2048]{1,0:T(8,128)(2,1)S(1)}, bf16[128,2048]{1,0:T(8,128)(2,1)S(1)}, u32[]{:S(2)}, u32[]{:S(2)}) collective-permute-start(bf16[128,2048]{1,0:T(8,128)(2,1)S(1)} %add_convert_fusion.7), channel_id=1, source_target_pairs={{1,2},{2,1},{5,6},{6,5},{9,10},{10,9},{13,14},{14,13},{17,18},{18,... | collective-permute-start | bytes 1572872 | tf_op jit(solution)/shard_map/ppermute | solution.py:912
  473.7 19.0 %collective-permute-start.33 = (bf16[128,2048]{1,0:T(8,128)(2,1)S(1)}, bf16[128,2048]{1,0:T(8,128)(2,1)S(1)}, u32[]{:S(2)}, u32[]{:S(2)}) collective-permute-start(bf16[128,2048]{1,0:T(8,128)(2,1)S(1)} %fusion.7), channel_id=1, source_target_pairs={{0,1},{3,2},{4,5},{7,6},{8,9},{11,10},{12,13},{15,14},{16,17},{19,... | collective-permute-start | bytes 1572872 | tf_op jit(solution)/shard_map/ppermute | solution.py:910
  479.9 29.8 %collective-permute-start.57 = (bf16[512,1024]{1,0:T(8,128)(2,1)S(1)}, bf16[512,1024]{1,0:T(8,128)(2,1)S(1)}, u32[]{:S(2)}, u32[]{:S(2)}) collective-permute-start(bf16[512,1024]{1,0:T(8,128)(2,1)S(1)} %fusion.1), channel_id=1, source_target_pairs={{0,1},{3,2},{4,5},{7,6},{8,9},{11,10},{12,13},{15,14},{16,17},{19,... | collective-permute-start | bytes 3145736 | tf_op jit(solution)/shard_map/ppermute | solution.py:910
  489.6 36.3 %collective-permute-start.51 = (bf16[128,4096]{1,0:T(8,128)(2,1)S(1)}, bf16[128,4096]{1,0:T(8,128)(2,1)S(1)}, u32[]{:S(2)}, u32[]{:S(2)}) collective-permute-start(bf16[128,4096]{1,0:T(8,128)(2,1)S(1)} %fusion.2), channel_id=1, source_target_pairs={{0,1},{3,2},{4,5},{7,6},{8,9},{11,10},{12,13},{15,14},{16,17},{19,... | collective-permute-start | bytes 3145736 | tf_op jit(solution)/shard_map/ppermute | solution.py:910
  491.3 35.5 %collective-permute-start.47 = (bf16[128,2048]{1,0:T(8,128)(2,1)S(1)}, bf16[128,2048]{1,0:T(8,128)(2,1)S(1)}, u32[]{:S(2)}, u32[]{:S(2)}) collective-permute-start(bf16[128,2048]{1,0:T(8,128)(2,1)S(1)} %add_convert_fusion.6), channel_id=1, source_target_pairs={{1,0},{2,3},{5,4},{6,7},{9,8},{10,11},{13,12},{14,15},{17,16},{18,... | collective-permute-start | bytes 1572872 | tf_op jit(solution)/shard_map/ppermute | solution.py:914
  492.8 35.1 %collective-permute-start.34 = (bf16[128,2048]{1,0:T(8,128)(2,1)S(1)}, bf16[128,2048]{1,0:T(8,128)(2,1)S(1)}, u32[]{:S(2)}, u32[]{:S(2)}) collective-permute-start(bf16[128,2048]{1,0:T(8,128)(2,1)S(1)} %add_convert_fusion.10), channel_id=1, source_target_pairs={{1,2},{2,1},{5,6},{6,5},{9,10},{10,9},{13,14},{14,13},{17,18},{18,... | collective-permute-start | bytes 1572872 | tf_op jit(solution)/shard_map/ppermute | solution.py:912
  510.1 19.3 %collective-permute-start.58 = (bf16[512,1024]{1,0:T(8,128)(2,1)S(1)}, bf16[512,1024]{1,0:T(8,128)(2,1)S(1)}, u32[]{:S(2)}, u32[]{:S(2)}) collective-permute-start(bf16[512,1024]{1,0:T(8,128)(2,1)S(1)} %add_convert_fusion.1), channel_id=1, source_target_pairs={{1,2},{2,1},{5,6},{6,5},{9,10},{10,9},{13,14},{14,13},{17,18},{18,... | collective-permute-start | bytes 3145736 | tf_op jit(solution)/shard_map/ppermute | solution.py:912
  528.1 18.2 %collective-permute-start.35 = (bf16[128,2048]{1,0:T(8,128)(2,1)S(1)}, bf16[128,2048]{1,0:T(8,128)(2,1)S(1)}, u32[]{:S(2)}, u32[]{:S(2)}) collective-permute-start(bf16[128,2048]{1,0:T(8,128)(2,1)S(1)} %add_convert_fusion.9), channel_id=1, source_target_pairs={{1,0},{2,3},{5,4},{6,7},{9,8},{10,11},{13,12},{14,15},{17,16},{18,... | collective-permute-start | bytes 1572872 | tf_op jit(solution)/shard_map/ppermute | solution.py:914
  529.8 39.0 %collective-permute-start.59 = (bf16[512,1024]{1,0:T(8,128)(2,1)S(1)}, bf16[512,1024]{1,0:T(8,128)(2,1)S(1)}, u32[]{:S(2)}, u32[]{:S(2)}) collective-permute-start(bf16[512,1024]{1,0:T(8,128)(2,1)S(1)} %add_convert_fusion), channel_id=1, source_target_pairs={{1,0},{2,3},{5,4},{6,7},{9,8},{10,11},{13,12},{14,15},{17,16},{18,... | collective-permute-start | bytes 3145736 | tf_op jit(solution)/shard_map/ppermute | solution.py:914
  531.4 52.7 %collective-permute-start.53 = (bf16[128,4096]{1,0:T(8,128)(2,1)S(1)}, bf16[128,4096]{1,0:T(8,128)(2,1)S(1)}, u32[]{:S(2)}, u32[]{:S(2)}) collective-permute-start(bf16[128,4096]{1,0:T(8,128)(2,1)S(1)} %add_convert_fusion.3), channel_id=1, source_target_pairs={{1,0},{2,3},{5,4},{6,7},{9,8},{10,11},{13,12},{14,15},{17,16},{18,... | collective-permute-start | bytes 3145736 | tf_op jit(solution)/shard_map/ppermute | solution.py:914
  (120 other events, 1534.7 us)

commit v3 on v2

--- a/solution.py
+++ b/solution.py
@@ -27,6 +27,7 @@
 BF = jnp.bfloat16
 F32 = jnp.float32
 MIB = 1 << 20
+LONG = 1e11
 
 
 def swapped(value, axis, distance):
@@ -79,34 +80,51 @@
     return pl.BlockSpec(dims, lambda *_: (0,) * len(dims), pipeline_mode=pl.Buffered(1))
 
 
-def run(kernel, outs, args, grid, in_specs, out_specs, scratch=(), flops=0, limit=32, flags=None):
-    nbytes = sum(math.prod(a.shape) * a.dtype.itemsize for a in args) + sum(
-        math.prod(o.shape) * o.dtype.itemsize for o in outs
-    )
-    prefetch = () if flags is None else (flags,)
-    return pl.pallas_call(
-        kernel,
-        out_shape=outs,
-        grid_spec=pltpu.PrefetchScalarGridSpec(
-            num_scalar_prefetch=len(prefetch),
-            grid=grid,
-            in_specs=in_specs,
-            out_specs=out_specs,
-            scratch_shapes=list(scratch),
-        ),
-        compiler_params=pltpu.CompilerParams(
-            dimension_semantics=("arbitrary",) * len(grid), vmem_limit_bytes=limit * MIB
-        ),
-        cost_estimate=pl.CostEstimate(
-            flops=int(flops), bytes_accessed=int(nbytes), transcendentals=0
-        ),
-    )(*prefetch, *args)
+class Clock:
+    def __init__(self, flags):
+        self.flags = flags
+
+    def after(self, *values):
+        self.flags = lax.optimization_barrier((self.flags, values))[0]
+
+    def at(self, value):
+        return lax.optimization_barrier((value, self.flags))[0]
+
+    def run(self, kernel, outs, args, grid, in_specs, out_specs, scratch=(), flops=0, limit=24, stream=False):
+        nbytes = sum(math.prod(a.shape) * a.dtype.itemsize for a in args) + sum(
+            math.prod(o.shape) * o.dtype.itemsize for o in outs
+        )
+        args = [
+            pltpu.with_memory_space_constraint(arg, pltpu.HBM)
+            if stream and spec.block_shape != arg.shape
+            else arg
+            for arg, spec in zip(args, in_specs)
+        ]
+        results = pl.pallas_call(
+            kernel,
+            out_shape=outs,
+            grid_spec=pltpu.PrefetchScalarGridSpec(
+                num_scalar_prefetch=1,
+                grid=grid,
+                in_specs=in_specs,
+                out_specs=out_specs,
+                scratch_shapes=list(scratch),
+            ),
+            compiler_params=pltpu.CompilerParams(
+                dimension_semantics=("arbitrary",) * len(grid), vmem_limit_bytes=limit * MIB
+            ),
+            cost_estimate=pl.CostEstimate(
+                flops=int(flops), bytes_accessed=int(nbytes), transcendentals=0
+            ),
+        )(self.flags, *args)
+        self.after(results[0])
+        return results
 
 
 START, CORE, CHIP = 0, 1, 2
 
 
-def front_kernel(tokens, gain, wq, wk, wv, normed, queries, pair):
+def front_kernel(flags, tokens, gain, wq, wk, wv, normed, queries, pair):
     @pl.when(pl.program_id(0) == 0)
     def _():
         inputs = tokens[...].astype(F32)
@@ -118,10 +136,10 @@
     pair[1] = product(rows, wv[...]).astype(BF)
 
 
-def front(tokens, gain, wq, wk, wv):
+def front(clock, tokens, gain, wq, wk, wv):
     step = 256
-    column = pl.BlockSpec((D, step), lambda j: (0, j))
-    return run(
+    column = pl.BlockSpec((D, step), lambda j, *_: (0, j))
+    return clock.run(
         front_kernel,
         (shape((W, D), BF), shape((W, D), BF), shape((2, W, D), BF)),
         (tokens, gain, wq, wk, wv),
@@ -129,11 +147,38 @@
         [whole((W, D)), whole((1, D)), column, column, column],
         (
             whole((W, D)),
-            pl.BlockSpec((W, step), lambda j: (0, j)),
-            pl.BlockSpec((2, W, step), lambda j: (0, 0, j)),
+            pl.BlockSpec((W, step), lambda j, *_: (0, j)),
+            pl.BlockSpec((2, W, step), lambda j, *_: (0, 0, j)),
         ),
         flops=6 * W * D * D,
-    )
+        stream=True,
+    )
+
+
+def left_kernel(flags, tokens, gain, wk, wv, pair, normed):
+    @pl.when(pl.program_id(0) == 0)
+    def _():
+        inputs = tokens[...].astype(F32)
+        normed[...] = (inputs * rms_scale(inputs) * gain[...]).astype(BF)
+
+    rows = normed[...]
+    pair[0] = product(rows, wk[...]).astype(BF)
+    pair[1] = product(rows, wv[...]).astype(BF)
+
+
+def left_pair(clock, tokens, gain, wk, wv):
+    step = 256
+    column = pl.BlockSpec((D, step), lambda j, *_: (0, j))
+    return clock.run(
+        left_kernel,
+        (shape((2, W, D), BF),),
+        (tokens, gain, wk, wv),
+        (D // step,),
+        [whole((W, D)), whole((1, D)), column, column],
+        (pl.BlockSpec((2, W, step), lambda j, *_: (0, 0, j)),),
+        [pltpu.VMEM((W, D), BF)],
+        flops=LONG,
+    )[0]
 
 
 def summary_probs_of(keys, asks):
@@ -173,12 +218,12 @@
             give[part] = work[part, pl.ds(others, HALF)].astype(BF)
 
 
-def gates(flags, asks, pair, state_weight, bias, initial):
+def gates(clock, asks, pair, state_weight, bias, initial):
     step = 256
     early = lambda i, *_: (0, jnp.minimum(i, 3))
     late = lambda i, *_: (0, jnp.maximum(i - 4, 0))
     late3 = lambda i, *_: (0, 0, jnp.maximum(i - 4, 0))
-    return run(
+    return clock.run(
         gates_kernel,
         (
             shape((NS, D), BF),
@@ -206,7 +251,6 @@
         ),
         [pltpu.VMEM((2, NS, step), F32)],
         flops=4 * NS * W * D + 4 * NS * D * D,
-        flags=flags,
     )
 
 
@@ -292,8 +336,8 @@
     give[...] = jnp.where(odd_core, between, entry).astype(BF)
 
 
-def small(kernel, outs, args, scratch, flags):
-    return run(
+def small(clock, kernel, outs, args, scratch):
+    return clock.run(
         kernel,
         tuple(shape(dims, BF) for dims in outs),
         args,
@@ -301,9 +345,7 @@
         [whole(a.shape) for a in args],
         tuple(whole(dims) for dims in outs),
         [pltpu.VMEM(dims, F32) for dims in scratch],
-        flops=1,
-        limit=16,
-        flags=flags,
+        limit=10,
     )
 
 
@@ -313,48 +355,34 @@
     )
 
 
-def scan_states(flags, own, give):
-    recv = swapped(give, "seq", 1)
-    quarters = small(
-        compose_kernel, [(2, QUARTER, D)] * 4, (own, recv), [(2, HALF, D)], flags
-    )
-    got = to_chips(quarters)
-    enter = small(
-        prefix_kernel, [(QUARTER, D)] * 4, got, [(4, 2, QUARTER, D), (4, QUARTER, D)], flags
-    )
-    back = to_chips(enter)
+PAIR_WORK = [(4, 2, QUARTER, D), (4, QUARTER, D)]
+
+
+def compose(clock, own, recv):
+    return to_chips(small(clock, compose_kernel, [(2, QUARTER, D)] * 4, (own, recv), [(2, HALF, D)]))
+
+
+def prefix(clock, got):
+    return to_chips(small(clock, prefix_kernel, [(QUARTER, D)] * 4, got, PAIR_WORK))
+
+
+def previous(clock, back, own, recv):
     mine, other = small(
-        previous_kernel, [(HALF, D)] * 2, back + (own, recv), [(HALF, D)], flags
-    )
-    return mine, swapped(other, "seq", 1), (own, recv, got)
-
-
-def scan_grads(flags, own, give, kept):
-    own_pair, recv_pair, kept_chips = kept
-    recv = swapped(give, "seq", 1)
-    quarters = small(
-        compose_back_kernel,
-        [(QUARTER, D)] * 4,
-        (own, recv, own_pair, recv_pair),
-        [(HALF, D)],
-        flags,
-    )
-    got = to_chips(quarters)
-    enter = small(
-        suffix_kernel,
-        [(QUARTER, D)] * 4,
-        got + kept_chips,
-        [(4, 2, QUARTER, D), (4, QUARTER, D)],
-        flags,
-    )
-    back = to_chips(enter)
-    mine, other = small(
-        following_kernel,
-        [(HALF, D)] * 2,
-        back + (own, recv, own_pair, recv_pair),
-        [(HALF, D)],
-        flags,
-    )
+        clock, previous_kernel, [(HALF, D)] * 2, back + (own, recv), [(HALF, D)]
+    )
+    return mine, swapped(other, "seq", 1)
+
+
+def compose_back(clock, *args):
+    return to_chips(small(clock, compose_back_kernel, [(QUARTER, D)] * 4, args, [(HALF, D)]))
+
+
+def suffix(clock, got, kept):
+    return to_chips(small(clock, suffix_kernel, [(QUARTER, D)] * 4, got + kept, PAIR_WORK))
+
+
+def following(clock, back, *args):
+    mine, other = small(clock, following_kernel, [(HALF, D)] * 2, back + args, [(HALF, D)])
     return mine, swapped(other, "seq", 1)
 
 
@@ -377,10 +405,10 @@
     pair[1] = product(rows, wv[...]).astype(BF)
 
 
-def state_pair(flags, mine, other, initial, forget, update, wk, wv):
+def state_pair(clock, mine, other, initial, forget, update, wk, wv):
     step = 256
     column = pl.BlockSpec((D, step), lambda j, *_: (0, j))
-    return run(
+    return clock.run(
         state_kernel,
         (shape((NS, D), F32), shape((NS, D), BF), shape((NS, D), F32), shape((2, NS, D), BF)),
         (mine, other, initial, forget, update, wk, wv),
@@ -393,7 +421,6 @@
             pl.BlockSpec((2, NS, step), lambda j, *_: (0, 0, j)),
         ),
         flops=4 * NS * D * D,
-        flags=flags,
     )
 
 
@@ -423,10 +450,10 @@
     lse[0] = peak + jnp.log2(total)
 
 
-def attend(flags, queries, left, own, state):
+def attend(clock, queries, left, own, state):
     head = pl.BlockSpec((W, HEAD_DIM), lambda h, *_: (0, h))
     pair = pl.BlockSpec((2, W, HEAD_DIM), lambda h, *_: (0, 0, h))
-    return run(
+    return clock.run(
         attend_kernel,
         (shape((W, D), BF), shape((HEADS, 1, W), F32)),
         (queries, left, own, state),
@@ -434,7 +461,7 @@
         [head, pair, pair, pair],
         (head, pl.BlockSpec((1, 1, W), lambda h, *_: (h, 0, 0))),
         flops=4 * W * (2 * W + NS) * D,
-        flags=flags,
+        stream=True,
     )
 
 
@@ -461,10 +488,10 @@
     queries_grad[...] = (total * SCALE).T.astype(BF)
 
 
-def attend_back(flags, queries, left, own, state, grad, lse):
+def attend_back(clock, queries, left, own, state, grad, lse):
     head = pl.BlockSpec((W, HEAD_DIM), lambda h, *_: (0, h))
     pair = pl.BlockSpec((2, W, HEAD_DIM), lambda h, *_: (0, 0, h))
-    return run(
+    return clock.run(
         attend_back_kernel,
         (shape((W, D), BF), shape((2, W, D), BF), shape((2, W, D), F32), shape((2, NS, D), BF)),
         (queries, left, own, state, grad, lse),
@@ -472,8 +499,7 @@
         [head, pair, pair, pair, head, pl.BlockSpec((1, 1, W), lambda h, *_: (h, 0, 0))],
         (head, pair, pair, pair),
         flops=10 * W * (2 * W + NS) * D,
-        limit=48,
-        flags=flags,
+        stream=True,
     )
 
 
@@ -488,29 +514,40 @@
     return value, slope
 
 
-def mlp_kernel(
+def mlp_step(normed_mlp, cotangent, up1, up2, down, up, activated, upper_grad, total, grad):
+    half = up1.shape[1]
+    up[:, :half] = up1[...]
+    up[:, half:] = up2[...]
+    rows = down[...].reshape(2 * half, D)
+    value, slope = gelu_parts(product(normed_mlp[...], up[...]))
+    value = value.astype(BF)
+    activated[...] = value
+    total[...] += product(value, rows)
+    back = product_nt(cotangent[...], rows).astype(BF).astype(F32)
+    back = (back * slope).astype(BF)
+    upper_grad[...] = back
+    grad[...] += product_nt(back, up[...])
+
+
+def mlp_first_kernel(
+    flags,
     attended,
     tokens,
     out_weight,
     gain,
     cotangent,
-    up,
+    up1,
+    up2,
     down,
-    mixed,
     activated,
     upper_grad,
     normed_mlp,
-    hidden_grad,
-    attended_grad,
-    heads_grad,
-    gain_grad,
     hidden,
     total,
     grad,
+    up,
 ):
-    step = pl.program_id(0)
-
-    @pl.when(step == 0)
+    @pl.when(pl.program_id(0) == 0)
     def _():
         field = tokens[...].astype(F32) + product(attended[...], out_weight[...])
         hidden[...] = field
@@ -518,14 +555,40 @@
         total[...] = field
         grad[...] = jnp.zeros_like(field)
 
-    value, slope = gelu_parts(product(normed_mlp[...], up[...]))
-    value = value.astype(BF)
-    activated[...] = value
-    total[...] += product(value, down[...])
-    back = product_nt(cotangent[...], down[...]).astype(BF).astype(F32)
-    back = (back * slope).astype(BF)
-    upper_grad[...] = back
-    grad[...] += product_nt(back, up[...])
+    mlp_step(normed_mlp, cotangent, up1, up2, down, up, activated, upper_grad, total, grad)
+
+
+def mlp_second_kernel(
+    flags,
+    normed_mlp,
+    hidden,
+    total_in,
+    grad_in,
+    out_weight,
+    gain,
+    cotangent,
+    up1,
+    up2,
+    down,
+    activated,
+    upper_grad,
+    mixed,
+    hidden_grad,
+    attended_grad,
+    heads_grad,
+    gain_grad,
+    total,
+    grad,
+    up,
+):
+    step = pl.program_id(0)
+
+    @pl.when(step == 0)
+    def _():
+        total[...] = total_in[...]
+        grad[...] = grad_in[...]
+
+    mlp_step(normed_mlp, cotangent, up1, up2, down, up, activated, upper_grad, total, grad)
 
     @pl.when(step == pl.num_programs(0) - 1)
     def _():
@@ -546,45 +609,66 @@
         heads_grad[...] = product_nt(low, out_weight[...]).astype(BF)
 
 
-def mlp(attended, tokens, out_weight, gain, cotangent, up, down):
-    step = 512
+PIECE = 256
+PAIRS = FF // (4 * PIECE)
+
+
+def mlp_specs(part):
+    return [
+        pl.BlockSpec((D, PIECE), lambda j, *_: (0, 4 * j + part)),
+        pl.BlockSpec((D, PIECE), lambda j, *_: (0, 4 * j + 2 + part)),
+        pl.BlockSpec((2, PIECE, D), lambda j, *_: (j, part, 0)),
+    ]
+
+
+def mlp_halves():
+    return pl.BlockSpec((W, 2 * PIECE), lambda j, *_: (0, j))
+
+
+def mlp_first(clock, attended, tokens, out_weight, gain, cotangent, up, down):
     rows = whole((W, D))
-    return run(
-        mlp_kernel,
+    return clock.run(
+        mlp_first_kernel,
         (
+            shape((W, FF // 2), BF),
+            shape((W, FF // 2), BF),
             shape((W, D), BF),
-            shape((W, FF), BF),
-            shape((W, FF), BF),
+            shape((W, D), F32),
+            shape((W, D), F32),
+            shape((W, D), F32),
+        ),
+        (attended, tokens, out_weight, gain, cotangent, up, up, down),
+        (PAIRS,),
+        [fixed((W, D)), fixed((W, D)), fixed((D, D)), fixed((1, D)), fixed((W, D))] + mlp_specs(0),
+        (mlp_halves(), mlp_halves(), rows, rows, rows, rows),
+        [pltpu.VMEM((D, 2 * PIECE), BF)],
+        flops=4 * W * D * FF + 2 * W * D * D,
+        limit=36,
+    )
+
+
+def mlp_second(clock, normed_mlp, hidden, total, grad, out_weight, gain, cotangent, up, down):
+    rows = whole((W, D))
+    return clock.run(
+        mlp_second_kernel,
+        (
+            shape((W, FF // 2), BF),
+            shape((W, FF // 2), BF),
             shape((W, D), BF),
             shape((W, D), F32),
             shape((W, D), BF),
             shape((W, D), BF),
             shape((1, D), F32),
         ),
-        (attended, tokens, out_weight, gain, cotangent, up, down),
-        (FF // step,),
-        [
-            fixed((W, D)),
-            fixed((W, D)),
-            fixed((D, D)),
-            fixed((1, D)),
-            fixed((W, D)),
-            pl.BlockSpec((D, step), lambda j: (0, j)),
-            pl.BlockSpec((step, D), lambda j: (j, 0)),
-        ],
-        (
-            rows,
-            pl.BlockSpec((W, step), lambda j: (0, j)),
-            pl.BlockSpec((W, step), lambda j: (0, j)),
-            rows,
-            rows,
-            rows,
-            rows,
-            whole((1, D)),
-        ),
-        [pltpu.VMEM((W, D), F32)] * 3,
-        flops=8 * W * D * FF + 4 * W * D * D,
-        limit=48,
+        (normed_mlp, hidden, total, grad, out_weight, gain, cotangent, up, up, down),
+        (PAIRS,),
+        [fixed((W, D))] * 4
+        + [fixed((D, D)), fixed((1, D)), fixed((W, D))]
+        + mlp_specs(1),
+        (mlp_halves(), mlp_halves(), rows, rows, rows, rows, whole((1, D))),
+        [pltpu.VMEM((W, D), F32), pltpu.VMEM((W, D), F32), pltpu.VMEM((D, 2 * PIECE), BF)],
+        flops=4 * W * D * FF + 2 * W * D * D,
+        limit=36,
     )
 
 
@@ -597,12 +681,12 @@
     give[...] = work[pl.ds(pl.multiple_of((1 - flags[CORE]) * HALF, HALF), HALF)].astype(BF)
 
 
-def direct_grad(flags, state_grad, wk, wv, forget, cotangent):
+def direct_grad(clock, state_grad, wk, wv, forget, cotangent):
     step = 256
     row = pl.BlockSpec((step, D), lambda j, *_: (j, 0))
     column = pl.BlockSpec((NS, step), lambda j, *_: (0, j))
     half = pl.BlockSpec((HALF, step), lambda j, *_: (0, j))
-    return run(
+    return clock.run(
         direct_kernel,
         (shape((NS, D), F32), shape((HALF, D), BF), shape((HALF, D), BF)),
         (state_grad, wk, wv, forget, cotangent),
@@ -611,7 +695,6 @@
         (column, half, half),
         [pltpu.VMEM((NS, step), F32)],
         flops=4 * NS * D * D,
-        flags=flags,
     )
 
 
@@ -662,11 +745,11 @@
         summary_grad[...] = total[...].astype(BF)
 
 
-def state_back(flags, mine, other, cotangent, forget, update, state_in, direct, state_weight):
+def state_back(clock, mine, other, cotangent, forget, update, state_in, direct, state_weight):
     step = 256
     column = pl.BlockSpec((NS, step), lambda j, *_: (0, j))
     half = pl.BlockSpec((HALF, step), lambda j, *_: (0, j))
-    return run(
+    return clock.run(
         state_back_kernel,
         (
             shape((NS, D), BF),
@@ -689,11 +772,10 @@
         ),
         [pltpu.VMEM((NS, step), F32), pltpu.VMEM((NS, D), F32)],
         flops=4 * NS * D * D,
-        flags=flags,
-    )
-
-
-def summary_back_kernel(asks, pair, grad, own_grad, returned, asks_grad, pair_total):
+    )
+
+
+def summary_back_kernel(flags, asks, pair, grad, own_grad, asks_grad, pair_total):
     queries, out_grad = asks[...], grad[...]
     expos, total = summary_probs_of(pair[0], queries)
     probs = expos * (1.0 / total)
@@ -701,30 +783,39 @@
     rowdot = jnp.sum(probs * prob_grad, axis=0, keepdims=True)
     score_grad = (probs * (prob_grad - rowdot)).astype(BF)
     asks_grad[...] = (product_tn(pair[0], score_grad) * SCALE).T.astype(BF)
-    pair_total[0] = (
-        own_grad[0] + returned[0].astype(F32) + product(score_grad, queries) * SCALE
-    ).astype(BF)
-    pair_total[1] = (
-        own_grad[1] + returned[1].astype(F32) + product(probs.astype(BF), out_grad)
-    ).astype(BF)
-
-
-def summary_back(asks, pair, grad, own_grad, returned):
-    head = pl.BlockSpec((W, HEAD_DIM), lambda h: (0, h))
-    both = pl.BlockSpec((2, W, HEAD_DIM), lambda h: (0, 0, h))
-    return run(
+    pair_total[0] = (own_grad[0] + product(score_grad, queries) * SCALE).astype(BF)
+    pair_total[1] = (own_grad[1] + product(probs.astype(BF), out_grad)).astype(BF)
+
+
+def summary_back(clock, asks, pair, grad, own_grad):
+    head = pl.BlockSpec((W, HEAD_DIM), lambda h, *_: (0, h))
+    both = pl.BlockSpec((2, W, HEAD_DIM), lambda h, *_: (0, 0, h))
+    return clock.run(
         summary_back_kernel,
         (shape((NS, D), BF), shape((2, W, D), BF)),
-        (asks, pair, grad, own_grad, returned),
+        (asks, pair, grad, own_grad),
         (HEADS,),
-        [head, both, head, both, both],
+        [head, both, head, both],
         (head, both),
         flops=10 * NS * W * D,
+        stream=True,
     )
 
 
 def tokens_back_kernel(
-    queries_grad, pair_total, wq, wk, wv, tokens, gain, hidden_grad, tokens_grad, gain_grad, total
+    flags,
+    queries_grad,
+    pair_total,
+    returned,
+    wq,
+    wk,
+    wv,
+    tokens,
+    gain,
+    hidden_grad,
+    tokens_grad,
+    gain_grad,
+    total,
 ):
     step = pl.program_id(0)
 
@@ -735,11 +826,11 @@
 
     @pl.when((step >= 2) & (step < 4))
     def _():
-        total[...] += product_nt(pair_total[0], wk[...])
+        total[...] += product_nt(add_low(pair_total[0], returned[0]), wk[...])
 
     @pl.when(step >= 4)
     def _():
-        total[...] += product_nt(pair_total[0], wv[...])
+        total[...] += product_nt(add_low(pair_total[0], returned[0]), wv[...])
 
     @pl.when(step == 5)
     def _():
@@ -756,25 +847,27 @@
         )
 
 
-def tokens_back(queries_grad, pair_total, wq, wk, wv, tokens, gain, hidden_grad):
+def tokens_back(clock, queries_grad, pair_total, returned, wq, wk, wv, tokens, gain, hidden_grad):
     step = D // 2
     clamp = lambda i, low: jnp.clip(i - low, 0, 1)
-    weight = lambda low: pl.BlockSpec((D, step), lambda i: (0, clamp(i, low)))
+    weight = lambda low: pl.BlockSpec((D, step), lambda i, *_: (0, clamp(i, low)))
     later = lambda i: jnp.maximum(i - 2, 0)
-    return run(
+    pair = pl.BlockSpec((1, W, step), lambda i, *_: (later(i) // 2, 0, later(i) % 2))
+    return clock.run(
         tokens_back_kernel,
         (shape((W, D), F32), shape((1, D), F32)),
-        (queries_grad, pair_total, wq, wk, wv, tokens, gain, hidden_grad),
+        (queries_grad, pair_total, returned, wq, wk, wv, tokens, gain, hidden_grad),
         (6,),
         [
-            pl.BlockSpec((W, step), lambda i: (0, clamp(i, 0))),
-            pl.BlockSpec((1, W, step), lambda i: (later(i) // 2, 0, later(i) % 2)),
+            pl.BlockSpec((W, step), lambda i, *_: (0, clamp(i, 0))),
+            pair,
+            pair,
             weight(0),
             weight(2),
             weight(4),
-            whole((W, D)),
-            whole((1, D)),
-            whole((W, D)),
+            fixed((W, D)),
+            fixed((1, D)),
+            fixed((W, D)),
         ],
         (whole((W, D)), whole((1, D))),
         [pltpu.VMEM((W, D), F32)],
@@ -782,33 +875,6 @@
     )
 
 
-def weight_kernel(chunk_of, rows, pairs, merge, flags, *refs):
-    lefts, rights = refs[: 2 * pairs : 2], refs[1 : 2 * pairs : 2]
-    recv = refs[2 * pairs] if merge else None
-    outs, work = refs[2 * pairs + merge : -1], refs[-1]
-
-    @pl.when(pl.program_id(0) == 0)
-    def _():
-        for pair, left in enumerate(lefts):
-            for place in range(4):
-                chunk = 2 * chunk_of(flags, place) + (
-                    flags[CORE] if merge else 1 - flags[CORE]
-                )
-                block = left[:, pl.ds(pl.multiple_of(chunk * rows, rows), rows)]
-                work[pair, place * rows : (place + 1) * rows] = block.T
-
-    total = product(work[0], rights[0][0])
-    for pair in range(1, pairs):
-        total = total + product(work[pair], rights[pair][0])
-    for place in range(4):
-        part = total[place * rows : (place + 1) * rows]
-        if merge:
-            part = part + recv[chunk_of(flags, place)].astype(F32)
-            outs[place // 2][place % 2] = part.astype(BF)
-        else:
-            outs[0][place] = part.astype(BF)
-
-
 def chunk_natural(flags, place):
     return place
 
@@ -823,40 +889,119 @@
     return 2 * (1 - y if place < 2 else y) + place % 2
 
 
-def weight_part(flags, chunk_of, pairs, recv):
-    left, right = pairs[0]
-    rows = left.shape[1] // 8
-    blocks, tokens, width = right.shape
-    columns = blocks * width
-    step = 512
-    per = width // step
-    specs, args = [], []
-    for one, two in pairs:
-        specs += [
-            fixed(one.shape),
-            pl.BlockSpec((1, tokens, step), lambda j, *_: (j // per, 0, j % per)),
-        ]
-        args += [one, two]
+def column_blocks(terms):
+    return terms[0][1][0][0].shape[2] // D
+
+
+def weight_kernel(plan, merge, flags, *refs):
+    refs = list(refs)
+    lefts = [refs.pop(0) for _ in range(plan["lefts"])]
+    rights = [[refs.pop(0) for _ in adds] for adds in plan["rights"]]
+    recv = refs.pop(0) if merge else None
+    work = refs.pop()
+    step, base, start = pl.program_id(0), 0, 0
+    for rows, blocks, terms, along in plan["grads"]:
+        chunk_of = (chunk_along_x, chunk_along_y)[along] if merge else chunk_natural
+
+        @pl.when(step == base)
+        def _():
+            for term, (left, _) in enumerate(terms):
+                for place in range(4):
+                    chunk = 2 * chunk_of(flags, place) + (
+                        flags[CORE] if merge else 1 - flags[CORE]
+                    )
+                    block = lefts[left][:, pl.ds(pl.multiple_of(chunk * rows, rows), rows)]
+                    work[term, place * rows : (place + 1) * rows] = block.T
+
+        for block in range(blocks):
+
+            @pl.when(step == base + block)
+            def _():
+                total = 0.0
+                for term, (_, right) in enumerate(terms):
+                    parts = [part[0] for part in rights[right]]
+                    value = parts[0] if len(parts) == 1 else add_low(*parts)
+                    total = total + product(work[term, : 4 * rows], value)
+                at = start + block * rows
+                for place in range(4):
+                    part = total[place * rows : (place + 1) * rows]
+                    if merge:
+                        part = part + recv[chunk_of(flags, place), at : at + rows].astype(F32)
+                        refs[2 * along + place // 2][place % 2] = part.astype(BF)
+                    else:
+                        refs[0][place, at : at + rows] = part.astype(BF)
+
+        base += blocks
+        start += blocks * rows
+
+
+def weight_pair(clock, grads, recv):
+    lefts, left_ids, rights, args, specs, plans = [], {}, [], [], [], []
+    base, start, tokens = 0, 0, grads[0][0][0][0].shape[0]
+    sizes = []
+    for along, group in enumerate(grads):
+        first, total = base, 0
+        for terms in group:
+            rows, blocks = terms[0][0].shape[1] // 8, column_blocks(terms)
+            plan = []
+            for left, adds in terms:
+                if id(left) not in left_ids:
+                    left_ids[id(left)] = len(lefts)
+                    lefts.append(left)
+                plan.append((left_ids[id(left)], len(rights)))
+                rights.append(tuple(index for _, index in adds))
+                for right, index in adds:
+                    args.append(right)
+                    specs.append(
+                        pl.BlockSpec(
+                            (1, tokens, D),
+                            lambda j, *_, index=index, base=base, blocks=blocks: (
+                                index,
+                                0,
+                                jnp.clip(j - base, 0, blocks - 1),
+                            ),
+                        )
+                    )
+            plans.append((rows, blocks, plan, along))
+            base += blocks
+            total += blocks
+            start += blocks * rows
+        sizes.append((rows, total, first))
+    args = lefts + args
+    specs = [fixed(left.shape) for left in lefts] + specs
     merge = recv is not None
     if merge:
-        specs.append(pl.BlockSpec((4, rows, step), lambda j, *_: (0, 0, j)))
         args.append(recv)
-        outs = (shape((2, rows, columns), BF),) * 2
-        out_specs = (pl.BlockSpec((2, rows, step), lambda j, *_: (0, 0, j)),) * 2
+        specs.append(fixed(recv.shape))
+        outs, out_specs = [], []
+        for rows, blocks, first in sizes:
+            outs += [shape((2, rows * blocks, D), BF)] * 2
+            out_specs += [
+                pl.BlockSpec(
+                    (2, rows, D),
+                    lambda j, *_, first=first, blocks=blocks: (
+                        0,
+                        jnp.clip(j - first, 0, blocks - 1),
+                        0,
+                    ),
+                )
+            ] * 2
     else:
-        outs = (shape((4, rows, columns), BF),)
-        out_specs = (pl.BlockSpec((4, rows, step), lambda j, *_: (0, 0, j)),)
-    return run(
-        functools.partial(weight_kernel, chunk_of, rows, len(pairs), int(merge)),
-        outs,
+        outs = [shape((4, start, D), BF)]
+        out_specs = [whole((4, start, D))]
+    most = max(rows for rows, _, _ in sizes)
+    return clock.run(
+        functools.partial(
+            weight_kernel, {"lefts": len(lefts), "rights": rights, "grads": plans}, merge
+        ),
+        tuple(outs),
         tuple(args),
-        (columns // step,),
+        (base,),
         specs,
-        out_specs,
-        [pltpu.VMEM((len(pairs), 4 * rows, tokens), BF)],
-        flops=len(pairs) * tokens * left.shape[1] * columns,
-        flags=flags,
-        limit=40,
+        tuple(out_specs),
+        [pltpu.VMEM((len(grads[0][0]), 4 * most, tokens), BF)],
+        flops=2 * tokens * 4 * start * D * len(grads[0][0]),
+        limit=30,
     )
 
 
@@ -881,40 +1026,156 @@
     return scatter_bits(value, bits, names)
 
 
-def weight_scatter(flags, pairs, along_x):
-    count = lax.axis_size("seq")
-    rows = pairs[0][0].shape[1] // count
-    if count != 8:
-        total = sum(
-            product_tn(left, right.transpose(1, 0, 2).reshape(left.shape[0], -1))
-            for left, right in pairs
+def in_rows(value):
+    return jnp.concatenate([value[:, at : at + D] for at in range(0, value.shape[1], D)], axis=0)
+
+
+def turn_kernel(flags, kept1, recv1, kept2, recv2, send1, send2):
+    send1[...] = add_low(kept1[0], recv1[0])
+    send2[...] = add_low(kept2[0], recv2[0])
+
+
+def pack_kernel(flags, *refs):
+    out, start = refs[-1], 0
+    for at in range(0, len(refs) - 1, 3):
+        kept, recv, last = refs[at : at + 3]
+        rows = last.shape[0]
+        out[start : start + rows] = add_low(kept[0], recv[0], last[...])
+        start += rows
+
+
+class Scatter:
+    def __init__(self, clock, firsts, seconds):
+        self.grads, self.plain = (firsts, seconds), None
+        if lax.axis_size("seq") != 8:
+            sums = []
+            for number, group in enumerate(self.grads):
+                for terms in group:
+                    total = 0.0
+                    for left, adds in terms:
+                        parts = [right[index] for right, index in adds]
+                        right = add_low(*parts) if len(parts) > 1 else parts[0]
+                        total = total + product_tn(left, right)
+                    sums.append(in_rows(whole_scatter(total.astype(BF), number == 0)))
+            self.plain = jnp.concatenate(sums, axis=0)
+            return
+        (self.give,) = weight_pair(clock, self.grads, None)
+
+    def core(self, clock):
+        if self.plain is None:
+            self.recv = swapped(clock.at(self.give), "seq", 1)
+
+    def keep(self, clock):
+        if self.plain is None:
+            send1, kept1, send2, kept2 = weight_pair(clock, self.grads, self.recv)
+            self.kept, self.send = (kept1, kept2), (send1, send2)
+
+    def near(self, clock):
+        if self.plain is None:
+            self.recv = tuple(
+                swapped(clock.at(send), "seq", far) for send, far in zip(self.send, (2, 4))
+            )
+
+    def held(self, other):
+        args, specs = [], []
+        for number, (kept, recv) in enumerate(zip(self.kept, self.recv)):
+            bit = 1 - number
+            mine = lambda i, flags, bit=bit: (((flags[CHIP] >> bit) & 1) ^ other, 0, 0)
+            args.append([kept, recv])
+            specs.append([pl.BlockSpec((1,) + kept.shape[1:], mine)] * 2)
+        return args, specs
+
+    def turn(self, clock, flops=0):
+        if self.plain is None:
+            args, specs = self.held(1)
+            dims = [kept.shape[1:] for kept in self.kept]
+            self.send = clock.run(
+                turn_kernel,
+                tuple(shape(d, BF) for d in dims),
+                tuple(args[0] + args[1]),
+                (1,),
+                specs[0] + specs[1],
+                tuple(whole(d) for d in dims),
+                flops=flops,
+                limit=10,
+            )
+
+    def far(self, clock):
+        if self.plain is None:
+            self.last = tuple(
+                swapped(clock.at(send), "seq", far) for send, far in zip(self.send, (4, 2))
+            )
+
+    def parts(self):
+        args, specs = self.held(0)
+        for number, last in enumerate(self.last):
+            args[number].append(last)
+            specs[number].append(whole(last.shape))
+        return args[0] + args[1], specs[0] + specs[1]
+
+
+def pack(clock, *scatters):
+    if scatters[0].plain is not None:
+        return jnp.concatenate([scatter.plain for scatter in scatters], axis=0)
+    args, specs = [], []
+    for scatter in scatters:
+        more = scatter.parts()
+        args += more[0]
+        specs += more[1]
+    total = sum(arg.shape[0] for arg in args[2::3])
+    return clock.run(
+        pack_kernel,
+        (shape((total, D), BF),),
+        tuple(args),
+        (1,),
+        specs,
+        (whole((total, D)),),
+        limit=16,
+    )[0]
+
+
+class Line:
+    def __init__(self, clock, value):
+        count = lax.axis_size("dp")
+        half = count // 2
+        self.value = value
+        self.rounds = (
+            [([(s, s + 1), (count - 1 - s, count - 2 - s)], None) for s in range(half - 1)]
+            + [([(half - 1, half), (half, half - 1)], None)]
+            + [
+                ([(s + 1, s), (count - 2 - s, count - 1 - s)], (s, count - 1 - s))
+                for s in range(half - 2, -1, -1)
+            ]
         )
-        return whole_scatter(total.astype(BF), along_x)
-    (give,) = weight_part(flags, chunk_natural, pairs, None)
-    recv = swapped(give, "seq", 1)
-    send, keep = weight_part(flags, chunk_along_x if along_x else chunk_along_y, pairs, recv)
-    near, far = (2, 4) if along_x else (4, 2)
-    recv = swapped(send, "seq", near)
-    mine = (flags[CHIP] >> 1) & 1 if along_x else flags[CHIP] & 1
-    send = add_low(pick(keep, 1 - mine, 0), pick(recv, 1 - mine, 0))
-    last = swapped(send, "seq", far)
-    return add_low(pick(keep, mine, 0), pick(recv, mine, 0), last)
-
-
-def sum_over_dp(value):
-    count, place = lax.axis_size("dp"), lax.axis_index("dp")
-    half = count // 2
-    for step in range(half - 1):
-        value = add_low(
-            value,
-            lax.ppermute(value, "dp", [(step, step + 1), (count - 1 - step, count - 2 - step)]),
-        )
-    value = add_low(value, lax.ppermute(value, "dp", [(half - 1, half), (half, half - 1)]))
-    for step in range(half - 2, -1, -1):
-        recv = lax.ppermute(value, "dp", [(step + 1, step), (count - 2 - step, count - 1 - step)])
-        outer = (place == step) | (place == count - 1 - step)
-        value = jnp.where(outer, recv, value)
-    return value.astype(F32)
+        self.send(clock)
+
+    def send(self, clock):
+        self.recv = lax.ppermute(clock.at(self.value), "dp", self.rounds[0][0])
+
+    def step(self, clock):
+        place = lax.axis_index("dp")
+        takers = self.rounds.pop(0)[1]
+        value = clock.at(self.value)
+        if takers is None:
+            self.value = add_low(value, self.recv)
+        else:
+            outer = (place == takers[0]) | (place == takers[1])
+            self.value = jnp.where(outer, self.recv, value)
+        if self.rounds:
+            clock.after(self.value)
+            self.send(clock)
+
+    def finish(self, clock):
+        while self.rounds:
+            self.step(clock)
+        return self.value.astype(F32)
+
+
+def interleaved(first, second):
+    blocks = []
+    for at in range(0, first.shape[1], PIECE):
+        blocks += [first[:, at : at + PIECE], second[:, at : at + PIECE]]
+    return jnp.concatenate(blocks, axis=1)
 
 
 def body(
@@ -937,55 +1198,122 @@
 ):
     count = lax.axis_size("seq")
     place = lax.axis_index("seq")
-    flags = jnp.stack([item_starts[0, 0], place & 1, (place >> 1) & 3]).astype(jnp.int32)
+    clock = Clock(
+        jnp.stack([item_starts[0, 0], place & 1, (place >> 1) & 3]).astype(jnp.int32)
+    )
     tokens, cotangent, state_cot = tokens[0], out_cotangent[0], state_cotangent[0, 0]
     attn_gain, gate_bias, mlp_gain = attn_gain[None], gate_bias[None], mlp_gain[None]
-
-    normed, queries, own = front(tokens, attn_gain, query_weight, key_weight, value_weight)
-    left = shifted(own, "seq", 1)
-    summary, forget, update, give_scan, own_scan = gates(
-        flags, state_queries, own, state_weight, gate_bias, initial_state
-    )
-    mine, other, kept = scan_states(flags, own_scan, give_scan)
+    down_weight = down_weight.reshape(FF // (2 * PIECE), 2 * PIECE, D)
+
+    tokens_left = shifted(tokens, "seq", 1)
+    normed, queries, own = front(clock, tokens, attn_gain, query_weight, key_weight, value_weight)
+    summary, forget, update, give_pair, own_pair = gates(
+        clock, state_queries, own, state_weight, gate_bias, initial_state
+    )
+    recv_pair = swapped(give_pair, "seq", 1)
+    left = left_pair(clock, tokens_left, attn_gain, key_weight, value_weight)
+    kept_chips = compose(clock, own_pair, recv_pair)
+    back = prefix(clock, kept_chips)
+    mine, other = previous(clock, back, own_pair, recv_pair)
     state_in, state_low, state_out, state = state_pair(
-        flags, mine, other, initial_state, forget, update, key_weight, value_weight
-    )
-    attended, lse = attend(flags, queries, left, own, state)
-    (
-        mixed,
-        activated,
-        upper_grad,
-        normed_mlp,
-        hidden_grad,
-        attended_grad,
-        heads_grad,
-        mlp_gain_grad,
-    ) = mlp(attended, tokens, output_weight, mlp_gain, cotangent, up_weight, down_weight)
-
-    down_grad = weight_scatter(flags, [(activated, cotangent[None])], True)
-    up_grad = weight_scatter(flags, [(normed_mlp, upper_grad[None])], False)
-    output_grad = weight_scatter(flags, [(attended, attended_grad[None])], True)
-
+        clock, mine, other, initial_state, forget, update, key_weight, value_weight
+    )
+    attended, lse = attend(clock, queries, left, own, state)
+    split = count == 8
+    activated1, upper_grad1, normed_mlp, hidden, total, grad = mlp_first(
+        clock, attended, tokens, output_weight, mlp_gain, cotangent, up_weight, down_weight
+    )
+    out_grads = (cotangent[None], 0)
+    if split:
+        feed1 = Scatter(
+            clock,
+            [[(activated1, [out_grads])]],
+            [[(normed_mlp, [(upper_grad1[None], 0)])]],
+        )
+        feed1.core(clock)
+        feed1.keep(clock)
+        feed1.near(clock)
+    activated2, upper_grad2, mixed, hidden_grad, attended_grad, heads_grad, mlp_gain_grad = (
+        mlp_second(
+            clock,
+            normed_mlp,
+            hidden,
+            total,
+            grad,
+            output_weight,
+            mlp_gain,
+            cotangent,
+            up_weight,
+            down_weight,
+        )
+    )
+    if split:
+        feed2 = Scatter(
+            clock,
+            [[(activated2, [out_grads])]],
+            [[(normed_mlp, [(upper_grad2[None], 0)])]],
+        )
+        feed2.core(clock)
+        feed1.turn(clock, LONG)
+        feed1.far(clock)
+        feed2.keep(clock)
+        feed2.near(clock)
+    else:
+        feed1 = Scatter(
+            clock,
+            [[(interleaved(activated1, activated2), [out_grads])]],
+            [[(normed_mlp, [(interleaved(upper_grad1, upper_grad2)[None], 0)])]],
+        )
     queries_grad, left_grad, own_grad, state_grad = attend_back(
-        flags, queries, left, own, state, heads_grad, lse
-    )
-    query_grad = weight_scatter(flags, [(normed, queries_grad[None])], False)
-    returned = shifted(left_grad, "seq", -1)
-    direct, own_scan, give_scan = direct_grad(
-        flags, state_grad, key_weight, value_weight, forget, state_cot
-    )
-    mine, other = scan_grads(flags, own_scan, give_scan, kept)
+        clock, queries, left, own, state, heads_grad, lse
+    )
+    if split:
+        feed2.turn(clock)
+        feed2.far(clock)
+    direct, own_base, give_base = direct_grad(
+        clock, state_grad, key_weight, value_weight, forget, state_cot
+    )
+    recv_base = swapped(give_base, "seq", 1)
+    packed1 = pack(clock, feed1)
+    got = compose_back(clock, own_base, recv_base, own_pair, recv_pair)
+    packed2 = pack(clock, feed2) if split else None
+    line1 = Line(clock, packed1)
+    line2 = Line(clock, packed2) if split else None
+    back = suffix(clock, got, kept_chips)
+    mine, other = following(clock, back, own_base, recv_base, own_pair, recv_pair)
+    returned = shifted(clock.at(left_grad), "seq", -1)
     initial_grad, projected_grad, gate_bias_grad, summary_grad = state_back(
-        flags, mine, other, state_cot, forget, update, state_in, direct, state_weight
-    )
-    state_weight_grad = weight_scatter(flags, [(summary, projected_grad)], True)
+        clock, mine, other, state_cot, forget, update, state_in, direct, state_weight
+    )
+    line1.step(clock)
+    others = Scatter(
+        clock,
+        [[(attended, [(attended_grad[None], 0)])], [(summary, [(projected_grad, 0)])]],
+        [[(normed, [(queries_grad[None], 0)])], [(summary, [(projected_grad, 1)])]],
+    )
+    others.core(clock)
     state_queries_grad, pair_total = summary_back(
-        state_queries, own, summary_grad, own_grad, returned
-    )
-    pair_grad = weight_scatter(flags, [(normed, pair_total), (state_low, state_grad)], False)
+        clock, state_queries, own, summary_grad, own_grad
+    )
+    if split:
+        line2.step(clock)
+    others.keep(clock)
+    others.near(clock)
+    line1.step(clock)
+    keys_values = Scatter(
+        clock,
+        [[(normed, [(pair_total, 0), (returned, 0)]), (state_low, [(state_grad, 0)])]],
+        [[(normed, [(pair_total, 1), (returned, 1)]), (state_low, [(state_grad, 1)])]],
+    )
+    keys_values.core(clock)
+    if split:
+        line2.step(clock)
+    keys_values.keep(clock)
     tokens_grad, attn_gain_grad = tokens_back(
+        clock,
         queries_grad,
         pair_total,
+        returned,
         query_weight,
         key_weight,
         value_weight,
@@ -993,7 +1321,14 @@
         attn_gain,
         hidden_grad,
     )
-
+    line1 = line1.finish(clock)
+    clock.after(line1)
+    others.turn(clock)
+    others.far(clock)
+    keys_values.near(clock)
+    if split:
+        line2 = line2.finish(clock)
+        clock.after(line2)
     lanes, rows = D // count, NS // count
     vectors = jnp.concatenate([attn_gain_grad, gate_bias_grad, mlp_gain_grad])
     vectors = vectors.reshape(3, count, lanes).transpose(1, 0, 2).reshape(count, 1, 3 * lanes)
@@ -1007,14 +1342,40 @@
         axis=1,
     )
     rest = whole_scatter(rest.reshape(-1, D), True)
-
-    down_grad = sum_over_dp(down_grad)
-    up_grad = sum_over_dp(up_grad)
-    output_grad = sum_over_dp(output_grad)
-    query_grad = sum_over_dp(query_grad)
-    state_weight_grad = sum_over_dp(state_weight_grad)
-    pair_grad = sum_over_dp(pair_grad)
-    rest = sum_over_dp(rest)
+    line3 = Line(clock, pack(clock, others))
+    keys_values.turn(clock)
+    keys_values.far(clock)
+    line3.step(clock)
+    line4 = Line(clock, jnp.concatenate([pack(clock, keys_values), rest], axis=0))
+    line3.step(clock)
+    line4.step(clock)
+    line4.step(clock)
+
+    def unpack(packed, *dims):
+        pieces, start = [], 0
+        for high, wide in dims:
+            parts = [
+                packed[start + high * part : start + high * (part + 1)] for part in range(wide // D)
+            ]
+            start += high * (wide // D)
+            pieces.append(parts[0] if len(parts) == 1 else jnp.concatenate(parts, axis=1))
+        return pieces
+
+    high, deep = D // count, FF // count
+    if split:
+        down1, up1 = unpack(line1, (deep // 2, D), (high, FF // 2))
+        down2, up2 = unpack(line2, (deep // 2, D), (high, FF // 2))
+        down_grad = jnp.concatenate([down1, down2], axis=0)
+        up_grad = interleaved(up1, up2)
+    else:
+        down_grad, up_grad = unpack(line1, (deep, D), (high, FF))
+    output_grad, first_grad, query_grad, second_grad = unpack(
+        line3.finish(clock), (high, D), (high, D), (high, D), (high, D)
+    )
+    state_weight_grad = jnp.concatenate([first_grad, second_grad], axis=1)
+    key_grad, value_grad, rest = unpack(
+        line4.finish(clock), (high, D), (high, D), (2 * rows + 8, D)
+    )
     vectors = rest[2 * rows, : 3 * lanes]
     return (
         mixed[None],
@@ -1022,8 +1383,8 @@
         tokens_grad[None],
         vectors[:lanes],
         query_grad,
-        pair_grad[:, :D],
-        pair_grad[:, D:],
+        key_grad,
+        value_grad,
         output_grad,
         rest[:rows],
         state_weight_grad,

time: 593 us -> 457 us (0.77)
  waiting for transfers between devices: 252 us -> 150 us
  local copies, waits for them, and re-layouts: 42.3 us -> 25.5 us
  other arithmetic: 24.5 us -> 12.1 us
  Pallas kernels: 192 us -> 182 us
    ppermute x37 -> x39, waiting for transfers between devices: 159 us -> 61.8 us  [swapped(): lax.ppermute(value, axis, [(place, place ^ distance) for place in range(c...]
    unnamed x187 -> x186, local copies, waits for them, and re-layouts: 36.9 us -> 21.6 us
    convert_element_type x29 -> x11, other arithmetic: 17.4 us -> 7.38 us  [add_low(): return total.astype(BF)]
    pallas_call x28 -> x34, Pallas kernels: 192 us -> 182 us  [run(): pl.pallas_call(kernel, out_shape=outs, grid_spec=pltpu.PrefetchScalarGrid...]
    ppermute x21 -> x12, waiting for transfers between devices: 92.8 us -> 88 us  [send(): self.recv = lax.ppermute(clock.at(self.value), 'dp', self.rounds[0][0])]
    ppermute x21 -> x12, starting transfers between devices: 32.2 us -> 34.5 us  [send(): self.recv = lax.ppermute(clock.at(self.value), 'dp', self.rounds[0][0])]
    ppermute x37 -> x39, starting transfers between devices: 36.8 us -> 38.2 us  [swapped(): lax.ppermute(value, axis, [(place, place ^ distance) for place in range(c...]
  transfers between devices with their start and end apart: 60 -> 53, of which waited for: 28 -> 25; matrix products, arithmetic and copies ran while one was open for 5% -> 3% of each run, Pallas kernels for 18% -> 27%
where the time goes in v3:
time: 457 us; the launch traced here: 449 us
  Pallas kernels  182 us (40%)
  waiting for transfers between devices  150 us (33%)
  starting transfers between devices  76.4 us (17%)
  local copies, waits for them, and re-layouts  25.5 us (6%)
  other arithmetic  12.1 us (3%)
    pallas_call x34, Pallas kernels, run(): pl.pallas_call(kernel, out_shape=outs, grid_spec=pltpu.PrefetchScalarGrid...  182 us
    ppermute x12, waiting for transfers between devices, send(): self.recv = lax.ppermute(clock.at(self.value), 'dp', self.rounds[0][0])  88 us
    ppermute x39, waiting for transfers between devices, swapped(): lax.ppermute(value, axis, [(place, place ^ distance) for place in range(c...  61.8 us
    ppermute x39, starting transfers between devices, swapped(): lax.ppermute(value, axis, [(place, place ^ distance) for place in range(c...  38.2 us
    ppermute x12, starting transfers between devices, send(): self.recv = lax.ppermute(clock.at(self.value), 'dp', self.rounds[0][0])  34.5 us
    unnamed x186, local copies, waits for them, and re-layouts  21.6 us
  transfers between devices with their start and end apart: 53, of which 25 were waited for; matrix products, arithmetic and copies ran while one was open for 3% of the time, Pallas kernels for 27%

profile of v3, /device:TPU:0, one launch (start us, length us, event | category | flops | bytes accessed | tf_op | source)
XLA Modules:
  0.0 449.2 jit_solution(9650230252718399295)
XLA Ops:
  5.7 7.3 %shard_map.271 = (bf16[512,1024]{1,0:T(8,128)(2,1)S(1)}, bf16[512,1024]{1,0:T(8,128)(2,1)S(1)}, bf16[2,512,1024]{2,1,0:T(8,128)(2,1)S(1)}) custom-call(s32[3]{0:T(128)S(1)} %pad_add_fusion.flags, bf16[512,1024]{1,0:T(8,128)(2,1)S(1)} %bitcast.68, f32[1,1024]{1,0:T(1,128)S(1)} %bitcast.74, bf16[1024,1024]{1,0:T(8,128)(2,1)} %wq.3, bf16[1024,1024]{1,0:T(8,128)(2,1)} %wk.9, ...), custom_call_target="tpu_custom_call" | custom-call | flops 3221225472 | bytes 11538432 | tf_op jit(solution)/shard_map/pallas_call | solution.py:103
  14.1 10.9 %shard_map.272 = (bf16[512,1024]{1,0:T(8,128)(2,1)S(1)}, f32[512,1024]{1,0:T(8,128)S(1)}, f32[512,1024]{1,0:T(8,128)S(1)}, bf16[2,256,1024]{2,1,0:T(8,128)(2,1)S(1)}, bf16[2,256,1024]{2,1,0:T(8,128)(2,1)S(1)}) custom-call(s32[3]{0:T(128)S(1)} %pad_add_fusion.flags, bf16[512,1024]{1,0:T(8,128)(2,1)S(1)} %copy-done.40, ...), custom_call_target="tpu_custom_call" | custom-call | flops 3221225472 | bytes 20975616 | tf_op jit(solution)/shard_map/pallas_call | solution.py:103
  27.6 4.6 %shard_map.273.left = bf16[2,512,1024]{2,1,0:T(8,128)(2,1)S(1)} custom-call(s32[3]{0:T(128)S(1)} %pad_add_fusion.flags, bf16[512,1024]{1,0:T(8,128)(2,1)S(1)} %collective-permute-done.tokens, f32[1,1024]{1,0:T(1,128)S(1)} %bitcast.75, bf16[1024,1024]{1,0:T(8,128)(2,1)S(1)} %copy-done.6, bf16[1024,1024]{1,0:T(8,128)(2,1)S(1)} %copy-done.8), custom_call_target="tpu_custom_call" | custom-call | flops 99999997952 | bytes 7344128 | tf_op jit(solution)/shard_map/pallas_call | solution.py:103
  38.6 5.7 %collective-permute-done.2.from1.kept1 = bf16[2,64,1024]{2,1,0:T(8,128)(2,1)S(1)} collective-permute-done((bf16[2,64,1024]{2,1,0:T(8,128)(2,1)S(1)}, bf16[2,64,1024]{2,1,0:T(8,128)(2,1)S(1)}, u32[]{:S(2)}, u32[]{:S(2)}) %collective-permute-start.2) | collective-permute-done | bytes 262176 | tf_op jit(solution)/shard_map/ppermute | solution.py:35
  44.3 5.9 %collective-permute-done.3.from2.kept2 = bf16[2,64,1024]{2,1,0:T(8,128)(2,1)S(1)} collective-permute-done((bf16[2,64,1024]{2,1,0:T(8,128)(2,1)S(1)}, bf16[2,64,1024]{2,1,0:T(8,128)(2,1)S(1)}, u32[]{:S(2)}, u32[]{:S(2)}) %collective-permute-start.3) | collective-permute-done | bytes 262176 | tf_op jit(solution)/shard_map/ppermute | solution.py:35
  62.7 5.5 %shard_map.277 = (f32[512,1024]{1,0:T(8,128)S(1)}, bf16[512,1024]{1,0:T(8,128)(2,1)S(1)}, f32[512,1024]{1,0:T(8,128)}, bf16[2,512,1024]{2,1,0:T(8,128)(2,1)S(1)}) custom-call(s32[3]{0:T(128)S(1)} %pad_add_fusion.flags, bf16[256,1024]{1,0:T(8,128)(2,1)S(1)} %get-tuple-element.206.mine, bf16[256,1024]{1,0:T(8,128)(2,1)S(1)} %collective-permute-done.8.other, ...), custom_call_target="tpu_custom_call" | custom-call | flops 2147483648 | bytes 18874368 | tf_op jit(solution)/shard_map/pallas_call | solution.py:103
  69.5 15.0 %shard_map.278 = (bf16[512,1024]{1,0:T(8,128)(2,1)S(1)}, f32[8,1,512]{2,1,0:T(1,128)S(1)}) custom-call(s32[3]{0:T(128)S(1)} %pad_add_fusion.flags, bf16[512,1024]{1,0:T(8,128)(2,1)} %copy-done.77, bf16[2,512,1024]{2,1,0:T(8,128)(2,1)} %copy-done.76, bf16[2,512,1024]{2,1,0:T(8,128)(2,1)} %copy-done.37, bf16[2,512,1024]{2,1,0:T(8,128)(2,1)} %copy-done.65), custom_call_target="tpu_custom_call" | custom-call | flops 3221225472 | bytes 8404992 | tf_op jit(solution)/shard_map/pallas_call | solution.py:103
  85.2 15.3 %shard_map.279 = (bf16[512,2048]{1,0:T(8,128)(2,1)S(1)}, bf16[512,2048]{1,0:T(8,128)(2,1)S(1)}, bf16[512,1024]{1,0:T(8,128)(2,1)S(1)}, f32[512,1024]{1,0:T(8,128...) custom-call(s32[3]{0:T(128)S(1)} %pad_add_fusion.flags, ...), custom_call_target="tpu_custom_call" | custom-call | flops 9663676416 | bytes 41947136 | tf_op jit(solution)/shard_map/pallas_call | solution.py:103
  107.0 7.0 %collective-permute-done.9.refs_4_ = bf16[4,512,1024]{2,1,0:T(8,128)(2,1)S(1)} collective-permute-done((bf16[4,512,1024]{2,1,0:T(8,128)(2,1)S(1)}, bf16[4,512,1024]{2,1,0:T(8,128)(2,1)S(1)}, u32[]{:S(2)}, u32[]{:S(2)}) %collective-permute-start.9) | collective-permute-done | bytes 4194336 | tf_op jit(solution)/shard_map/ppermute | solution.py:35
  114.0 3.8 shard_map.281
  121.8 17.9 %shard_map.282 = (bf16[512,2048]{1,0:T(8,128)(2,1)S(1)}, bf16[512,2048]{1,0:T(8,128)(2,1)S(1)}, bf16[512,1024]{1,0:T(8,128)(2,1)}, f32[512,1024]{1,0:T(8,128)S(1...) custom-call(s32[3]{0:T(128)S(1)} %pad_add_fusion.flags, ...), custom_call_target="tpu_custom_call" | custom-call | flops 9663676416 | bytes 45096960 | tf_op jit(solution)/shard_map/pallas_call | solution.py:103
  147.7 3.8 collective-permute-done.12.refs_4_
  151.5 3.8 shard_map.285
  159.4 24.5 %shard_map.286 = (bf16[512,1024]{1,0:T(8,128)(2,1)S(1)}, bf16[2,512,1024]{2,1,0:T(8,128)(2,1)S(1)}, f32[2,512,1024]{2,1,0:T(8,128)S(1)}, bf16[2,512,1024]{2,1,0:T(8,128)(2,1)S(1)}) custom-call(s32[3]{0:T(128)S(1)} %pad_add_fusion.flags, bf16[512,1024]{1,0:T(8,128)(2,1)} %copy-done.77, bf16[2,512,1024]{2,1,0:T(8,128)(2,1)} %copy-done.76, ...), custom_call_target="tpu_custom_call" | custom-call | flops 8053063680 | bytes 17842176 | tf_op jit(solution)/shard_map/pallas_call | solution.py:103
  188.6 4.3 shard_map.288
  198.5 8.8 %collective-permute-done.19.refs_5_ = bf16[256,1024]{1,0:T(8,128)(2,1)S(1)} collective-permute-done((bf16[256,1024]{1,0:T(8,128)(2,1)S(1)}, bf16[256,1024]{1,0:T(8,128)(2,1)S(1)}, u32[]{:S(2)}, u32[]{:S(2)}) %collective-permute-start.19) | collective-permute-done | bytes 524320 | tf_op jit(solution)/shard_map/ppermute | solution.py:35
  233.6 6.6 %shard_map.294 = (bf16[512,1024]{1,0:T(8,128)(2,1)S(1)}, bf16[2,512,1024]{2,1,0:T(8,128)(2,1)S(1)}, f32[1,1024]{1,0:T(1,128)S(1)}, bf16[512,1024]{1,0:T(8,128)(2,1)S(1)}) custom-call(s32[3]{0:T(128)S(1)} %pad_add_fusion.flags, bf16[256,1024]{1,0:T(8,128)(2,1)S(1)} %get-tuple-element.278.mine, bf16[256,1024]{1,0:T(8,128)(2,1)S(1)} %collective-permute-done.26.other, ...), custom_call_target="tpu_custom_call" | custom-call | flops 2147483648 | bytes 24121344 | tf_op jit(solution)/shard_map/pallas_call | solution.py:103
  242.6 3.7 shard_map.295
  250.0 13.0 %shard_map.296 = (bf16[512,1024]{1,0:T(8,128)(2,1)S(1)}, bf16[2,512,1024]{2,1,0:T(8,128)(2,1)S(1)}) custom-call(s32[3]{0:T(128)S(1)} %pad_add_fusion.flags, bf16[512,1024]{1,0:T(8,128)(2,1)} %asks.3, bf16[2,512,1024]{2,1,0:T(8,128)(2,1)} %copy-done.37, bf16[512,1024]{1,0:T(8,128)(2,1)} %copy-done.68, f32[2,512,1024]{2,1,0:T(8,128)} %copy-done.75), custom_call_target="tpu_custom_call" | custom-call | flops 2684354560 | bytes 11534336 | tf_op jit(solution)/shard_map/pallas_call | solution.py:103
  263.0 9.3 %collective-permute-done.28 = bf16[512,1024]{1,0:T(8,128)(2,1)S(1)} collective-permute-done((bf16[512,1024]{1,0:T(8,128)(2,1)S(1)}, bf16[512,1024]{1,0:T(8,128)(2,1)S(1)}, u32[]{:S(2)}, u32[]{:S(2)}) %collective-permute-start.28) | collective-permute-done | bytes 1048608 | tf_op jit(solution)/shard_map/ppermute | solution.py:1153
  273.8 4.1 shard_map.297
  280.0 4.6 %shard_map.298 = bf16[4,256,1024]{2,1,0:T(8,128)(2,1)} custom-call(s32[3]{0:T(128)S(1)} %pad_add_fusion.flags, bf16[512,1024]{1,0:T(8,128)(2,1)S(1)} %get-tuple-element.188.refs_2_.refs_0_, bf16[512,1024]{1,0:T(8,128)(2,1)S(1)} %copy-done.22, bf16[2,512,1024]{2,1,0:T(8,128)(2,1)S(1)} %get-tuple-element.303.refs_2_.refs_5_.pair_total, ...), custom_call_target="tpu_custom_call" | custom-call | flops 2147483648 | bytes 16777216 | tf_op jit(solution)/shard_map/pallas_call | solution.py:103
  296.3 5.6 %shard_map.299 = (bf16[2,128,1024]{2,1,0:T(8,128)(2,1)S(1)}, bf16[2,128,1024]{2,1,0:T(8,128)(2,1)S(1)}, bf16[2,128,1024]{2,1,0:T(8,128)(2,1)S(1)}, bf16[2,128,1024]{2,1,0:T(8,128)(2,1)S(1)}) custom-call(s32[3]{0:T(128)S(1)} %pad_add_fusion.flags, bf16[512,1024]{1,0:T(8,128)(2,1)S(1)} %get-tuple-element.188.refs_2_.refs_0_, bf16[512,1024]{1,0:T(8,128)(2,1)S(1)} %copy-done.23, ...), custom_call_target="tpu_custom_call" | custom-call | flops 2147483648 | bytes 18874368 | tf_op jit(solution)/shard_map/pallas_call | solution.py:103
  302.0 8.7 %shard_map.300 = (f32[512,1024]{1,0:T(8,128)}, f32[1,1024]{1,0:T(1,128)S(1)}) custom-call(s32[3]{0:T(128)S(1)} %pad_add_fusion.flags, bf16[512,1024]{1,0:T(8,128)(2,1)S(1)} %copy-done.16, bf16[2,512,1024]{2,1,0:T(8,128)(2,1)S(1)} %copy-done.3, bf16[2,512,1024]{2,1,0:T(8,128)(2,1)S(1)} %collective-permute-done.31.refs_3_.refs_6_.returned, ...), custom_call_target="tpu_custom_call" | custom-call | flops 3221225472 | bytes 16785408 | tf_op jit(solution)/shard_map/pallas_call | solution.py:103
  310.7 4.9 %collective-permute-done.34 = bf16[512,1024]{1,0:T(8,128)(2,1)} collective-permute-done((bf16[512,1024]{1,0:T(8,128)(2,1)}, bf16[512,1024]{1,0:T(8,128)(2,1)}, u32[]{:S(2)}, u32[]{:S(2)}) %collective-permute-start.34) | collective-permute-done | bytes 1048608 | tf_op jit(solution)/shard_map/ppermute | solution.py:1153
  321.2 19.5 %collective-permute-done.37 = bf16[512,1024]{1,0:T(8,128)(2,1)S(1)} collective-permute-done((bf16[512,1024]{1,0:T(8,128)(2,1)S(1)}, bf16[512,1024]{1,0:T(8,128)(2,1)S(1)}, u32[]{:S(2)}, u32[]{:S(2)}) %collective-permute-start.37) | collective-permute-done | bytes 1048608 | tf_op jit(solution)/shard_map/ppermute | solution.py:1153
  344.9 12.5 %collective-permute-start.42 = (bf16[512,1024]{1,0:T(8,128)(2,1)S(1)}, bf16[512,1024]{1,0:T(8,128)(2,1)S(1)}, u32[]{:S(2)}, u32[]{:S(2)}) collective-permute-start(bf16[512,1024]{1,0:T(8,128)(2,1)S(1)} %shard_map.302), channel_id=1, source_target_pairs={{0,1},{3,2},{4,5},{7,6},{8,9},{11,10},{12,13},{15,14},{16,17},{19,... | collective-permute-start | bytes 3145736 | tf_op jit(solution)/shard_map/ppermute | solution.py:1153
  361.9 10.1 %collective-permute-done.46 = bf16[2,136,1024]{2,1,0:T(8,128)(2,1)S(1)} collective-permute-done((bf16[2,136,1024]{2,1,0:T(8,128)(2,1)S(1)}, bf16[2,136,1024]{2,1,0:T(8,128)(2,1)S(1)}, u32[]{:S(2)}, u32[]{:S(2)}) %collective-permute-start.46) | collective-permute-done | bytes 557088 | tf_op jit(solution)/shard_map/ppermute | solution.py:35
  378.9 7.6 %collective-permute-start.49 = (bf16[392,1024]{1,0:T(8,128)(2,1)S(1)}, bf16[392,1024]{1,0:T(8,128)(2,1)S(1)}, u32[]{:S(2)}, u32[]{:S(2)}) collective-permute-start(bf16[392,1024]{1,0:T(8,128)(2,1)S(1)} %pad_maximum_fusion.3), channel_id=1, source_target_pairs={{0,1},{3,2},{4,5},{7,6},{8,9},{11,10},{12,13},{15,14},{16,17},{19,... | collective-permute-start | bytes 2408456 | tf_op jit(solution)/shard_map/ppermute | solution.py:1153
  388.6 13.6 %collective-permute-done.49 = bf16[392,1024]{1,0:T(8,128)(2,1)S(1)} collective-permute-done((bf16[392,1024]{1,0:T(8,128)(2,1)S(1)}, bf16[392,1024]{1,0:T(8,128)(2,1)S(1)}, u32[]{:S(2)}, u32[]{:S(2)}) %collective-permute-start.49) | collective-permute-done | bytes 802848 | tf_op jit(solution)/shard_map/ppermute | solution.py:1153
  406.7 24.0 %collective-permute-done.52 = bf16[512,1024]{1,0:T(8,128)(2,1)S(1)} collective-permute-done((bf16[512,1024]{1,0:T(8,128)(2,1)S(1)}, bf16[512,1024]{1,0:T(8,128)(2,1)S(1)}, u32[]{:S(2)}, u32[]{:S(2)}) %collective-permute-start.52) | collective-permute-done | bytes 1048608 | tf_op jit(solution)/shard_map/ppermute | solution.py:1153
  433.1 13.1 %collective-permute-done.51 = bf16[392,1024]{1,0:T(8,128)(2,1)S(1)} collective-permute-done((bf16[392,1024]{1,0:T(8,128)(2,1)S(1)}, bf16[392,1024]{1,0:T(8,128)(2,1)S(1)}, u32[]{:S(2)}, u32[]{:S(2)}) %collective-permute-start.51) | collective-permute-done | bytes 802848 | tf_op jit(solution)/shard_map/ppermute | solution.py:1153
  (331 shorter events, 141.0 us)
Async XLA Ops:
  0.6 27.0 %collective-permute-start = (bf16[512,1024]{1,0:T(8,128)(2,1)}, bf16[512,1024]{1,0:T(8,128)(2,1)S(1)}, u32[]{:S(2)}, u32[]{:S(2)}) collective-permute-start(bf16[512,1024]{1,0:T(8,128)(2,1)} %bitcast.67), channel_id=1, source_target_pairs={{0,4},{4,8},{8,12},{12,16},{16,20},{20,24},{24,28},{1,5},{5,9},{9,... | collective-permute-start | bytes 3145736 | tf_op jit(solution)/shard_map/ppermute | solution.py:41
  36.6 13.6 %collective-permute-start.3 = (bf16[2,64,1024]{2,1,0:T(8,128)(2,1)S(1)}, bf16[2,64,1024]{2,1,0:T(8,128)(2,1)S(1)}, u32[]{:S(2)}, u32[]{:S(2)}) collective-permute-start(bf16[2,64,1024]{2,1,0:T(8,128)(2,1)S(1)} %get-tuple-element.199), channel_id=1, source_target_pairs={{0,16},{4,20},{8,24},{12,28},{16,0},{20,4},{24,8},{28,12},{1,17},{... | collective-permute-start | bytes 786440 | tf_op jit(solution)/shard_map/ppermute | solution.py:35
  36.7 13.5 %collective-permute-start.4 = (bf16[2,64,1024]{2,1,0:T(8,128)(2,1)S(1)}, bf16[2,64,1024]{2,1,0:T(8,128)(2,1)S(1)}, u32[]{:S(2)}, u32[]{:S(2)}) collective-permute-start(bf16[2,64,1024]{2,1,0:T(8,128)(2,1)S(1)} %get-tuple-element.200), channel_id=1, source_target_pairs={{0,24},{4,28},{8,16},{12,20},{16,8},{20,12},{24,0},{28,4},{1,25},{... | collective-permute-start | bytes 786440 | tf_op jit(solution)/shard_map/ppermute | solution.py:35
  119.8 25.2 %collective-permute-start.11 = (bf16[2,256,1024]{2,1,0:T(8,128)(2,1)S(1)}, bf16[2,256,1024]{2,1,0:T(8,128)(2,1)S(1)}, u32[]{:S(2)}, u32[]{:S(2)}) collective-permute-start(bf16[2,256,1024]{2,1,0:T(8,128)(2,1)S(1)} %get-tuple-element.238), channel_id=1, source_target_pairs={{0,16},{4,20},{8,24},{12,28},{16,0},{20,4},{24,8},{28,12},{1,17},{... | collective-permute-start | bytes 3145736 | tf_op jit(solution)/shard_map/ppermute | solution.py:35
  120.9 25.0 %collective-permute-start.10 = (bf16[2,256,1024]{2,1,0:T(8,128)(2,1)S(1)}, bf16[2,256,1024]{2,1,0:T(8,128)(2,1)}, u32[]{:S(2)}, u32[]{:S(2)}) collective-permute-start(bf16[2,256,1024]{2,1,0:T(8,128)(2,1)S(1)} %get-tuple-element.235), channel_id=1, source_target_pairs={{0,8},{4,12},{8,0},{12,4},{16,24},{20,28},{24,16},{28,20},{1,9},{5... | collective-permute-start | bytes 3145736 | tf_op jit(solution)/shard_map/ppermute | solution.py:35
  155.3 30.6 %collective-permute-start.14 = (bf16[2,256,1024]{2,1,0:T(8,128)(2,1)S(1)}, bf16[2,256,1024]{2,1,0:T(8,128)(2,1)S(1)}, u32[]{:S(2)}, u32[]{:S(2)}) collective-permute-start(bf16[2,256,1024]{2,1,0:T(8,128)(2,1)S(1)} %get-tuple-element.252), channel_id=1, source_target_pairs={{0,16},{4,20},{8,24},{12,28},{16,0},{20,4},{24,8},{28,12},{1,17},{... | collective-permute-start | bytes 3145736 | tf_op jit(solution)/shard_map/ppermute | solution.py:35
  156.2 29.7 %collective-permute-start.13 = (bf16[2,256,1024]{2,1,0:T(8,128)(2,1)S(1)}, bf16[2,256,1024]{2,1,0:T(8,128)(2,1)S(1)}, u32[]{:S(2)}, u32[]{:S(2)}) collective-permute-start(bf16[2,256,1024]{2,1,0:T(8,128)(2,1)S(1)} %get-tuple-element.249), channel_id=1, source_target_pairs={{0,8},{4,12},{8,0},{12,4},{16,24},{20,28},{24,16},{28,20},{1,9},{5... | collective-permute-start | bytes 3145736 | tf_op jit(solution)/shard_map/ppermute | solution.py:35
  157.4 37.7 %collective-permute-start.16 = (bf16[256,1024]{1,0:T(8,128)(2,1)S(1)}, bf16[256,1024]{1,0:T(8,128)(2,1)S(1)}, u32[]{:S(2)}, u32[]{:S(2)}) collective-permute-start(bf16[256,1024]{1,0:T(8,128)(2,1)S(1)} %get-tuple-element.260), channel_id=1, source_target_pairs={{0,8},{4,12},{8,0},{12,4},{16,24},{20,28},{24,16},{28,20},{1,9},{5... | collective-permute-start | bytes 1572872 | tf_op jit(solution)/shard_map/ppermute | solution.py:35
  158.2 36.9 %collective-permute-start.15 = (bf16[256,1024]{1,0:T(8,128)(2,1)S(1)}, bf16[256,1024]{1,0:T(8,128)(2,1)S(1)}, u32[]{:S(2)}, u32[]{:S(2)}) collective-permute-start(bf16[256,1024]{1,0:T(8,128)(2,1)S(1)} %get-tuple-element.258), channel_id=1, source_target_pairs={{0,16},{4,20},{8,24},{12,28},{16,0},{20,4},{24,8},{28,12},{1,17},{... | collective-permute-start | bytes 1572872 | tf_op jit(solution)/shard_map/ppermute | solution.py:35
  193.0 14.3 %collective-permute-start.19 = (bf16[256,1024]{1,0:T(8,128)(2,1)S(1)}, bf16[256,1024]{1,0:T(8,128)(2,1)S(1)}, u32[]{:S(2)}, u32[]{:S(2)}) collective-permute-start(bf16[256,1024]{1,0:T(8,128)(2,1)S(1)} %get-tuple-element.268), channel_id=1, source_target_pairs={{0,8},{4,12},{8,0},{12,4},{16,24},{20,28},{24,16},{28,20},{1,9},{5... | collective-permute-start | bytes 1572872 | tf_op jit(solution)/shard_map/ppermute | solution.py:35
  194.1 14.0 %collective-permute-start.18 = (bf16[256,1024]{1,0:T(8,128)(2,1)S(1)}, bf16[256,1024]{1,0:T(8,128)(2,1)S(1)}, u32[]{:S(2)}, u32[]{:S(2)}) collective-permute-start(bf16[256,1024]{1,0:T(8,128)(2,1)S(1)} %get-tuple-element.266), channel_id=1, source_target_pairs={{0,16},{4,20},{8,24},{12,28},{16,0},{20,4},{24,8},{28,12},{1,17},{... | collective-permute-start | bytes 1572872 | tf_op jit(solution)/shard_map/ppermute | solution.py:35
  209.0 31.3 %collective-permute-start.27 = (bf16[512,1024]{1,0:T(8,128)(2,1)S(1)}, bf16[512,1024]{1,0:T(8,128)(2,1)S(1)}, u32[]{:S(2)}, u32[]{:S(2)}) collective-permute-start(bf16[512,1024]{1,0:T(8,128)(2,1)S(1)} %shard_map.289), channel_id=1, source_target_pairs={{0,1},{3,2},{4,5},{7,6},{8,9},{11,10},{12,13},{15,14},{16,17},{19,... | collective-permute-start | bytes 3145736 | tf_op jit(solution)/shard_map/ppermute | solution.py:1153
  246.3 27.5 %collective-permute-start.29 = (bf16[4,512,1024]{2,1,0:T(8,128)(2,1)S(1)}, bf16[4,512,1024]{2,1,0:T(8,128)(2,1)S(1)}, u32[]{:S(2)}, u32[]{:S(2)}) collective-permute-start(bf16[4,512,1024]{2,1,0:T(8,128)(2,1)S(1)} %shard_map.295), channel_id=1, source_target_pairs={{0,4},{4,0},{8,12},{12,8},{16,20},{20,16},{24,28},{28,24},{1,5},{5... | collective-permute-start | bytes 12582920 | tf_op jit(solution)/shard_map/ppermute | solution.py:35
  246.5 32.9 %collective-permute-start.31 = (bf16[2,512,1024]{2,1,0:T(8,128)(2,1)S(1)}, bf16[2,512,1024]{2,1,0:T(8,128)(2,1)S(1)}, u32[]{:S(2)}, u32[]{:S(2)}) collective-permute-start(bf16[2,512,1024]{2,1,0:T(8,128)(2,1)S(1)} %get-tuple-element.305), channel_id=1, source_target_pairs={{4,0},{8,4},{12,8},{16,12},{20,16},{24,20},{28,24},{5,1},{9,5},{13... | collective-permute-start | bytes 6291464 | tf_op jit(solution)/shard_map/ppermute | solution.py:41
  247.8 24.6 %collective-permute-start.28 = (bf16[512,1024]{1,0:T(8,128)(2,1)S(1)}, bf16[512,1024]{1,0:T(8,128)(2,1)S(1)}, u32[]{:S(2)}, u32[]{:S(2)}) collective-permute-start(bf16[512,1024]{1,0:T(8,128)(2,1)S(1)} %shard_map.291), channel_id=1, source_target_pairs={{0,1},{3,2},{4,5},{7,6},{8,9},{11,10},{12,13},{15,14},{16,17},{19,... | collective-permute-start | bytes 3145736 | tf_op jit(solution)/shard_map/ppermute | solution.py:1153
  249.2 28.8 %collective-permute-start.30 = (bf16[512,1024]{1,0:T(8,128)(2,1)S(1)}, bf16[512,1024]{1,0:T(8,128)(2,1)S(1)}, u32[]{:S(2)}, u32[]{:S(2)}) collective-permute-start(bf16[512,1024]{1,0:T(8,128)(2,1)S(1)} %add_convert_fusion.5), channel_id=1, source_target_pairs={{1,2},{2,1},{5,6},{6,5},{9,10},{10,9},{13,14},{14,13},{17,18},{18,... | collective-permute-start | bytes 3145736 | tf_op jit(solution)/shard_map/ppermute | solution.py:1153
  286.8 28.9 %collective-permute-start.34 = (bf16[512,1024]{1,0:T(8,128)(2,1)}, bf16[512,1024]{1,0:T(8,128)(2,1)}, u32[]{:S(2)}, u32[]{:S(2)}) collective-permute-start(bf16[512,1024]{1,0:T(8,128)(2,1)} %add_convert_fusion.3), channel_id=1, source_target_pairs={{1,0},{2,3},{5,4},{6,7},{9,8},{10,11},{13,12},{14,15},{17,16},{18,... | collective-permute-start | bytes 3145736 | tf_op jit(solution)/shard_map/ppermute | solution.py:1153
  288.1 28.9 %collective-permute-start.36 = (bf16[2,256,1024]{2,1,0:T(8,128)(2,1)}, bf16[2,256,1024]{2,1,0:T(8,128)(2,1)S(1)}, u32[]{:S(2)}, u32[]{:S(2)}) collective-permute-start(bf16[2,256,1024]{2,1,0:T(8,128)(2,1)} %copy-done.67), channel_id=1, source_target_pairs={{0,16},{4,20},{8,24},{12,28},{16,0},{20,4},{24,8},{28,12},{1,17},{... | collective-permute-start | bytes 3145736 | tf_op jit(solution)/shard_map/ppermute | solution.py:35
  289.3 27.8 %collective-permute-start.35 = (bf16[2,256,1024]{2,1,0:T(8,128)(2,1)}, bf16[2,256,1024]{2,1,0:T(8,128)(2,1)S(1)}, u32[]{:S(2)}, u32[]{:S(2)}) collective-permute-start(bf16[2,256,1024]{2,1,0:T(8,128)(2,1)} %copy-done.66), channel_id=1, source_target_pairs={{0,8},{4,12},{8,0},{12,4},{16,24},{20,28},{24,16},{28,20},{1,9},{5... | collective-permute-start | bytes 3145736 | tf_op jit(solution)/shard_map/ppermute | solution.py:35
  292.2 48.5 %collective-permute-start.37 = (bf16[512,1024]{1,0:T(8,128)(2,1)S(1)}, bf16[512,1024]{1,0:T(8,128)(2,1)S(1)}, u32[]{:S(2)}, u32[]{:S(2)}) collective-permute-start(bf16[512,1024]{1,0:T(8,128)(2,1)S(1)} %add_convert_fusion.2), channel_id=1, source_target_pairs={{1,0},{2,3},{5,4},{6,7},{9,8},{10,11},{13,12},{14,15},{17,16},{18,... | collective-permute-start | bytes 3145736 | tf_op jit(solution)/shard_map/ppermute | solution.py:1153
  317.9 26.1 %collective-permute-start.39 = (bf16[256,1024]{1,0:T(8,128)(2,1)S(1)}, bf16[256,1024]{1,0:T(8,128)(2,1)S(1)}, u32[]{:S(2)}, u32[]{:S(2)}) collective-permute-start(bf16[256,1024]{1,0:T(8,128)(2,1)S(1)} %get-tuple-element.331), channel_id=1, source_target_pairs={{0,8},{4,12},{8,0},{12,4},{16,24},{20,28},{24,16},{28,20},{1,9},{5... | collective-permute-start | bytes 1572872 | tf_op jit(solution)/shard_map/ppermute | solution.py:35
  319.5 24.5 %collective-permute-start.38 = (bf16[256,1024]{1,0:T(8,128)(2,1)S(1)}, bf16[256,1024]{1,0:T(8,128)(2,1)S(1)}, u32[]{:S(2)}, u32[]{:S(2)}) collective-permute-start(bf16[256,1024]{1,0:T(8,128)(2,1)S(1)} %get-tuple-element.329), channel_id=1, source_target_pairs={{0,16},{4,20},{8,24},{12,28},{16,0},{20,4},{24,8},{28,12},{1,17},{... | collective-permute-start | bytes 1572872 | tf_op jit(solution)/shard_map/ppermute | solution.py:35
  321.2 36.3 %collective-permute-start.45 = (bf16[2,2,136,1024]{3,2,0,1:T(8,128)(2,1)S(1)}, bf16[2,2,136,1024]{3,2,0,1:T(8,128)(2,1)S(1)}, u32[]{:S(2)}, u32[]{:S(2)}) collective-permute-start(bf16[2,2,136,1024]{3,2,0,1:T(8,128)(2,1)S(1)} %bitcast.79), channel_id=1, source_target_pairs={{0,4},{4,0},{8,12},{12,8},{16,20},{20,16},{24,28},{28,24},{1,5},{5... | collective-permute-start | bytes 3342344 | tf_op jit(solution)/shard_map/ppermute | solution.py:35
  341.0 17.7 %collective-permute-start.41 = (bf16[2,128,1024]{2,1,0:T(8,128)(2,1)S(1)}, bf16[2,128,1024]{2,1,0:T(8,128)(2,1)S(1)}, u32[]{:S(2)}, u32[]{:S(2)}) collective-permute-start(bf16[2,128,1024]{2,1,0:T(8,128)(2,1)S(1)} %get-tuple-element.337), channel_id=1, source_target_pairs={{0,16},{4,20},{8,24},{12,28},{16,0},{20,4},{24,8},{28,12},{1,17},{... | collective-permute-start | bytes 1572872 | tf_op jit(solution)/shard_map/ppermute | solution.py:35
  343.1 15.6 %collective-permute-start.40 = (bf16[2,128,1024]{2,1,0:T(8,128)(2,1)S(1)}, bf16[2,128,1024]{2,1,0:T(8,128)(2,1)S(1)}, u32[]{:S(2)}, u32[]{:S(2)}) collective-permute-start(bf16[2,128,1024]{2,1,0:T(8,128)(2,1)S(1)} %get-tuple-element.334), channel_id=1, source_target_pairs={{0,8},{4,12},{8,0},{12,4},{16,24},{20,28},{24,16},{28,20},{1,9},{5... | collective-permute-start | bytes 1572872 | tf_op jit(solution)/shard_map/ppermute | solution.py:35
  344.9 31.9 %collective-permute-start.42 = (bf16[512,1024]{1,0:T(8,128)(2,1)S(1)}, bf16[512,1024]{1,0:T(8,128)(2,1)S(1)}, u32[]{:S(2)}, u32[]{:S(2)}) collective-permute-start(bf16[512,1024]{1,0:T(8,128)(2,1)S(1)} %shard_map.302), channel_id=1, source_target_pairs={{0,1},{3,2},{4,5},{7,6},{8,9},{11,10},{12,13},{15,14},{16,17},{19,... | collective-permute-start | bytes 3145736 | tf_op jit(solution)/shard_map/ppermute | solution.py:1153
  357.9 14.0 %collective-permute-start.46 = (bf16[2,136,1024]{2,1,0:T(8,128)(2,1)S(1)}, bf16[2,136,1024]{2,1,0:T(8,128)(2,1)S(1)}, u32[]{:S(2)}, u32[]{:S(2)}) collective-permute-start(bf16[2,136,1024]{2,1,0:T(8,128)(2,1)S(1)} %dynamic-slice_bitcast_fusion), channel_id=1, source_target_pairs={{0,8},{4,12},{8,0},{12,4},{16,24},{20,28},{24,16},{28,20},{1,9},{5... | collective-permute-start | bytes 1671176 | tf_op jit(solution)/shard_map/ppermute | solution.py:35
  359.3 17.9 %collective-permute-start.44 = (bf16[128,1024]{1,0:T(8,128)(2,1)S(1)}, bf16[128,1024]{1,0:T(8,128)(2,1)S(1)}, u32[]{:S(2)}, u32[]{:S(2)}) collective-permute-start(bf16[128,1024]{1,0:T(8,128)(2,1)S(1)} %get-tuple-element.345), channel_id=1, source_target_pairs={{0,8},{4,12},{8,0},{12,4},{16,24},{20,28},{24,16},{28,20},{1,9},{5... | collective-permute-start | bytes 786440 | tf_op jit(solution)/shard_map/ppermute | solution.py:35
  360.9 16.4 %collective-permute-start.43 = (bf16[128,1024]{1,0:T(8,128)(2,1)S(1)}, bf16[128,1024]{1,0:T(8,128)(2,1)S(1)}, u32[]{:S(2)}, u32[]{:S(2)}) collective-permute-start(bf16[128,1024]{1,0:T(8,128)(2,1)S(1)} %get-tuple-element.343), channel_id=1, source_target_pairs={{0,16},{4,20},{8,24},{12,28},{16,0},{20,4},{24,8},{28,12},{1,17},{... | collective-permute-start | bytes 786440 | tf_op jit(solution)/shard_map/ppermute | solution.py:35
  378.9 23.2 %collective-permute-start.49 = (bf16[392,1024]{1,0:T(8,128)(2,1)S(1)}, bf16[392,1024]{1,0:T(8,128)(2,1)S(1)}, u32[]{:S(2)}, u32[]{:S(2)}) collective-permute-start(bf16[392,1024]{1,0:T(8,128)(2,1)S(1)} %pad_maximum_fusion.3), channel_id=1, source_target_pairs={{0,1},{3,2},{4,5},{7,6},{8,9},{11,10},{12,13},{15,14},{16,17},{19,... | collective-permute-start | bytes 2408456 | tf_op jit(solution)/shard_map/ppermute | solution.py:1153
  387.1 43.6 %collective-permute-start.52 = (bf16[512,1024]{1,0:T(8,128)(2,1)S(1)}, bf16[512,1024]{1,0:T(8,128)(2,1)S(1)}, u32[]{:S(2)}, u32[]{:S(2)}) collective-permute-start(bf16[512,1024]{1,0:T(8,128)(2,1)S(1)} %add_convert_fusion), channel_id=1, source_target_pairs={{1,0},{2,3},{5,4},{6,7},{9,8},{10,11},{13,12},{14,15},{17,16},{18,... | collective-permute-start | bytes 3145736 | tf_op jit(solution)/shard_map/ppermute | solution.py:1153
  405.4 40.8 %collective-permute-start.51 = (bf16[392,1024]{1,0:T(8,128)(2,1)S(1)}, bf16[392,1024]{1,0:T(8,128)(2,1)S(1)}, u32[]{:S(2)}, u32[]{:S(2)}) collective-permute-start(bf16[392,1024]{1,0:T(8,128)(2,1)S(1)} %add_convert_fusion.6), channel_id=1, source_target_pairs={{1,0},{2,3},{5,4},{6,7},{9,8},{10,11},{13,12},{14,15},{17,16},{18,... | collective-permute-start | bytes 2408456 | tf_op jit(solution)/shard_map/ppermute | solution.py:1153
  (107 other events, 1344.7 us)
